TPU v7x, 256 devices: a whole 4x4x8 slice. The times are simulated.
256 devices in a mesh: ctx: 32 (over z, y), tp: 8 (over x, core).
Axes of the slice: x: 4, y: 4, z: 8, core: 2. Of those that a mesh axis runs over, the one named last changes fastest.
Arguments:
- tokens: bfloat16 [24576, 4096], P(('ctx', 'tp')), may hold values from -6 to 6
- norm_gain: float32 [4096], replicated, may hold values from 0.1 to 1.9
- w_qkv: bfloat16 [4096, 8192], P('ctx', 'tp'), may hold values from -0.09375 to 0.09375
- w_out: bfloat16 [4096, 4096], P('tp', 'ctx'), may hold values from -0.09375 to 0.09375
- head_gain: float32 [4096], P('tp'), may hold values from 0.1 to 1.9
- input_codes: int32 [8, 24576], P('tp', 'ctx'), may hold values from -4 to 4
- forget_codes: int32 [8, 24576], P('tp', 'ctx'), may hold values from -24 to 4
- forget_bias: float32 [8], P('tp'), may hold values from 3 to 13.5, as said below
- document_begin_flags: int32 [24576], P('ctx'), may hold values 0 or 1
Outputs:
- mixed: bfloat16 [24576, 4096], P(('ctx', 'tp'))
Inputs may be any that keep to these rules, and one draw needn't show every extreme that they name: `forget_bias`: a bias for each head.
All inputs are finite; a program needn't handle non-finite values. No bound on the sum of `document_begin_flags` on one device may be relied on, other than what follows from the above.
Results may differ from a plain program's by a relative error of at most 0.017.
Values may be sent and summed in bfloat16 or wider, within the bound.
A program may use at most 64 MiB of HBM per device.

v0:
```python
import jax
import jax.numpy as jnp
from jax import lax
from jax.sharding import PartitionSpec as P

DK = 256
DV = 512


EPSILON = 1e-06
FORGET_STEP = 0.5
INPUT_STEP = 0.5


def carried_in(shard, axis, combine, identity):
    count, position = (lax.axis_size(axis), lax.axis_index(axis))
    everything = jax.tree.map(
        lambda part, kind: lax.all_gather(part.astype(kind), axis),
        shard,
        (jnp.bfloat16, jnp.bfloat16),
    )
    start = jax.tree.map(
        lambda part, zero: jnp.broadcast_to(jnp.asarray(zero, part.dtype), part.shape),
        shard,
        identity,
    )

    def hop(k, before):
        reached = k < position
        new = combine(
            before, jax.tree.map(lambda part, own: part[k].astype(own.dtype), everything, shard)
        )
        return jax.tree.map(lambda a, b: jnp.where(reached, a, b), new, before)

    return lax.fori_loop(0, count, hop, start)


def rms_rows(embedded_entries, norm_gain):
    token_float = embedded_entries.astype(jnp.float32)
    moment = jnp.mean(token_float * token_float, axis=1, keepdims=True)
    return (token_float * lax.rsqrt(moment + EPSILON) * norm_gain).astype(jnp.bfloat16)


def local_terms(queries, key_rows, values, log_forget, input_gate, starts):
    length = queries.shape[0]
    scaling = queries.shape[1] ** (-0.5)
    segment = jnp.cumsum(starts)
    levels = jnp.cumsum(log_forget)
    position = jnp.arange(length)
    allowed = (position[:, None] >= position[None, :]) & (segment[:, None] == segment[None, :])
    decays = jnp.where(
        allowed,
        jnp.exp(jnp.minimum(levels[:, None] - levels[None, :], 0.0) + input_gate[None, :]),
        0.0,
    )
    scores = jnp.dot(queries, key_rows.T, preferred_element_type=jnp.float32) * scaling
    weights = (scores * decays).astype(jnp.bfloat16)
    inner_part = jnp.dot(weights, values, preferred_element_type=jnp.float32)
    last_level = levels[-1]
    last_seg = segment[-1]
    keeping = jnp.where(segment == last_seg, jnp.exp(last_level - levels + input_gate), 0.0)
    weighted = (key_rows.astype(jnp.float32) * keeping[:, None]).astype(jnp.bfloat16)
    local_state = lax.dot_general(
        weighted, values, (((0,), (0,)), ((), ())), preferred_element_type=jnp.float32
    )
    passing = jnp.where(last_seg == 0, jnp.exp(last_level), 0.0)
    carried = jnp.where(segment == 0, jnp.exp(levels), 0.0) * scaling
    return (inner_part, local_state, passing, carried)


def apply_state(queries, carried, incoming):
    lifted = queries.astype(jnp.float32) * carried[:, None]
    return jnp.dot(
        lifted, incoming, precision=lax.Precision.HIGHEST, preferred_element_type=jnp.float32
    )


def head_norm(head_out, gain):
    centre = jnp.mean(head_out, axis=1, keepdims=True)
    shifted = head_out - centre
    spread = jnp.mean(shifted * shifted, axis=1, keepdims=True)
    return (shifted * lax.rsqrt(spread + EPSILON) * gain).astype(jnp.bfloat16)


def combine(earlier, later):
    return (earlier[0] * later[0], later[0][:, None, None] * earlier[1] + later[1])


def local(
    tokens,
    norm_gain,
    w_qkv,
    w_out,
    head_gain,
    input_codes,
    forget_codes,
    forget_bias,
    document_begin_flags,
):
    normed = rms_rows(tokens, norm_gain)
    every_row_list = lax.all_gather(normed, "tp", axis=0, tiled=True)
    parameter_collection = lax.all_gather(w_qkv, "ctx", axis=0, tiled=True)
    rows_combined = jnp.dot(
        every_row_list, parameter_collection, preferred_element_type=jnp.float32
    )
    rows_combined = rows_combined.astype(jnp.bfloat16)
    heads_here = forget_bias.shape[0]
    stride = 2 * DK + DV
    query_list, inner_list, state_list, passing_list, carried_list = ([], [], [], [], [])
    attention_slot_number = 0
    offset = attention_slot_number * stride
    queries = rows_combined[:, offset : offset + DK]
    key_rows = rows_combined[:, offset + DK : offset + 2 * DK]
    values = rows_combined[:, offset + 2 * DK : offset + stride]
    log_forget = jax.nn.log_sigmoid(
        FORGET_STEP * forget_codes[attention_slot_number].astype(jnp.float32)
        + forget_bias[attention_slot_number]
    )
    input_gate = INPUT_STEP * input_codes[attention_slot_number].astype(jnp.float32)
    inner_part, local_state, passing, carried = local_terms(
        queries, key_rows, values, log_forget, input_gate, document_begin_flags
    )
    query_list.append(queries)
    inner_list.append(inner_part)
    state_list.append(local_state)
    passing_list.append(passing)
    carried_list.append(carried)
    identity = (jnp.ones((heads_here,), jnp.float32), jnp.zeros((heads_here, DK, DV), jnp.float32))
    scanned = carried_in((jnp.stack(passing_list), jnp.stack(state_list)), "ctx", combine, identity)
    incoming = scanned[1]
    attention_slot_number = 0
    head_out = inner_list[attention_slot_number] + apply_state(
        query_list[attention_slot_number],
        carried_list[attention_slot_number],
        incoming[attention_slot_number],
    )
    normed_heads = head_norm(head_out, head_gain)
    out_columns = lax.all_gather(w_out, "ctx", axis=1, tiled=True)
    summed = lax.psum_scatter(
        jnp.dot(normed_heads, out_columns, preferred_element_type=jnp.float32).astype(jnp.bfloat16),
        "tp",
        scatter_dimension=0,
        tiled=True,
    ).astype(jnp.float32)
    return (tokens.astype(jnp.float32) + summed).astype(jnp.bfloat16)


def solution(mesh):
    placed = (
        P(("ctx", "tp"), None),
        P(),
        P("ctx", "tp"),
        P("tp", "ctx"),
        P("tp"),
        P("tp", "ctx"),
        P("tp", "ctx"),
        P("tp"),
        P("ctx"),
    )
    return jax.shard_map(
        local, mesh=mesh, in_specs=placed, out_specs=P(("ctx", "tp"), None), check_vma=False
    )
```

profile of v0, /device:TPU:224, one launch (start us, length us, event | category | flops | bytes accessed | tf_op | source)
XLA Modules:
  0.0 408.3 jit_solution(12727475956866767131)
XLA Ops:
  6.5 1.4 fusion.2
  8.0 2.3 fusion.4
  14.2 1.3 exponential_select_fusion
  15.5 38.8 %all-gather.6.cloned.1.call-done = bf16[768,4096]{1,0:T(8,128)(2,1)} async-done(((bf16[96,4096]{1,0:T(8,128)(2,1)}), bf16[768,4096]{1,0:T(8,128)(2,1)}) %all-gather.6.cloned.1.call-update) | async-done | bytes 6291472 | tf_op jit(solution)/shard_map/all_gather | solution.py:101
  54.3 99.3 %all-gather.8.cloned.1.call-done = bf16[4096,1024]{1,0:T(8,128)(2,1)} async-done(((bf16[128,1024]{1,0:T(8,128)(2,1)}), bf16[4096,1024]{1,0:T(8,128)(2,1)}) %all-gather.8.cloned.1.call-update) | async-done | bytes 8388624 | tf_op jit(solution)/shard_map/all_gather | solution.py:102
  153.6 10.9 %convolution_convert_fusion.1 = bf16[768,1024]{1,0:T(8,128)(2,1)S(1)} fusion(bf16[768,4096]{1,0:T(8,128)(2,1)} %all-gather.6.cloned.1.call-done, bf16[4096,1024]{1,0:T(8,128)(2,1)} %all-gather.8.cloned.1.call-done), kind=kOutput, calls=%fused_computation.10 | convolution fusion | flops 6443237376 | bytes 16252928 | tf_op jit(solution)/shard_map/dot_general | solution.py:103
  164.6 1.3 convolution_convert_fusion.2
  168.6 0.7 dynamic-update-slice
  169.3 66.0 %all-reduce = bf16[32]{0:T(256)(128)(2,1)S(1)} all-reduce(bf16[32]{0:T(256)(128)(2,1)S(1)} %dynamic-update-slice), channel_id=1, replica_groups=mesh['ctx'=32,'tp'=8] {'ctx'}, use_global_device_ids=true, to_apply=%add | all-reduce | flops 32 | bytes 128
  235.3 2.5 fusion.6
  237.8 23.9 %all-gather.12.cloned.1.call-done = bf16[8192,512]{1,0:T(8,128)(2,1)} async-done(((bf16[256,512]{1,0:T(8,128)(2,1)}), bf16[8192,512]{1,0:T(8,128)(2,1)}) %all-gather.12.cloned.1.call-update) | async-done | bytes 8388624 | tf_op jit(solution)/shard_map/all_gather | solution.py:18
  261.8 81.1 %while.14 = (s32[]{:T(128)}, f32[1,256,512]{2,1,0:T(8,128)S(1)}, s32[]{:T(128)}, bf16[32,1]{0,1:T(2,128)(2,1)S(1)}, bf16[32,1,256,512]{3,2,1,0:T(8,128)(2,1)}, /*index=5*/s32[]{:T(128)}, s32[]{:T(128)}) while((s32[]{:T(128)}, f32[1,256,512]{2,1,0:T(8,128)S(1)}, s32[]{:T(128)}, bf16[32,1]{0,1:T(2,128)(2,1)S(1)}, ...), condition=%wide.region_6.7_spmd.clone, body=%wide.region_5.6_spmd.clone.sunk | while | flops 655365 | bytes 1310839 | solution.py:35
  263.0 1.3 fusion.42
  265.6 1.3 fusion.42
  268.1 1.3 fusion.42
  270.6 1.3 fusion.42
  273.2 1.3 fusion.42
  275.7 1.3 fusion.42
  278.2 1.3 fusion.42
  280.8 1.3 fusion.42
  283.3 1.3 fusion.42
  285.8 1.3 fusion.42
  288.4 1.3 fusion.42
  290.9 1.3 fusion.42
  293.4 1.3 fusion.42
  296.0 1.3 fusion.42
  298.5 1.3 fusion.42
  301.0 1.3 fusion.42
  303.6 1.3 fusion.42
  306.1 1.3 fusion.42
  308.6 1.3 fusion.42
  311.2 1.3 fusion.42
  313.7 1.3 fusion.42
  316.3 1.3 fusion.42
  318.8 1.3 fusion.42
  321.3 1.3 fusion.42
  323.9 1.3 fusion.42
  326.4 1.3 fusion.42
  328.9 1.3 fusion.42
  331.5 1.3 fusion.42
  334.0 1.3 fusion.42
  336.6 1.3 fusion.42
  339.1 1.3 fusion.42
  341.6 1.3 fusion.42
  342.9 3.2 fusion.37
  346.8 7.7 %convolution_convert_fusion = bf16[768,4096]{1,0:T(8,128)(2,1)} fusion(bf16[512,4096]{1,0:T(8,128)(2,1)} %all-gather.10.cloned.1.call-done, f32[768,512]{0,1:T(8,128)S(1)} %get-tuple-element.142, f32[512]{0:T(512)S(1)} %copy-done.5, f32[768]{0:T(1024)S(1)} %add_rsqrt_fusion, f32[768]{0:T(1024)S(1)} %broadcast_multiply_fusion), kind=kOutput, calls=%fused_computation.3 | convolution fusion | flops 3225944064 | bytes 12066816 | tf_op jit(solution)/shard_map/dot_general | solution.py:140
  354.6 45.0 %reduce-scatter.2.cloned.1.call-done = bf16[96,4096]{1,0:T(8,128)(2,1)} async-done(((bf16[768,4096]{1,0:T(8,128)(2,1)}), bf16[96,4096]{1,0:T(8,128)(2,1)}) %reduce-scatter.2.cloned.1.call-update) | async-done | bytes 786448 | tf_op jit(solution)/shard_map/reduce_scatter | solution.py:139
  399.5 2.2 fusion.5
  (78 shorter events, 23.9 us)
Async XLA Ops:
  6.5 5.2 %copy-start.4 = (s32[1,768]{1,0:T(1,128)S(1)}, s32[1,768]{1,0:T(1,128)}, u32[]{:S(2)}) copy-start(s32[1,768]{1,0:T(1,128)} %param.17) | copy-start | bytes 9220
  6.5 5.6 %copy-start.2 = (s32[768]{0:T(1024)S(1)}, s32[768]{0:T(1024)}, u32[]{:S(2)}) copy-start(s32[768]{0:T(1024)} %param.19) | copy-start | bytes 9220
  6.5 47.8 %all-gather.6.cloned.1.call-start = ((), (), s32[]{:S(2)}) async-start(), calls=%async_computation.1 | async-start | bytes 7077888 | tf_op jit(solution)/shard_map/all_gather | solution.py:101
  8.0 6.2 %copy-start.3 = (s32[1,768]{1,0:T(1,128)S(1)}, s32[1,768]{1,0:T(1,128)}, u32[]{:S(2)}) copy-start(s32[1,768]{1,0:T(1,128)} %param.16) | copy-start | bytes 9220
  10.3 143.4 %all-gather.8.cloned.1.call-start = ((), (), s32[]{:S(2)}) async-start(), calls=%async_computation.2 | async-start | bytes 8650752 | tf_op jit(solution)/shard_map/all_gather | solution.py:102
  11.0 250.7 %all-gather.12.cloned.1.call-start = ((), (), s32[]{:S(2)}) async-start(), calls=%async_computation.5 | async-start | bytes 8650752 | tf_op jit(solution)/shard_map/all_gather | solution.py:18
  164.5 73.3 %copy-start.1 = (bf16[768,1024]{1,0:T(8,128)(2,1)}, bf16[768,1024]{1,0:T(8,128)(2,1)S(1)}, u32[]{:S(2)}) copy-start(bf16[768,1024]{1,0:T(8,128)(2,1)S(1)} %convolution_convert_fusion.1) | copy-start | bytes 4718596
  164.6 3.3 copy-start.6
  165.9 180.5 %all-gather.10.cloned.1.call-start = ((), (), s32[]{:S(2)}) async-start(), calls=%async_computation.3 | async-start | bytes 4325376 | tf_op jit(solution)/shard_map/all_gather | solution.py:138
  166.5 233.1 %reduce-scatter.2.cloned.1.call-start = ((), (), s32[]{:S(2)}) async-start(), calls=%async_computation.4 | async-start | bytes 7077888 | tf_op jit(solution)/shard_map/reduce_scatter | solution.py:139
  346.1 0.7 copy-start.5
  354.6 45.0 %copy-start = (bf16[96,4096]{1,0:T(8,128)(2,1)S(1)}, bf16[96,4096]{1,0:T(8,128)(2,1)}, u32[]{:S(2)}) copy-start(bf16[96,4096]{1,0:T(8,128)(2,1)} %param.11) | copy-start | bytes 2359300
Sparse Core Ops, SparseCore 0:
  10.4 43.8 all-gather.5
  56.9 96.7 all-gather.7
  166.0 95.7 all-gather.11
  264.1 81.7 all-gather.9
  354.7 44.7 reduce-scatter.1
where the time goes:
time: 413 us; the launch traced here: 408 us
  waiting for transfers between devices  208 us (50%)
  blocking collectives  66 us (16%)
  other arithmetic  48.8 us (12%)
  matrix products  25.7 us (6%)
  local copies, waits for them, and re-layouts  22.3 us (5%)
  loops' own time  21.7 us (5%)
  between operations  15.3 us (4%)
    all_gather x1, waiting for transfers between devices, local(): parameter_collection = lax.all_gather(w_qkv, 'ctx', axis=0, tiled=True)  99.3 us
    unnamed x1, blocking collectives  66 us
    reduce_scatter x1, waiting for transfers between devices, local(): lax.psum_scatter(jnp.dot(normed_heads, out_columns, preferred_element_typ...  45 us
    select_n x32, other arithmetic, hop(): return jax.tree.map(lambda a, b: jnp.where(reached, a, b), new, before)  40.6 us
    all_gather x1, waiting for transfers between devices, local(): every_row_list = lax.all_gather(normed, 'tp', axis=0, tiled=True)  38.8 us
    all_gather x1, waiting for transfers between devices, carried_in(): lax.all_gather(part.astype(kind), axis)  23.9 us
    another operation x1, loops' own time, carried_in(): return lax.fori_loop(0, count, hop, start)  21.7 us
    dynamic_slice x32, local copies, waits for them, and re-layouts, hop(): part[k].astype(own.dtype)  18.7 us
  transfers between devices with their start and end apart: 5, of which 4 were waited for; matrix products, arithmetic and copies ran while one was open for 17% of the time, Pallas kernels for 0%

commit v1 on v0

--- a/solution.py
+++ b/solution.py
@@ -12,27 +12,30 @@
 INPUT_STEP = 0.5
 
 
-def carried_in(shard, axis, combine, identity):
-    count, position = (lax.axis_size(axis), lax.axis_index(axis))
-    everything = jax.tree.map(
-        lambda part, kind: lax.all_gather(part.astype(kind), axis),
-        shard,
-        (jnp.bfloat16, jnp.bfloat16),
-    )
-    start = jax.tree.map(
-        lambda part, zero: jnp.broadcast_to(jnp.asarray(zero, part.dtype), part.shape),
-        shard,
-        identity,
-    )
+def carried_in(passing, state, axis):
+    count = lax.axis_size(axis)
+    if count == 1:
+        return jnp.zeros_like(state)
 
-    def hop(k, before):
-        reached = k < position
-        new = combine(
-            before, jax.tree.map(lambda part, own: part[k].astype(own.dtype), everything, shard)
-        )
-        return jax.tree.map(lambda a, b: jnp.where(reached, a, b), new, before)
+    def shifted(part, k, kind):
+        pairs = [(i, i + k) for i in range(count - k)]
+        return lax.ppermute(part.astype(kind), axis, pairs).astype(jnp.float32)
 
-    return lax.fori_loop(0, count, hop, start)
+    decay = shifted(passing, 1, jnp.float32)
+    total = shifted(state, 1, jnp.bfloat16)
+    if count > 2:
+        decay_far = shifted(passing, 2, jnp.float32)
+        total_far = shifted(state, 2, jnp.bfloat16)
+        total = decay[:, None, None] * total_far + total
+        decay = decay * decay_far
+    k = 2
+    while k < count:
+        decay_far = shifted(decay, k, jnp.float32)
+        total_far = shifted(total, k, jnp.bfloat16)
+        total = decay[:, None, None] * total_far + total
+        decay = decay * decay_far
+        k *= 2
+    return total
 
 
 def rms_rows(embedded_entries, norm_gain):
@@ -82,10 +85,6 @@
     return (shifted * lax.rsqrt(spread + EPSILON) * gain).astype(jnp.bfloat16)
 
 
-def combine(earlier, later):
-    return (earlier[0] * later[0], later[0][:, None, None] * earlier[1] + later[1])
-
-
 def local(
     tokens,
     norm_gain,
@@ -125,9 +124,7 @@
     state_list.append(local_state)
     passing_list.append(passing)
     carried_list.append(carried)
-    identity = (jnp.ones((heads_here,), jnp.float32), jnp.zeros((heads_here, DK, DV), jnp.float32))
-    scanned = carried_in((jnp.stack(passing_list), jnp.stack(state_list)), "ctx", combine, identity)
-    incoming = scanned[1]
+    incoming = carried_in(jnp.stack(passing_list), jnp.stack(state_list), "ctx")
     attention_slot_number = 0
     head_out = inner_list[attention_slot_number] + apply_state(
         query_list[attention_slot_number],

time: 413 us -> 328 us (0.79)
  blocking collectives: 66 us -> 0 us
  other arithmetic: 48.8 us -> 10.9 us
  starting transfers between devices: 0.16 us -> 32.7 us
  waiting for transfers between devices: 208 us -> 233 us
  loops' own time: 21.7 us -> 0 us
  local copies, waits for them, and re-layouts: 22.3 us -> 2.56 us
    unnamed x1 -> x0, blocking collectives: 66 us -> none
    ppermute x0 -> x11, waiting for transfers between devices: none -> 45.5 us  [shifted(): return lax.ppermute(part.astype(kind), axis, pairs).astype(jnp.float32)]
    select_n x32 -> x0, other arithmetic: 40.6 us -> none  [hop(): return jax.tree.map(lambda a, b: jnp.where(reached, a, b), new, before)]
    ppermute x0 -> x11, starting transfers between devices: none -> 32.6 us  [shifted(): return lax.ppermute(part.astype(kind), axis, pairs).astype(jnp.float32)]
    all_gather x1 -> x0, waiting for transfers between devices: 23.9 us -> none  [carried_in(): lax.all_gather(part.astype(kind), axis)]
    another operation x1 -> x0, loops' own time: 21.7 us -> none  [carried_in(): return lax.fori_loop(0, count, hop, start)]
    dynamic_slice x32 -> x0, local copies, waits for them, and re-layouts: 18.7 us -> none  [hop(): part[k].astype(own.dtype)]
  transfers between devices with their start and end apart: 5 -> 15, of which waited for: 4 -> 10; matrix products, arithmetic and copies ran while one was open for 17% -> 8% of each run, Pallas kernels for 0% -> 0%
where the time goes in v1:
time: 328 us; the launch traced here: 325 us
  waiting for transfers between devices  233 us (71%)
  starting transfers between devices  32.7 us (10%)
  matrix products  27.2 us (8%)
  between operations  18.3 us (6%)
  other arithmetic  10.9 us (3%)
    all_gather x1, waiting for transfers between devices, local(): parameter_collection = lax.all_gather(w_qkv, 'ctx', axis=0, tiled=True)  99.3 us
    reduce_scatter x1, waiting for transfers between devices, local(): lax.psum_scatter(jnp.dot(normed_heads, out_columns, preferred_element_typ...  48.7 us
    ppermute x11, waiting for transfers between devices, shifted(): return lax.ppermute(part.astype(kind), axis, pairs).astype(jnp.float32)  45.5 us
    all_gather x1, waiting for transfers between devices, local(): every_row_list = lax.all_gather(normed, 'tp', axis=0, tiled=True)  38.2 us
    ppermute x11, starting transfers between devices, shifted(): return lax.ppermute(part.astype(kind), axis, pairs).astype(jnp.float32)  32.6 us
    dot_general x1, matrix products, local(): jnp.dot(every_row_list, parameter_collection, preferred_element_type=jnp....  10.9 us
    dot_general x1, matrix products, local(): jnp.dot(normed_heads, out_columns, preferred_element_type=jnp.float32)  7.74 us
  transfers between devices with their start and end apart: 15, of which 10 were waited for; matrix products, arithmetic and copies ran while one was open for 8% of the time, Pallas kernels for 0%

profile of v1, /device:TPU:224, one launch (start us, length us, event | category | flops | bytes accessed | tf_op | source)
XLA Modules:
  0.0 324.9 jit_solution(11162119031132698088)
XLA Ops:
  6.5 1.4 fusion.1
  8.0 2.3 fusion.3
  10.3 0.7 all-gather.6.cloned.1.call-update
  11.1 0.7 all-gather.8.cloned.1.call-update
  12.5 0.3 reduce-window.24
  12.8 0.1 slice.33
  12.9 0.3 reduce-window.16
  13.2 0.1 slice.31
  13.3 0.1 slice_reduce_fusion
  13.4 0.1 slice_reduce_fusion.1
  13.5 0.1 select_multiply_fusion
  13.6 0.6 slice.36
  14.2 0.6 slice.37
  14.8 1.2 exponential_select_fusion
  16.1 38.2 %all-gather.4.cloned.1.call-done = bf16[768,4096]{1,0:T(8,128)(2,1)} async-done(((bf16[96,4096]{1,0:T(8,128)(2,1)}), bf16[768,4096]{1,0:T(8,128)(2,1)}) %all-gather.4.cloned.1.call-update) | async-done | bytes 6291472 | tf_op jit(solution)/shard_map/all_gather | solution.py:100
  54.3 99.3 %all-gather.6.cloned.1.call-done = bf16[4096,1024]{1,0:T(8,128)(2,1)} async-done(((bf16[128,1024]{1,0:T(8,128)(2,1)}), bf16[4096,1024]{1,0:T(8,128)(2,1)}) %all-gather.6.cloned.1.call-update) | async-done | bytes 8388624 | tf_op jit(solution)/shard_map/all_gather | solution.py:101
  153.6 10.9 %convolution_convert_fusion.1 = bf16[768,1024]{1,0:T(8,128)(2,1)S(1)} fusion(bf16[768,4096]{1,0:T(8,128)(2,1)} %all-gather.4.cloned.1.call-done, bf16[4096,1024]{1,0:T(8,128)(2,1)} %all-gather.6.cloned.1.call-done), kind=kOutput, calls=%fused_computation.7 | convolution fusion | flops 6443237376 | bytes 16252928 | tf_op jit(solution)/shard_map/dot_general | solution.py:102
  164.6 0.6 fusion.13
  165.1 0.6 copy-done.1
  165.7 3.4 %collective-permute-start.5 = (bf16[1,256,512]{2,1,0:T(8,128)(2,1)S(1)}, bf16[1,256,512]{2,1,0:T(8,128)(2,1)S(1)}, u32[]{:S(2)}, u32[]{:S(2)}) collective-permute-start(bf16[1,256,512]{2,1,0:T(8,128)(2,1)S(1)} %fusion.13), channel_id=1, source_target_pairs={{0,16},{8,24},{16,32},{24,40},{32,48},{40,56},{48,64},{56,72},{64,... | collective-permute-start | bytes 786440 | tf_op jit(solution)/shard_map/ppermute | solution.py:22
  169.1 2.1 collective-permute-start.6
  172.5 8.5 %collective-permute-start = (f32[1]{0:T(128)}, f32[1]{0:T(128)}, u32[]{:S(2)}, u32[]{:S(2)}) collective-permute-start(f32[1]{0:T(128)} %bitcast.6), channel_id=1, source_target_pairs={{0,8},{8,16},{16,24},{24,32},{32,40},{40,48},{48,56},{56,64},{64,7... | collective-permute-start | bytes 20 | tf_op jit(solution)/shard_map/ppermute | solution.py:22
  181.0 3.9 %collective-permute-done = f32[1]{0:T(128)} collective-permute-done((f32[1]{0:T(128)}, f32[1]{0:T(128)}, u32[]{:S(2)}, u32[]{:S(2)}) %collective-permute-start) | collective-permute-done | bytes 36 | tf_op jit(solution)/shard_map/ppermute | solution.py:22
  184.9 0.6 fusion.25
  185.5 2.9 collective-permute-start.7
  188.4 5.7 %collective-permute-start.1 = (f32[1]{0:T(128)}, f32[1]{0:T(128)}, u32[]{:S(2)}, u32[]{:S(2)}) collective-permute-start(f32[1]{0:T(128)} %bitcast.6), channel_id=1, source_target_pairs={{0,16},{8,24},{16,32},{24,40},{32,48},{40,56},{48,64},{56,72},{64,... | collective-permute-start | bytes 20 | tf_op jit(solution)/shard_map/ppermute | solution.py:22
  194.1 3.6 %collective-permute-done.1 = f32[1]{0:T(128)} collective-permute-done((f32[1]{0:T(128)}, f32[1]{0:T(128)}, u32[]{:S(2)}, u32[]{:S(2)}) %collective-permute-start.1) | collective-permute-done | bytes 36 | tf_op jit(solution)/shard_map/ppermute | solution.py:22
  198.8 0.7 fusion.44
  199.5 1.3 collective-permute-start.8
  200.8 3.6 %collective-permute-start.2 = (f32[1]{0:T(128)}, f32[1]{0:T(128)}, u32[]{:S(2)}, u32[]{:S(2)}) collective-permute-start(f32[1]{0:T(128)} %mul.163), channel_id=1, source_target_pairs={{0,16},{8,24},{16,32},{24,40},{32,48},{40,56},{48,64},{56,72},{64,... | collective-permute-start | bytes 20 | tf_op jit(solution)/shard_map/ppermute | solution.py:22
  204.4 4.2 %collective-permute-done.2 = f32[1]{0:T(128)} collective-permute-done((f32[1]{0:T(128)}, f32[1]{0:T(128)}, u32[]{:S(2)}, u32[]{:S(2)}) %collective-permute-start.2) | collective-permute-done | bytes 36 | tf_op jit(solution)/shard_map/ppermute | solution.py:22
  209.2 0.7 fusion.34
  209.9 1.3 collective-permute-start.9
  211.2 1.3 collective-permute-start.3
  212.5 4.7 %collective-permute-done.3 = f32[1]{0:T(128)} collective-permute-done((f32[1]{0:T(128)}, f32[1]{0:T(128)}, u32[]{:S(2)}, u32[]{:S(2)}) %collective-permute-start.3) | collective-permute-done | bytes 36 | tf_op jit(solution)/shard_map/ppermute | solution.py:22
  217.9 1.3 collective-permute-start.4
  219.2 20.1 %collective-permute-done.4 = f32[1]{0:T(128)} collective-permute-done((f32[1]{0:T(128)}, f32[1]{0:T(128)}, u32[]{:S(2)}, u32[]{:S(2)}) %collective-permute-start.4) | collective-permute-done | bytes 36 | tf_op jit(solution)/shard_map/ppermute | solution.py:22
  239.9 0.8 fusion.36
  240.7 1.3 collective-permute-start.10
  242.0 4.0 %fusion.5 = f32[768,512]{0,1:T(8,128)} fusion(f32[768]{0:T(1024)S(1)} %multiply_reduce_fusion.1, f32[768]{0:T(1024)S(1)} %get-tuple-element.7, s32[768]{0:T(1024)S(1)} %get-tuple-element.6, bf16[768,1024]{1,0:T(8,128)(2,1)} %copy-done.1), kind=kOutput, calls=%fused_computation.15 | convolution fusion | flops 911867904 | bytes 3166208 | tf_op jit(solution)/shard_map/dot_general | solution.py:61
  246.0 9.0 %collective-permute-done.10 = bf16[1,256,512]{2,1,0:T(8,128)(2,1)S(1)} collective-permute-done((bf16[1,256,512]{2,1,0:T(8,128)(2,1)S(1)}, bf16[1,256,512]{2,1,0:T(8,128)(2,1)S(1)}, u32[]{:S(2)}, u32[]{:S(2)}) %collective-permute-start.10) | collective-permute-done | bytes 262176 | tf_op jit(solution)/shard_map/ppermute | solution.py:22
  255.0 4.0 %fusion.45 = (f32[768]{0:T(1024)S(1)}, f32[768,512]{0,1:T(8,128)S(1)}) fusion(f32[768,512]{0,1:T(8,128)} %fusion.5, bf16[1,256,512]{2,1,0:T(8,128)(2,1)S(1)} %collective-permute-done.10, f32[]{:T(128)} %bitcast.7, bf16[1,256,512]{2,1,0:T(8,128)(2,1)S(1)} %collective-permute-done.8, f32[]{:T(128)} %bitcast.9, ...), kind=kOutput, calls=%fused_computation.73 | convolution fusion | flops 1211235584 | bytes 5120512 | tf_op jit(solution)/shard_map/dot_general | solution.py:76
  259.0 0.2 multiply_reduce_fusion
  259.2 0.1 all-gather.8.cloned.1.call-done
  259.3 0.4 copy-done.5
  259.7 7.7 %convolution_convert_fusion = bf16[768,4096]{1,0:T(8,128)(2,1)} fusion(bf16[512,4096]{1,0:T(8,128)(2,1)} %all-gather.8.cloned.1.call-done, f32[768,512]{0,1:T(8,128)S(1)} %get-tuple-element.9, f32[512]{0:T(512)S(1)} %copy-done.5, f32[768]{0:T(1024)S(1)} %add_rsqrt_fusion, f32[768]{0:T(1024)S(1)} %broadcast_multiply_fusion), kind=kOutput, calls=%fused_computation | convolution fusion | flops 3225944064 | bytes 12066816 | tf_op jit(solution)/shard_map/dot_general | solution.py:137
  267.5 48.7 %reduce-scatter.2.cloned.1.call-done = bf16[96,4096]{1,0:T(8,128)(2,1)} async-done(((bf16[768,4096]{1,0:T(8,128)(2,1)}), bf16[96,4096]{1,0:T(8,128)(2,1)}) %reduce-scatter.2.cloned.1.call-update) | async-done | bytes 786448 | tf_op jit(solution)/shard_map/reduce_scatter | solution.py:136
  316.2 2.2 fusion.4
  (29 shorter events, 0.3 us)
Async XLA Ops:
  6.5 47.8 %all-gather.4.cloned.1.call-start = ((), (), s32[]{:S(2)}) async-start(), calls=%async_computation.1 | async-start | bytes 7077888 | tf_op jit(solution)/shard_map/all_gather | solution.py:100
  7.9 4.5 %copy-start.4 = (s32[1,768]{1,0:T(1,128)S(1)}, s32[1,768]{1,0:T(1,128)}, u32[]{:S(2)}) copy-start(s32[1,768]{1,0:T(1,128)} %param.15) | copy-start | bytes 9220
  7.9 5.0 %copy-start.2 = (s32[768]{0:T(1024)S(1)}, s32[768]{0:T(1024)}, u32[]{:S(2)}) copy-start(s32[768]{0:T(1024)} %param.17) | copy-start | bytes 9220
  8.0 6.9 %copy-start.3 = (s32[1,768]{1,0:T(1,128)S(1)}, s32[1,768]{1,0:T(1,128)}, u32[]{:S(2)}) copy-start(s32[1,768]{1,0:T(1,128)} %param.14) | copy-start | bytes 9220
  10.3 143.4 %all-gather.6.cloned.1.call-start = ((), (), s32[]{:S(2)}) async-start(), calls=%async_computation.2 | async-start | bytes 8650752 | tf_op jit(solution)/shard_map/all_gather | solution.py:101
  11.0 248.3 %all-gather.8.cloned.1.call-start = ((), (), s32[]{:S(2)}) async-start(), calls=%async_computation.3 | async-start | bytes 4325376 | tf_op jit(solution)/shard_map/all_gather | solution.py:135
  11.8 304.4 %reduce-scatter.2.cloned.1.call-start = ((), (), s32[]{:S(2)}) async-start(), calls=%async_computation.4 | async-start | bytes 7077888 | tf_op jit(solution)/shard_map/reduce_scatter | solution.py:136
  164.5 1.2 copy-start.1
  165.7 19.2 %collective-permute-start.5 = (bf16[1,256,512]{2,1,0:T(8,128)(2,1)S(1)}, bf16[1,256,512]{2,1,0:T(8,128)(2,1)S(1)}, u32[]{:S(2)}, u32[]{:S(2)}) collective-permute-start(bf16[1,256,512]{2,1,0:T(8,128)(2,1)S(1)} %fusion.13), channel_id=1, source_target_pairs={{0,16},{8,24},{16,32},{24,40},{32,48},{40,56},{48,64},{56,72},{64,... | collective-permute-start | bytes 786440 | tf_op jit(solution)/shard_map/ppermute | solution.py:22
  169.1 15.8 %collective-permute-start.6 = (bf16[1,256,512]{2,1,0:T(8,128)(2,1)S(1)}, bf16[1,256,512]{2,1,0:T(8,128)(2,1)S(1)}, u32[]{:S(2)}, u32[]{:S(2)}) collective-permute-start(bf16[1,256,512]{2,1,0:T(8,128)(2,1)S(1)} %fusion.13), channel_id=1, source_target_pairs={{0,8},{8,16},{16,24},{24,32},{32,40},{40,48},{48,56},{56,64},{64,7... | collective-permute-start | bytes 786440 | tf_op jit(solution)/shard_map/ppermute | solution.py:22
  172.5 12.4 %collective-permute-start = (f32[1]{0:T(128)}, f32[1]{0:T(128)}, u32[]{:S(2)}, u32[]{:S(2)}) collective-permute-start(f32[1]{0:T(128)} %bitcast.6), channel_id=1, source_target_pairs={{0,8},{8,16},{16,24},{24,32},{32,40},{40,48},{48,56},{56,64},{64,7... | collective-permute-start | bytes 20 | tf_op jit(solution)/shard_map/ppermute | solution.py:22
  185.5 13.3 %collective-permute-start.7 = (bf16[1,256,512]{2,1,0:T(8,128)(2,1)S(1)}, bf16[1,256,512]{2,1,0:T(8,128)(2,1)S(1)}, u32[]{:S(2)}, u32[]{:S(2)}) collective-permute-start(bf16[1,256,512]{2,1,0:T(8,128)(2,1)S(1)} %fusion.25), channel_id=1, source_target_pairs={{0,16},{8,24},{16,32},{24,40},{32,48},{40,56},{48,64},{56,72},{64,... | collective-permute-start | bytes 786440 | tf_op jit(solution)/shard_map/ppermute | solution.py:22
  188.4 9.3 %collective-permute-start.1 = (f32[1]{0:T(128)}, f32[1]{0:T(128)}, u32[]{:S(2)}, u32[]{:S(2)}) collective-permute-start(f32[1]{0:T(128)} %bitcast.6), channel_id=1, source_target_pairs={{0,16},{8,24},{16,32},{24,40},{32,48},{40,56},{48,64},{56,72},{64,... | collective-permute-start | bytes 20 | tf_op jit(solution)/shard_map/ppermute | solution.py:22
  199.5 9.7 %collective-permute-start.8 = (bf16[1,256,512]{2,1,0:T(8,128)(2,1)S(1)}, bf16[1,256,512]{2,1,0:T(8,128)(2,1)S(1)}, u32[]{:S(2)}, u32[]{:S(2)}) collective-permute-start(bf16[1,256,512]{2,1,0:T(8,128)(2,1)S(1)} %fusion.44), channel_id=1, source_target_pairs={{0,32},{8,40},{16,48},{24,56},{32,64},{40,72},{48,80},{56,88},{64,... | collective-permute-start | bytes 786440 | tf_op jit(solution)/shard_map/ppermute | solution.py:22
  200.8 7.8 %collective-permute-start.2 = (f32[1]{0:T(128)}, f32[1]{0:T(128)}, u32[]{:S(2)}, u32[]{:S(2)}) collective-permute-start(f32[1]{0:T(128)} %mul.163), channel_id=1, source_target_pairs={{0,16},{8,24},{16,32},{24,40},{32,48},{40,56},{48,64},{56,72},{64,... | collective-permute-start | bytes 20 | tf_op jit(solution)/shard_map/ppermute | solution.py:22
  209.9 30.0 %collective-permute-start.9 = (bf16[1,256,512]{2,1,0:T(8,128)(2,1)S(1)}, bf16[1,256,512]{2,1,0:T(8,128)(2,1)S(1)}, u32[]{:S(2)}, u32[]{:S(2)}) collective-permute-start(bf16[1,256,512]{2,1,0:T(8,128)(2,1)S(1)} %fusion.34), channel_id=1, source_target_pairs={{0,64},{8,72},{16,80},{24,88},{32,96},{40,104},{48,112},{56,120},{... | collective-permute-start | bytes 786440 | tf_op jit(solution)/shard_map/ppermute | solution.py:22
  211.2 6.0 %collective-permute-start.3 = (f32[1]{0:T(128)}, f32[1]{0:T(128)}, u32[]{:S(2)}, u32[]{:S(2)}) collective-permute-start(f32[1]{0:T(128)} %mul.164), channel_id=1, source_target_pairs={{0,32},{8,40},{16,48},{24,56},{32,64},{40,72},{48,80},{56,88},{64,... | collective-permute-start | bytes 20 | tf_op jit(solution)/shard_map/ppermute | solution.py:22
  217.9 21.4 %collective-permute-start.4 = (f32[1]{0:T(128)}, f32[1]{0:T(128)}, u32[]{:S(2)}, u32[]{:S(2)}) collective-permute-start(f32[1]{0:T(128)} %mul.165), channel_id=1, source_target_pairs={{0,64},{8,72},{16,80},{24,88},{32,96},{40,104},{48,112},{56,120},{... | collective-permute-start | bytes 20 | tf_op jit(solution)/shard_map/ppermute | solution.py:22
  240.7 14.3 %collective-permute-start.10 = (bf16[1,256,512]{2,1,0:T(8,128)(2,1)S(1)}, bf16[1,256,512]{2,1,0:T(8,128)(2,1)S(1)}, u32[]{:S(2)}, u32[]{:S(2)}) collective-permute-start(bf16[1,256,512]{2,1,0:T(8,128)(2,1)S(1)} %fusion.36), channel_id=1, source_target_pairs={{0,128},{8,136},{16,144},{24,152},{32,160},{40,168},{48,176},{56,1... | collective-permute-start | bytes 786440 | tf_op jit(solution)/shard_map/ppermute | solution.py:22
  259.0 0.7 copy-start.5
  267.4 48.8 %copy-start = (bf16[96,4096]{1,0:T(8,128)(2,1)S(1)}, bf16[96,4096]{1,0:T(8,128)(2,1)}, u32[]{:S(2)}) copy-start(bf16[96,4096]{1,0:T(8,128)(2,1)} %param.9) | copy-start | bytes 2359300
Sparse Core Ops, SparseCore 0:
  10.4 43.8 all-gather.3
  56.9 96.7 all-gather.5
  156.1 103.1 all-gather.7
  267.6 48.5 reduce-scatter.1

commit v2 on v1

--- a/solution.py
+++ b/solution.py
@@ -16,22 +16,28 @@
     count = lax.axis_size(axis)
     if count == 1:
         return jnp.zeros_like(state)
+    heads, rows, width = state.shape
+    pad = 16
 
-    def shifted(part, k, kind):
+    def shifted(decay, total, k):
+        high = decay.astype(jnp.bfloat16)
+        low = (decay - high.astype(jnp.float32)).astype(jnp.bfloat16)
+        extra = jnp.zeros((heads, pad, width), jnp.bfloat16)
+        extra = extra.at[:, 0, 0].set(high).at[:, 0, 1].set(low)
+        message = jnp.concatenate([total.astype(jnp.bfloat16), extra], axis=1)
         pairs = [(i, i + k) for i in range(count - k)]
-        return lax.ppermute(part.astype(kind), axis, pairs).astype(jnp.float32)
+        got = lax.ppermute(message, axis, pairs)
+        got_decay = got[:, rows, 0].astype(jnp.float32) + got[:, rows, 1].astype(jnp.float32)
+        return got_decay, got[:, :rows].astype(jnp.float32)
 
-    decay = shifted(passing, 1, jnp.float32)
-    total = shifted(state, 1, jnp.bfloat16)
+    decay, total = shifted(passing, state, 1)
     if count > 2:
-        decay_far = shifted(passing, 2, jnp.float32)
-        total_far = shifted(state, 2, jnp.bfloat16)
+        decay_far, total_far = shifted(passing, state, 2)
         total = decay[:, None, None] * total_far + total
         decay = decay * decay_far
     k = 2
     while k < count:
-        decay_far = shifted(decay, k, jnp.float32)
-        total_far = shifted(total, k, jnp.bfloat16)
+        decay_far, total_far = shifted(decay, total, k)
         total = decay[:, None, None] * total_far + total
         decay = decay * decay_far
         k *= 2

time: 328 us -> 331 us (level)
  starting transfers between devices: 32.7 us -> 12.8 us
  waiting for transfers between devices: 233 us -> 246 us
  local copies, waits for them, and re-layouts: 2.56 us -> 12 us
  between operations: 18.3 us -> 21.8 us
    ppermute x11 -> x6, starting transfers between devices: 32.6 us -> 12.7 us  [shifted(): got = lax.ppermute(message, axis, pairs)]
    ppermute x11 -> x6, waiting for transfers between devices: 45.5 us -> 57.6 us  [shifted(): got = lax.ppermute(message, axis, pairs)]
    scatter x0 -> x10, local copies, waits for them, and re-layouts: none -> 6.7 us  [shifted(): extra = extra.at[:, 0, 0].set(high).at[:, 0, 1].set(low)]
  transfers between devices with their start and end apart: 15 -> 10, of which waited for: 10 -> 9; matrix products, arithmetic and copies ran while one was open for 8% -> 10% of each run, Pallas kernels for 0% -> 0%
where the time goes in v2:
time: 331 us; the launch traced here: 328 us
  waiting for transfers between devices  246 us (74%)
  matrix products  26.7 us (8%)
  between operations  21.8 us (7%)
  starting transfers between devices  12.8 us (4%)
  local copies, waits for them, and re-layouts  12 us (4%)
  other arithmetic  8.73 us (3%)
    all_gather x1, waiting for transfers between devices, local(): parameter_collection = lax.all_gather(w_qkv, 'ctx', axis=0, tiled=True)  99.3 us
    ppermute x6, waiting for transfers between devices, shifted(): got = lax.ppermute(message, axis, pairs)  57.6 us
    reduce_scatter x1, waiting for transfers between devices, local(): lax.psum_scatter(jnp.dot(normed_heads, out_columns, preferred_element_typ...  49.2 us
    all_gather x1, waiting for transfers between devices, local(): every_row_list = lax.all_gather(normed, 'tp', axis=0, tiled=True)  35.1 us
    ppermute x6, starting transfers between devices, shifted(): got = lax.ppermute(message, axis, pairs)  12.7 us
    dot_general x1, matrix products, local(): jnp.dot(every_row_list, parameter_collection, preferred_element_type=jnp....  10.9 us
    dot_general x1, matrix products, local(): jnp.dot(normed_heads, out_columns, preferred_element_type=jnp.float32)  7.74 us
    scatter x10, local copies, waits for them, and re-layouts, shifted(): extra = extra.at[:, 0, 0].set(high).at[:, 0, 1].set(low)  6.7 us
  transfers between devices with their start and end apart: 10, of which 9 were waited for; matrix products, arithmetic and copies ran while one was open for 10% of the time, Pallas kernels for 0%

profile of v2, /device:TPU:224, one launch (start us, length us, event | category | flops | bytes accessed | tf_op | source)
XLA Modules:
  0.0 327.6 jit_solution(11120573122175856235)
XLA Ops:
  6.5 1.4 fusion.1
  8.0 2.3 fusion.3
  10.3 0.7 all-gather.6.cloned.1.call-update
  11.1 0.7 all-gather.8.cloned.1.call-update
  12.5 0.3 reduce-window.24
  12.9 0.3 reduce-window.16
  13.3 0.1 slice_reduce_fusion
  13.4 0.1 slice_reduce_fusion.1
  13.6 0.6 slice.305
  14.7 0.6 slice.306
  16.0 0.6 fusion.51
  16.6 1.3 scatter.35
  18.0 1.2 exponential_select_fusion
  19.2 35.1 %all-gather.4.cloned.1.call-done = bf16[768,4096]{1,0:T(8,128)(2,1)} async-done(((bf16[96,4096]{1,0:T(8,128)(2,1)}), bf16[768,4096]{1,0:T(8,128)(2,1)}) %all-gather.4.cloned.1.call-update) | async-done | bytes 6291472 | tf_op jit(solution)/shard_map/all_gather | solution.py:106
  54.3 99.3 %all-gather.6.cloned.1.call-done = bf16[4096,1024]{1,0:T(8,128)(2,1)} async-done(((bf16[128,1024]{1,0:T(8,128)(2,1)}), bf16[4096,1024]{1,0:T(8,128)(2,1)}) %all-gather.6.cloned.1.call-update) | async-done | bytes 8388624 | tf_op jit(solution)/shard_map/all_gather | solution.py:107
  153.6 10.9 %convolution_convert_fusion.1 = bf16[768,1024]{1,0:T(8,128)(2,1)S(1)} fusion(bf16[768,4096]{1,0:T(8,128)(2,1)} %all-gather.4.cloned.1.call-done, bf16[4096,1024]{1,0:T(8,128)(2,1)} %all-gather.6.cloned.1.call-done), kind=kOutput, calls=%fused_computation.7 | convolution fusion | flops 6443237376 | bytes 16252928 | tf_op jit(solution)/shard_map/dot_general | solution.py:108
  164.6 0.6 fusion.13
  165.2 2.1 collective-permute-start
  167.3 4.0 %collective-permute-start.1 = (bf16[1,272,512]{2,1,0:T(8,128)(2,1)S(1)}, bf16[1,272,512]{2,1,0:T(8,128)(2,1)S(1)}, u32[]{:S(2)}, u32[]{:S(2)}) collective-permute-start(bf16[1,272,512]{2,1,0:T(8,128)(2,1)S(1)} %pad_maximum_fusion), channel_id=1, source_target_pairs={{0,16},{8,24},{16,32},{24,40},{32,48},{40,56},{48,64},{56,72},{64,... | collective-permute-start | bytes 835592 | tf_op jit(solution)/shard_map/ppermute | solution.py:29
  171.3 11.8 %collective-permute-done = bf16[1,272,512]{2,1,0:T(8,128)(2,1)S(1)} collective-permute-done((bf16[1,272,512]{2,1,0:T(8,128)(2,1)S(1)}, bf16[1,272,512]{2,1,0:T(8,128)(2,1)S(1)}, u32[]{:S(2)}, u32[]{:S(2)}) %collective-permute-start) | collective-permute-done | bytes 278560 | tf_op jit(solution)/shard_map/ppermute | solution.py:29
  183.0 0.6 fusion.50
  184.9 0.6 fusion.49
  186.8 1.3 scatter.39
  188.1 0.1 fusion.25
  188.3 2.7 collective-permute-start.2
  191.0 9.1 %collective-permute-done.2 = bf16[1,272,512]{2,1,0:T(8,128)(2,1)S(1)} collective-permute-done((bf16[1,272,512]{2,1,0:T(8,128)(2,1)S(1)}, bf16[1,272,512]{2,1,0:T(8,128)(2,1)S(1)}, u32[]{:S(2)}, u32[]{:S(2)}) %collective-permute-start.2) | collective-permute-done | bytes 278560 | tf_op jit(solution)/shard_map/ppermute | solution.py:29
  200.1 0.7 fusion.48
  202.0 1.3 scatter.41
  203.4 0.1 fusion.45
  203.5 1.3 collective-permute-start.3
  204.8 7.1 %collective-permute-done.3 = bf16[1,272,512]{2,1,0:T(8,128)(2,1)S(1)} collective-permute-done((bf16[1,272,512]{2,1,0:T(8,128)(2,1)S(1)}, bf16[1,272,512]{2,1,0:T(8,128)(2,1)S(1)}, u32[]{:S(2)}, u32[]{:S(2)}) %collective-permute-start.3) | collective-permute-done | bytes 278560 | tf_op jit(solution)/shard_map/ppermute | solution.py:29
  212.0 0.7 fusion.47
  213.9 1.3 scatter.45
  215.3 0.2 fusion.34
  215.5 1.3 collective-permute-start.4
  216.8 16.1 %collective-permute-done.4 = bf16[1,272,512]{2,1,0:T(8,128)(2,1)S(1)} collective-permute-done((bf16[1,272,512]{2,1,0:T(8,128)(2,1)S(1)}, bf16[1,272,512]{2,1,0:T(8,128)(2,1)S(1)}, u32[]{:S(2)}, u32[]{:S(2)}) %collective-permute-start.4) | collective-permute-done | bytes 278560 | tf_op jit(solution)/shard_map/ppermute | solution.py:29
  232.9 0.7 fusion.46
  234.8 1.3 scatter.49
  236.2 0.2 fusion.37
  236.4 1.3 collective-permute-start.5
  237.7 4.0 %fusion.5 = f32[768,512]{0,1:T(8,128)} fusion(f32[768]{0:T(1024)S(1)} %multiply_reduce_fusion.1, f32[768]{0:T(1024)S(1)} %get-tuple-element.143, s32[768]{0:T(1024)S(1)} %get-tuple-element.142, bf16[768,1024]{1,0:T(8,128)(2,1)} %copy-done.1), kind=kOutput, calls=%fused_computation.15 | convolution fusion | flops 911867904 | bytes 3166208 | tf_op jit(solution)/shard_map/dot_general | solution.py:67
  241.7 13.6 %collective-permute-done.5 = bf16[1,272,512]{2,1,0:T(8,128)(2,1)S(1)} collective-permute-done((bf16[1,272,512]{2,1,0:T(8,128)(2,1)S(1)}, bf16[1,272,512]{2,1,0:T(8,128)(2,1)S(1)}, u32[]{:S(2)}, u32[]{:S(2)}) %collective-permute-start.5) | collective-permute-done | bytes 278560 | tf_op jit(solution)/shard_map/ppermute | solution.py:29
  255.3 3.5 %fusion.52 = (f32[768]{0:T(1024)S(1)}, f32[768,512]{0,1:T(8,128)S(1)}) fusion(f32[768,512]{0,1:T(8,128)} %fusion.5, bf16[1,272,512]{2,1,0:T(8,128)(2,1)S(1)} %collective-permute-done.5, f32[]{:T(128)} %bitcast.25, bf16[1,272,512]{2,1,0:T(8,128)(2,1)S(1)} %collective-permute-done.3, f32[]{:T(128)} %bitcast.21, ...), kind=kOutput, calls=%fused_computation.85 | convolution fusion | flops 1211235584 | bytes 5121536 | tf_op jit(solution)/shard_map/dot_general | solution.py:82
  258.8 0.2 multiply_reduce_fusion
  259.0 2.9 all-gather.8.cloned.1.call-done
  261.9 7.7 %convolution_convert_fusion = bf16[768,4096]{1,0:T(8,128)(2,1)} fusion(bf16[512,4096]{1,0:T(8,128)(2,1)} %all-gather.8.cloned.1.call-done, f32[768,512]{0,1:T(8,128)S(1)} %get-tuple-element.157, f32[512]{0:T(512)S(1)} %copy-done.5, f32[768]{0:T(1024)S(1)} %add_rsqrt_fusion, f32[768]{0:T(1024)S(1)} %broadcast_multiply_fusion), kind=kOutput, calls=%fused_computation | convolution fusion | flops 3225944064 | bytes 12066816 | tf_op jit(solution)/shard_map/dot_general | solution.py:143
  269.6 49.2 %reduce-scatter.2.cloned.1.call-done = bf16[96,4096]{1,0:T(8,128)(2,1)} async-done(((bf16[768,4096]{1,0:T(8,128)(2,1)}), bf16[96,4096]{1,0:T(8,128)(2,1)}) %reduce-scatter.2.cloned.1.call-update) | async-done | bytes 786448 | tf_op jit(solution)/shard_map/reduce_scatter | solution.py:142
  318.9 2.2 fusion.4
  (41 shorter events, 0.7 us)
Async XLA Ops:
  6.5 47.8 %all-gather.4.cloned.1.call-start = ((), (), s32[]{:S(2)}) async-start(), calls=%async_computation.1 | async-start | bytes 7077888 | tf_op jit(solution)/shard_map/all_gather | solution.py:106
  7.9 4.5 %copy-start.4 = (s32[1,768]{1,0:T(1,128)S(1)}, s32[1,768]{1,0:T(1,128)}, u32[]{:S(2)}) copy-start(s32[1,768]{1,0:T(1,128)} %param.39) | copy-start | bytes 9220
  7.9 5.0 %copy-start.2 = (s32[768]{0:T(1024)S(1)}, s32[768]{0:T(1024)}, u32[]{:S(2)}) copy-start(s32[768]{0:T(1024)} %param.41) | copy-start | bytes 9220
  8.0 10.0 %copy-start.3 = (s32[1,768]{1,0:T(1,128)S(1)}, s32[1,768]{1,0:T(1,128)}, u32[]{:S(2)}) copy-start(s32[1,768]{1,0:T(1,128)} %param.38) | copy-start | bytes 9220
  10.3 143.4 %all-gather.6.cloned.1.call-start = ((), (), s32[]{:S(2)}) async-start(), calls=%async_computation.2 | async-start | bytes 8650752 | tf_op jit(solution)/shard_map/all_gather | solution.py:107
  11.0 250.8 %all-gather.8.cloned.1.call-start = ((), (), s32[]{:S(2)}) async-start(), calls=%async_computation.3 | async-start | bytes 4325376 | tf_op jit(solution)/shard_map/all_gather | solution.py:141
  11.8 307.1 %reduce-scatter.2.cloned.1.call-start = ((), (), s32[]{:S(2)}) async-start(), calls=%async_computation.4 | async-start | bytes 7077888 | tf_op jit(solution)/shard_map/reduce_scatter | solution.py:142
  164.5 20.4 %copy-start.1 = (bf16[768,1024]{1,0:T(8,128)(2,1)}, bf16[768,1024]{1,0:T(8,128)(2,1)S(1)}, u32[]{:S(2)}) copy-start(bf16[768,1024]{1,0:T(8,128)(2,1)S(1)} %convolution_convert_fusion.1) | copy-start | bytes 4718596
  165.2 17.9 %collective-permute-start = (bf16[1,272,512]{2,1,0:T(8,128)(2,1)S(1)}, bf16[1,272,512]{2,1,0:T(8,128)(2,1)S(1)}, u32[]{:S(2)}, u32[]{:S(2)}) collective-permute-start(bf16[1,272,512]{2,1,0:T(8,128)(2,1)S(1)} %pad_maximum_fusion), channel_id=1, source_target_pairs={{0,8},{8,16},{16,24},{24,32},{32,40},{40,48},{48,56},{56,64},{64,7... | collective-permute-start | bytes 835592 | tf_op jit(solution)/shard_map/ppermute | solution.py:29
  167.3 17.6 %collective-permute-start.1 = (bf16[1,272,512]{2,1,0:T(8,128)(2,1)S(1)}, bf16[1,272,512]{2,1,0:T(8,128)(2,1)S(1)}, u32[]{:S(2)}, u32[]{:S(2)}) collective-permute-start(bf16[1,272,512]{2,1,0:T(8,128)(2,1)S(1)} %pad_maximum_fusion), channel_id=1, source_target_pairs={{0,16},{8,24},{16,32},{24,40},{32,48},{40,56},{48,64},{56,72},{64,... | collective-permute-start | bytes 835592 | tf_op jit(solution)/shard_map/ppermute | solution.py:29
  188.3 11.8 %collective-permute-start.2 = (bf16[1,272,512]{2,1,0:T(8,128)(2,1)S(1)}, bf16[1,272,512]{2,1,0:T(8,128)(2,1)S(1)}, u32[]{:S(2)}, u32[]{:S(2)}) collective-permute-start(bf16[1,272,512]{2,1,0:T(8,128)(2,1)S(1)} %pad_maximum_fusion.1), channel_id=1, source_target_pairs={{0,16},{8,24},{16,32},{24,40},{32,48},{40,56},{48,64},{56,72},{64,... | collective-permute-start | bytes 835592 | tf_op jit(solution)/shard_map/ppermute | solution.py:29
  203.5 8.4 %collective-permute-start.3 = (bf16[1,272,512]{2,1,0:T(8,128)(2,1)S(1)}, bf16[1,272,512]{2,1,0:T(8,128)(2,1)S(1)}, u32[]{:S(2)}, u32[]{:S(2)}) collective-permute-start(bf16[1,272,512]{2,1,0:T(8,128)(2,1)S(1)} %pad_maximum_fusion.2), channel_id=1, source_target_pairs={{0,32},{8,40},{16,48},{24,56},{32,64},{40,72},{48,80},{56,88},{64,... | collective-permute-start | bytes 835592 | tf_op jit(solution)/shard_map/ppermute | solution.py:29
  215.5 17.4 %collective-permute-start.4 = (bf16[1,272,512]{2,1,0:T(8,128)(2,1)S(1)}, bf16[1,272,512]{2,1,0:T(8,128)(2,1)S(1)}, u32[]{:S(2)}, u32[]{:S(2)}) collective-permute-start(bf16[1,272,512]{2,1,0:T(8,128)(2,1)S(1)} %pad_maximum_fusion.3), channel_id=1, source_target_pairs={{0,64},{8,72},{16,80},{24,88},{32,96},{40,104},{48,112},{56,120},{... | collective-permute-start | bytes 835592 | tf_op jit(solution)/shard_map/ppermute | solution.py:29
  236.4 18.8 %collective-permute-start.5 = (bf16[1,272,512]{2,1,0:T(8,128)(2,1)S(1)}, bf16[1,272,512]{2,1,0:T(8,128)(2,1)S(1)}, u32[]{:S(2)}, u32[]{:S(2)}) collective-permute-start(bf16[1,272,512]{2,1,0:T(8,128)(2,1)S(1)} %pad_maximum_fusion.4), channel_id=1, source_target_pairs={{0,128},{8,136},{16,144},{24,152},{32,160},{40,168},{48,176},{56,1... | collective-permute-start | bytes 835592 | tf_op jit(solution)/shard_map/ppermute | solution.py:29
  258.8 3.1 copy-start.5
  269.6 49.3 %copy-start = (bf16[96,4096]{1,0:T(8,128)(2,1)S(1)}, bf16[96,4096]{1,0:T(8,128)(2,1)}, u32[]{:S(2)}) copy-start(bf16[96,4096]{1,0:T(8,128)(2,1)} %param.33) | copy-start | bytes 2359300
Sparse Core Ops, SparseCore 0:
  10.4 43.8 all-gather.3
  56.9 96.7 all-gather.5
  156.1 105.7 all-gather.7
  269.8 49.0 reduce-scatter.1

commit v3 on v2

--- a/solution.py
+++ b/solution.py
@@ -103,7 +103,9 @@
     document_begin_flags,
 ):
     normed = rms_rows(tokens, norm_gain)
-    every_row_list = lax.all_gather(normed, "tp", axis=0, tiled=True)
+    group = lax.axis_size("tp")
+    copies = jnp.broadcast_to(normed[None], (group,) + normed.shape)
+    every_row_list = lax.all_to_all(copies, "tp", 0, 0, tiled=True).reshape(-1, normed.shape[1])
     parameter_collection = lax.all_gather(w_qkv, "ctx", axis=0, tiled=True)
     rows_combined = jnp.dot(
         every_row_list, parameter_collection, preferred_element_type=jnp.float32

time: 331 us -> 285 us (0.86)
  waiting for transfers between devices: 246 us -> 192 us
  starting transfers between devices: 12.8 us -> 17.9 us
  local copies, waits for them, and re-layouts: 12 us -> 15.7 us
    all_gather x1, waiting for transfers between devices: 99.3 us -> 16.7 us  [local(): parameter_collection = lax.all_gather(w_qkv, 'ctx', axis=0, tiled=True)]
    all_to_all x0 -> x1, waiting for transfers between devices: none -> 63.8 us  [local(): lax.all_to_all(copies, 'tp', 0, 0, tiled=True).reshape(-1, normed.shape[1])]
    all_gather x1 -> x0, waiting for transfers between devices: 35.1 us -> none  [local(): every_row_list = lax.all_gather(normed, 'tp', axis=0, tiled=True)]
    all_to_all x0 -> x1, starting transfers between devices: none -> 4.93 us  [local(): lax.all_to_all(copies, 'tp', 0, 0, tiled=True).reshape(-1, normed.shape[1])]
    broadcast_in_dim x0 -> x1, local copies, waits for them, and re-layouts: none -> 3.35 us  [local(): copies = jnp.broadcast_to(normed[None], (group,) + normed.shape)]
  transfers between devices with their start and end apart: 10 -> 10, of which waited for: 9 -> 9; matrix products, arithmetic and copies ran while one was open for 10% -> 14% of each run, Pallas kernels for 0% -> 0%
where the time goes in v3:
time: 285 us; the launch traced here: 281 us
  waiting for transfers between devices  192 us (67%)
  matrix products  26.8 us (9%)
  between operations  21.9 us (8%)
  starting transfers between devices  17.9 us (6%)
  local copies, waits for them, and re-layouts  15.7 us (6%)
  other arithmetic  7.54 us (3%)
    all_to_all x1, waiting for transfers between devices, local(): lax.all_to_all(copies, 'tp', 0, 0, tiled=True).reshape(-1, normed.shape[1])  63.8 us
    ppermute x6, waiting for transfers between devices, shifted(): got = lax.ppermute(message, axis, pairs)  57.1 us
    reduce_scatter x1, waiting for transfers between devices, local(): lax.psum_scatter(jnp.dot(normed_heads, out_columns, preferred_element_typ...  49 us
    all_gather x1, waiting for transfers between devices, local(): parameter_collection = lax.all_gather(w_qkv, 'ctx', axis=0, tiled=True)  16.7 us
    ppermute x6, starting transfers between devices, shifted(): got = lax.ppermute(message, axis, pairs)  12.9 us
    dot_general x1, matrix products, local(): jnp.dot(every_row_list, parameter_collection, preferred_element_type=jnp....  10.9 us
    dot_general x1, matrix products, local(): jnp.dot(normed_heads, out_columns, preferred_element_type=jnp.float32)  7.74 us
    scatter x10, local copies, waits for them, and re-layouts, shifted(): extra = extra.at[:, 0, 0].set(high).at[:, 0, 1].set(low)  6.5 us
  transfers between devices with their start and end apart: 10, of which 9 were waited for; matrix products, arithmetic and copies ran while one was open for 14% of the time, Pallas kernels for 0%

profile of v3, /device:TPU:224, one launch (start us, length us, event | category | flops | bytes accessed | tf_op | source)
XLA Modules:
  0.0 281.4 jit_solution(16675667116050032039)
XLA Ops:
  6.5 0.7 all-gather.3.cloned.1.call-update
  7.3 1.4 fusion.1
  8.7 1.0 fusion.3
  9.7 3.3 %broadcast_in_dim.5 = bf16[8,96,4096]{2,1,0:T(8,128)(2,1)} broadcast(bf16[96,4096]{1,0:T(8,128)(2,1)S(1)} %fusion.3), dimensions={1,2} | broadcast | bytes 7077888 | tf_op jit(solution)/shard_map/broadcast_in_dim | solution.py:107
  13.0 4.9 %all-to-all-start = ((bf16[8,96,4096]{2,1,0:T(8,128)(2,1)}), bf16[8,96,4096]{2,1,0:T(8,128)(2,1)}, u32[]{:S(2)}, u32[]{:S(2)}) async-start(bf16[8,96,4096]{2,1,0:T(8,128)(2,1)} %broadcast_in_dim.5), calls=%async_computation | async-start | bytes 12582912 | tf_op jit(solution)/shard_map/all_to_all | solution.py:108
  18.0 0.7 all-gather.5.cloned.1.call-update
  19.4 0.3 reduce-window.24
  19.8 0.3 reduce-window.16
  20.5 0.6 slice.305
  21.8 0.6 slice.306
  23.1 0.6 fusion.51
  23.7 1.3 scatter.35
  25.0 1.3 exponential_select_fusion
  26.3 63.8 %all-to-all-done = bf16[8,96,4096]{2,1,0:T(8,128)(2,1)} async-done(((bf16[8,96,4096]{2,1,0:T(8,128)(2,1)}), bf16[8,96,4096]{2,1,0:T(8,128)(2,1)}, u32[]{:S(2)}, u32[]{:S(2)}) %all-to-all-start) | async-done | bytes 6291488 | tf_op jit(solution)/shard_map/all_to_all | solution.py:108
  90.1 16.7 %all-gather.3.cloned.1.call-done = bf16[4096,1024]{1,0:T(8,128)(2,1)} async-done(((bf16[128,1024]{1,0:T(8,128)(2,1)}), bf16[4096,1024]{1,0:T(8,128)(2,1)}) %all-gather.3.cloned.1.call-update) | async-done | bytes 8388624 | tf_op jit(solution)/shard_map/all_gather | solution.py:109
  106.8 10.9 %convolution_convert_fusion.1 = bf16[768,1024]{1,0:T(8,128)(2,1)S(1)} fusion(bf16[768,4096]{1,0:T(8,128)(2,1)} %bitcast, bf16[4096,1024]{1,0:T(8,128)(2,1)} %all-gather.3.cloned.1.call-done), kind=kOutput, calls=%fused_computation.7 | convolution fusion | flops 6443237376 | bytes 16252928 | tf_op jit(solution)/shard_map/dot_general | solution.py:110
  117.8 0.6 fusion.13
  118.4 2.1 collective-permute-start
  120.5 4.0 %collective-permute-start.1 = (bf16[1,272,512]{2,1,0:T(8,128)(2,1)S(1)}, bf16[1,272,512]{2,1,0:T(8,128)(2,1)S(1)}, u32[]{:S(2)}, u32[]{:S(2)}) collective-permute-start(bf16[1,272,512]{2,1,0:T(8,128)(2,1)S(1)} %pad_maximum_fusion), channel_id=1, source_target_pairs={{0,16},{8,24},{16,32},{24,40},{32,48},{40,56},{48,64},{56,72},{64,... | collective-permute-start | bytes 835592 | tf_op jit(solution)/shard_map/ppermute | solution.py:29
  124.5 11.8 %collective-permute-done = bf16[1,272,512]{2,1,0:T(8,128)(2,1)S(1)} collective-permute-done((bf16[1,272,512]{2,1,0:T(8,128)(2,1)S(1)}, bf16[1,272,512]{2,1,0:T(8,128)(2,1)S(1)}, u32[]{:S(2)}, u32[]{:S(2)}) %collective-permute-start) | collective-permute-done | bytes 278560 | tf_op jit(solution)/shard_map/ppermute | solution.py:29
  136.2 0.6 fusion.50
  138.1 0.6 fusion.49
  140.0 1.3 scatter.39
  141.4 2.7 collective-permute-start.2
  144.2 9.1 %collective-permute-done.2 = bf16[1,272,512]{2,1,0:T(8,128)(2,1)S(1)} collective-permute-done((bf16[1,272,512]{2,1,0:T(8,128)(2,1)S(1)}, bf16[1,272,512]{2,1,0:T(8,128)(2,1)S(1)}, u32[]{:S(2)}, u32[]{:S(2)}) %collective-permute-start.2) | collective-permute-done | bytes 278560 | tf_op jit(solution)/shard_map/ppermute | solution.py:29
  153.3 0.6 fusion.48
  155.2 1.3 scatter.41
  156.5 0.1 fusion.45
  156.7 1.3 collective-permute-start.3
  158.0 7.1 %collective-permute-done.3 = bf16[1,272,512]{2,1,0:T(8,128)(2,1)S(1)} collective-permute-done((bf16[1,272,512]{2,1,0:T(8,128)(2,1)S(1)}, bf16[1,272,512]{2,1,0:T(8,128)(2,1)S(1)}, u32[]{:S(2)}, u32[]{:S(2)}) %collective-permute-start.3) | collective-permute-done | bytes 278560 | tf_op jit(solution)/shard_map/ppermute | solution.py:29
  165.1 0.6 fusion.47
  167.0 1.3 scatter.45
  168.3 0.2 fusion.34
  168.5 1.3 collective-permute-start.4
  169.8 15.6 %collective-permute-done.4 = bf16[1,272,512]{2,1,0:T(8,128)(2,1)S(1)} collective-permute-done((bf16[1,272,512]{2,1,0:T(8,128)(2,1)S(1)}, bf16[1,272,512]{2,1,0:T(8,128)(2,1)S(1)}, u32[]{:S(2)}, u32[]{:S(2)}) %collective-permute-start.4) | collective-permute-done | bytes 278560 | tf_op jit(solution)/shard_map/ppermute | solution.py:29
  185.4 0.6 fusion.46
  187.4 1.3 scatter.49
  188.7 0.2 fusion.37
  189.0 1.5 collective-permute-start.5
  190.4 4.0 %fusion.5 = f32[768,512]{0,1:T(8,128)} fusion(f32[768]{0:T(1024)S(1)} %multiply_reduce_fusion.1, f32[768]{0:T(1024)S(1)} %get-tuple-element.143, s32[768]{0:T(1024)S(1)} %get-tuple-element.142, bf16[768,1024]{1,0:T(8,128)(2,1)} %copy-done.3), kind=kOutput, calls=%fused_computation.15 | convolution fusion | flops 911867904 | bytes 3166208 | tf_op jit(solution)/shard_map/dot_general | solution.py:67
  194.4 13.5 %collective-permute-done.5 = bf16[1,272,512]{2,1,0:T(8,128)(2,1)S(1)} collective-permute-done((bf16[1,272,512]{2,1,0:T(8,128)(2,1)S(1)}, bf16[1,272,512]{2,1,0:T(8,128)(2,1)S(1)}, u32[]{:S(2)}, u32[]{:S(2)}) %collective-permute-start.5) | collective-permute-done | bytes 278560 | tf_op jit(solution)/shard_map/ppermute | solution.py:29
  207.9 0.7 copy-done.2
  208.6 3.6 %fusion.52 = (f32[768]{0:T(1024)S(1)}, f32[768,512]{0,1:T(8,128)S(1)}) fusion(f32[768,512]{0,1:T(8,128)} %fusion.5, bf16[1,272,512]{2,1,0:T(8,128)(2,1)} %copy-done.2, f32[]{:T(128)} %bitcast.26, bf16[1,272,512]{2,1,0:T(8,128)(2,1)S(1)} %collective-permute-done.3, f32[]{:T(128)} %bitcast.22, bf16[1,272,512]{2,1,0:T(8,128)(2,1)} %copy-done.1, f32[]{:T(128)} %bitcast.27, ...), kind=kOutput, calls=%fused_computation.85 | convolution fusion | flops 1211235584 | bytes 5121536 | tf_op jit(solution)/shard_map/dot_general | solution.py:82
  212.3 0.2 multiply_reduce_fusion
  212.5 3.4 %all-gather.5.cloned.1.call-done = bf16[512,4096]{1,0:T(8,128)(2,1)} async-done(((bf16[512,128]{1,0:T(8,128)(2,1)}), bf16[512,4096]{1,0:T(8,128)(2,1)}) %all-gather.5.cloned.1.call-update) | async-done | bytes 4194320 | tf_op jit(solution)/shard_map/all_gather | solution.py:143
  215.9 7.7 %convolution_convert_fusion = bf16[768,4096]{1,0:T(8,128)(2,1)} fusion(bf16[512,4096]{1,0:T(8,128)(2,1)} %all-gather.5.cloned.1.call-done, f32[768,512]{0,1:T(8,128)S(1)} %get-tuple-element.157, f32[512]{0:T(512)S(1)} %copy-done.7, f32[768]{0:T(1024)S(1)} %add_rsqrt_fusion, f32[768]{0:T(1024)S(1)} %broadcast_multiply_fusion), kind=kOutput, calls=%fused_computation | convolution fusion | flops 3225944064 | bytes 12066816 | tf_op jit(solution)/shard_map/dot_general | solution.py:145
  223.6 49.0 %reduce-scatter.2.cloned.1.call-done = bf16[96,4096]{1,0:T(8,128)(2,1)} async-done(((bf16[768,4096]{1,0:T(8,128)(2,1)}), bf16[96,4096]{1,0:T(8,128)(2,1)}) %reduce-scatter.2.cloned.1.call-update) | async-done | bytes 786448 | tf_op jit(solution)/shard_map/reduce_scatter | solution.py:144
  272.7 2.2 fusion.4
  (45 shorter events, 0.9 us)
Async XLA Ops:
  6.5 2.1 copy-start
  6.5 100.3 %all-gather.3.cloned.1.call-start = ((), (), s32[]{:S(2)}) async-start(), calls=%async_computation.2 | async-start | bytes 8650752 | tf_op jit(solution)/shard_map/all_gather | solution.py:109
  13.0 6.4 %copy-start.6 = (s32[1,768]{1,0:T(1,128)S(1)}, s32[1,768]{1,0:T(1,128)}, u32[]{:S(2)}) copy-start(s32[1,768]{1,0:T(1,128)} %param.39) | copy-start | bytes 9220
  13.0 6.8 %copy-start.4 = (s32[768]{0:T(1024)S(1)}, s32[768]{0:T(1024)}, u32[]{:S(2)}) copy-start(s32[768]{0:T(1024)} %param.41) | copy-start | bytes 9220
  13.0 12.0 %copy-start.5 = (s32[1,768]{1,0:T(1,128)S(1)}, s32[1,768]{1,0:T(1,128)}, u32[]{:S(2)}) copy-start(s32[1,768]{1,0:T(1,128)} %param.38) | copy-start | bytes 9220
  13.0 77.1 %all-to-all-start = ((bf16[8,96,4096]{2,1,0:T(8,128)(2,1)}), bf16[8,96,4096]{2,1,0:T(8,128)(2,1)}, u32[]{:S(2)}, u32[]{:S(2)}) async-start(bf16[8,96,4096]{2,1,0:T(8,128)(2,1)} %broadcast_in_dim.5), calls=%async_computation | async-start | bytes 12582912 | tf_op jit(solution)/shard_map/all_to_all | solution.py:108
  17.9 197.9 %all-gather.5.cloned.1.call-start = ((), (), s32[]{:S(2)}) async-start(), calls=%async_computation.3 | async-start | bytes 4325376 | tf_op jit(solution)/shard_map/all_gather | solution.py:143
  18.7 254.0 %reduce-scatter.2.cloned.1.call-start = ((), (), s32[]{:S(2)}) async-start(), calls=%async_computation.4 | async-start | bytes 7077888 | tf_op jit(solution)/shard_map/reduce_scatter | solution.py:144
  117.8 20.4 %copy-start.3 = (bf16[768,1024]{1,0:T(8,128)(2,1)}, bf16[768,1024]{1,0:T(8,128)(2,1)S(1)}, u32[]{:S(2)}) copy-start(bf16[768,1024]{1,0:T(8,128)(2,1)S(1)} %convolution_convert_fusion.1) | copy-start | bytes 4718596
  118.4 17.9 %collective-permute-start = (bf16[1,272,512]{2,1,0:T(8,128)(2,1)S(1)}, bf16[1,272,512]{2,1,0:T(8,128)(2,1)S(1)}, u32[]{:S(2)}, u32[]{:S(2)}) collective-permute-start(bf16[1,272,512]{2,1,0:T(8,128)(2,1)S(1)} %pad_maximum_fusion), channel_id=1, source_target_pairs={{0,8},{8,16},{16,24},{24,32},{32,40},{40,48},{48,56},{56,64},{64,7... | collective-permute-start | bytes 835592 | tf_op jit(solution)/shard_map/ppermute | solution.py:29
  120.5 17.6 %collective-permute-start.1 = (bf16[1,272,512]{2,1,0:T(8,128)(2,1)S(1)}, bf16[1,272,512]{2,1,0:T(8,128)(2,1)S(1)}, u32[]{:S(2)}, u32[]{:S(2)}) collective-permute-start(bf16[1,272,512]{2,1,0:T(8,128)(2,1)S(1)} %pad_maximum_fusion), channel_id=1, source_target_pairs={{0,16},{8,24},{16,32},{24,40},{32,48},{40,56},{48,64},{56,72},{64,... | collective-permute-start | bytes 835592 | tf_op jit(solution)/shard_map/ppermute | solution.py:29
  141.4 11.9 %collective-permute-start.2 = (bf16[1,272,512]{2,1,0:T(8,128)(2,1)S(1)}, bf16[1,272,512]{2,1,0:T(8,128)(2,1)S(1)}, u32[]{:S(2)}, u32[]{:S(2)}) collective-permute-start(bf16[1,272,512]{2,1,0:T(8,128)(2,1)S(1)} %pad_maximum_fusion.1), channel_id=1, source_target_pairs={{0,16},{8,24},{16,32},{24,40},{32,48},{40,56},{48,64},{56,72},{64,... | collective-permute-start | bytes 835592 | tf_op jit(solution)/shard_map/ppermute | solution.py:29
  156.7 8.4 %collective-permute-start.3 = (bf16[1,272,512]{2,1,0:T(8,128)(2,1)S(1)}, bf16[1,272,512]{2,1,0:T(8,128)(2,1)S(1)}, u32[]{:S(2)}, u32[]{:S(2)}) collective-permute-start(bf16[1,272,512]{2,1,0:T(8,128)(2,1)S(1)} %pad_maximum_fusion.2), channel_id=1, source_target_pairs={{0,32},{8,40},{16,48},{24,56},{32,64},{40,72},{48,80},{56,88},{64,... | collective-permute-start | bytes 835592 | tf_op jit(solution)/shard_map/ppermute | solution.py:29
  168.5 16.9 %collective-permute-start.4 = (bf16[1,272,512]{2,1,0:T(8,128)(2,1)S(1)}, bf16[1,272,512]{2,1,0:T(8,128)(2,1)S(1)}, u32[]{:S(2)}, u32[]{:S(2)}) collective-permute-start(bf16[1,272,512]{2,1,0:T(8,128)(2,1)S(1)} %pad_maximum_fusion.3), channel_id=1, source_target_pairs={{0,64},{8,72},{16,80},{24,88},{32,96},{40,104},{48,112},{56,120},{... | collective-permute-start | bytes 835592 | tf_op jit(solution)/shard_map/ppermute | solution.py:29
  185.4 9.0 %copy-start.1 = (bf16[1,272,512]{2,1,0:T(8,128)(2,1)}, bf16[1,272,512]{2,1,0:T(8,128)(2,1)S(1)}, u32[]{:S(2)}) copy-start(bf16[1,272,512]{2,1,0:T(8,128)(2,1)S(1)} %collective-permute-done.4) | copy-start | bytes 835588
  189.0 19.0 %collective-permute-start.5 = (bf16[1,272,512]{2,1,0:T(8,128)(2,1)S(1)}, bf16[1,272,512]{2,1,0:T(8,128)(2,1)S(1)}, u32[]{:S(2)}, u32[]{:S(2)}) collective-permute-start(bf16[1,272,512]{2,1,0:T(8,128)(2,1)S(1)} %pad_maximum_fusion.4), channel_id=1, source_target_pairs={{0,128},{8,136},{16,144},{24,152},{32,160},{40,168},{48,176},{56,1... | collective-permute-start | bytes 835592 | tf_op jit(solution)/shard_map/ppermute | solution.py:29
  207.9 0.7 copy-start.2
  212.2 3.6 %copy-start.7 = (f32[512]{0:T(512)S(1)}, f32[512]{0:T(512)}, u32[]{:S(2)}) copy-start(f32[512]{0:T(512)} %param.37) | copy-start | bytes 6148
Sparse Core Ops, SparseCore 0:
  9.9 96.8 all-gather.2
  109.3 106.5 all-gather.4
  223.8 48.8 reduce-scatter.1

commit v4 on v3

--- a/solution.py
+++ b/solution.py
@@ -140,9 +140,12 @@
         incoming[attention_slot_number],
     )
     normed_heads = head_norm(head_out, head_gain)
-    out_columns = lax.all_gather(w_out, "ctx", axis=1, tiled=True)
+    out_rows = lax.all_gather(w_out.T, "ctx", axis=0, tiled=True)
+    projected = lax.dot_general(
+        normed_heads, out_rows, (((1,), (1,)), ((), ())), preferred_element_type=jnp.float32
+    )
     summed = lax.psum_scatter(
-        jnp.dot(normed_heads, out_columns, preferred_element_type=jnp.float32).astype(jnp.bfloat16),
+        projected.astype(jnp.bfloat16),
         "tp",
         scatter_dimension=0,
         tiled=True,

time: 285 us -> 285 us (level)
  no operation moved by 1% of the time
where the time goes in v4:
time: 285 us; the launch traced here: 281 us
  waiting for transfers between devices  192 us (67%)
  matrix products  26.8 us (9%)
  between operations  21.9 us (8%)
  starting transfers between devices  17.9 us (6%)
  local copies, waits for them, and re-layouts  15.7 us (6%)
  other arithmetic  7.54 us (3%)
    all_to_all x1, waiting for transfers between devices, local(): lax.all_to_all(copies, 'tp', 0, 0, tiled=True).reshape(-1, normed.shape[1])  63.8 us
    ppermute x6, waiting for transfers between devices, shifted(): got = lax.ppermute(message, axis, pairs)  57.1 us
    reduce_scatter x1, waiting for transfers between devices, local(): lax.psum_scatter(projected.astype(jnp.bfloat16), 'tp', scatter_dimension=...  49 us
    all_gather x1, waiting for transfers between devices, local(): parameter_collection = lax.all_gather(w_qkv, 'ctx', axis=0, tiled=True)  16.7 us
    ppermute x6, starting transfers between devices, shifted(): got = lax.ppermute(message, axis, pairs)  12.9 us
    dot_general x1, matrix products, local(): jnp.dot(every_row_list, parameter_collection, preferred_element_type=jnp....  10.9 us
    dot_general x1, matrix products, local(): lax.dot_general(normed_heads, out_rows, (((1,), (1,)), ((), ())), preferr...  7.74 us
    scatter x10, local copies, waits for them, and re-layouts, shifted(): extra = extra.at[:, 0, 0].set(high).at[:, 0, 1].set(low)  6.5 us
  transfers between devices with their start and end apart: 10, of which 9 were waited for; matrix products, arithmetic and copies ran while one was open for 14% of the time, Pallas kernels for 0%

profile of v4, /device:TPU:224, one launch (start us, length us, event | category | flops | bytes accessed | tf_op | source)
XLA Modules:
  0.0 281.4 jit_solution(16675667116050032039)
XLA Ops:
  6.5 0.7 all-gather.3.cloned.1.call-update
  7.3 1.4 fusion.1
  8.7 1.0 fusion.3
  9.7 3.3 %broadcast_in_dim.5 = bf16[8,96,4096]{2,1,0:T(8,128)(2,1)} broadcast(bf16[96,4096]{1,0:T(8,128)(2,1)S(1)} %fusion.3), dimensions={1,2} | broadcast | bytes 7077888 | tf_op jit(solution)/shard_map/broadcast_in_dim | solution.py:107
  13.0 4.9 %all-to-all-start = ((bf16[8,96,4096]{2,1,0:T(8,128)(2,1)}), bf16[8,96,4096]{2,1,0:T(8,128)(2,1)}, u32[]{:S(2)}, u32[]{:S(2)}) async-start(bf16[8,96,4096]{2,1,0:T(8,128)(2,1)} %broadcast_in_dim.5), calls=%async_computation | async-start | bytes 12582912 | tf_op jit(solution)/shard_map/all_to_all | solution.py:108
  18.0 0.7 all-gather.5.cloned.1.call-update
  19.4 0.3 reduce-window.24
  19.8 0.3 reduce-window.16
  20.5 0.6 slice.305
  21.8 0.6 slice.306
  23.1 0.6 fusion.51
  23.7 1.3 scatter.35
  25.0 1.3 exponential_select_fusion
  26.3 63.8 %all-to-all-done = bf16[8,96,4096]{2,1,0:T(8,128)(2,1)} async-done(((bf16[8,96,4096]{2,1,0:T(8,128)(2,1)}), bf16[8,96,4096]{2,1,0:T(8,128)(2,1)}, u32[]{:S(2)}, u32[]{:S(2)}) %all-to-all-start) | async-done | bytes 6291488 | tf_op jit(solution)/shard_map/all_to_all | solution.py:108
  90.1 16.7 %all-gather.3.cloned.1.call-done = bf16[4096,1024]{1,0:T(8,128)(2,1)} async-done(((bf16[128,1024]{1,0:T(8,128)(2,1)}), bf16[4096,1024]{1,0:T(8,128)(2,1)}) %all-gather.3.cloned.1.call-update) | async-done | bytes 8388624 | tf_op jit(solution)/shard_map/all_gather | solution.py:109
  106.8 10.9 %convolution_convert_fusion.1 = bf16[768,1024]{1,0:T(8,128)(2,1)S(1)} fusion(bf16[768,4096]{1,0:T(8,128)(2,1)} %bitcast, bf16[4096,1024]{1,0:T(8,128)(2,1)} %all-gather.3.cloned.1.call-done), kind=kOutput, calls=%fused_computation.7 | convolution fusion | flops 6443237376 | bytes 16252928 | tf_op jit(solution)/shard_map/dot_general | solution.py:110
  117.8 0.6 fusion.13
  118.4 2.1 collective-permute-start
  120.5 4.0 %collective-permute-start.1 = (bf16[1,272,512]{2,1,0:T(8,128)(2,1)S(1)}, bf16[1,272,512]{2,1,0:T(8,128)(2,1)S(1)}, u32[]{:S(2)}, u32[]{:S(2)}) collective-permute-start(bf16[1,272,512]{2,1,0:T(8,128)(2,1)S(1)} %pad_maximum_fusion), channel_id=1, source_target_pairs={{0,16},{8,24},{16,32},{24,40},{32,48},{40,56},{48,64},{56,72},{64,... | collective-permute-start | bytes 835592 | tf_op jit(solution)/shard_map/ppermute | solution.py:29
  124.5 11.8 %collective-permute-done = bf16[1,272,512]{2,1,0:T(8,128)(2,1)S(1)} collective-permute-done((bf16[1,272,512]{2,1,0:T(8,128)(2,1)S(1)}, bf16[1,272,512]{2,1,0:T(8,128)(2,1)S(1)}, u32[]{:S(2)}, u32[]{:S(2)}) %collective-permute-start) | collective-permute-done | bytes 278560 | tf_op jit(solution)/shard_map/ppermute | solution.py:29
  136.2 0.6 fusion.50
  138.1 0.6 fusion.49
  140.0 1.3 scatter.39
  141.4 2.7 collective-permute-start.2
  144.2 9.1 %collective-permute-done.2 = bf16[1,272,512]{2,1,0:T(8,128)(2,1)S(1)} collective-permute-done((bf16[1,272,512]{2,1,0:T(8,128)(2,1)S(1)}, bf16[1,272,512]{2,1,0:T(8,128)(2,1)S(1)}, u32[]{:S(2)}, u32[]{:S(2)}) %collective-permute-start.2) | collective-permute-done | bytes 278560 | tf_op jit(solution)/shard_map/ppermute | solution.py:29
  153.3 0.6 fusion.48
  155.2 1.3 scatter.41
  156.5 0.1 fusion.45
  156.7 1.3 collective-permute-start.3
  158.0 7.1 %collective-permute-done.3 = bf16[1,272,512]{2,1,0:T(8,128)(2,1)S(1)} collective-permute-done((bf16[1,272,512]{2,1,0:T(8,128)(2,1)S(1)}, bf16[1,272,512]{2,1,0:T(8,128)(2,1)S(1)}, u32[]{:S(2)}, u32[]{:S(2)}) %collective-permute-start.3) | collective-permute-done | bytes 278560 | tf_op jit(solution)/shard_map/ppermute | solution.py:29
  165.1 0.6 fusion.47
  167.0 1.3 scatter.45
  168.3 0.2 fusion.34
  168.5 1.3 collective-permute-start.4
  169.8 15.6 %collective-permute-done.4 = bf16[1,272,512]{2,1,0:T(8,128)(2,1)S(1)} collective-permute-done((bf16[1,272,512]{2,1,0:T(8,128)(2,1)S(1)}, bf16[1,272,512]{2,1,0:T(8,128)(2,1)S(1)}, u32[]{:S(2)}, u32[]{:S(2)}) %collective-permute-start.4) | collective-permute-done | bytes 278560 | tf_op jit(solution)/shard_map/ppermute | solution.py:29
  185.4 0.6 fusion.46
  187.4 1.3 scatter.49
  188.7 0.2 fusion.37
  189.0 1.5 collective-permute-start.5
  190.4 4.0 %fusion.5 = f32[768,512]{0,1:T(8,128)} fusion(f32[768]{0:T(1024)S(1)} %multiply_reduce_fusion.1, f32[768]{0:T(1024)S(1)} %get-tuple-element.143, s32[768]{0:T(1024)S(1)} %get-tuple-element.142, bf16[768,1024]{1,0:T(8,128)(2,1)} %copy-done.3), kind=kOutput, calls=%fused_computation.15 | convolution fusion | flops 911867904 | bytes 3166208 | tf_op jit(solution)/shard_map/dot_general | solution.py:67
  194.4 13.5 %collective-permute-done.5 = bf16[1,272,512]{2,1,0:T(8,128)(2,1)S(1)} collective-permute-done((bf16[1,272,512]{2,1,0:T(8,128)(2,1)S(1)}, bf16[1,272,512]{2,1,0:T(8,128)(2,1)S(1)}, u32[]{:S(2)}, u32[]{:S(2)}) %collective-permute-start.5) | collective-permute-done | bytes 278560 | tf_op jit(solution)/shard_map/ppermute | solution.py:29
  207.9 0.7 copy-done.2
  208.6 3.6 %fusion.52 = (f32[768]{0:T(1024)S(1)}, f32[768,512]{0,1:T(8,128)S(1)}) fusion(f32[768,512]{0,1:T(8,128)} %fusion.5, bf16[1,272,512]{2,1,0:T(8,128)(2,1)} %copy-done.2, f32[]{:T(128)} %bitcast.26, bf16[1,272,512]{2,1,0:T(8,128)(2,1)S(1)} %collective-permute-done.3, f32[]{:T(128)} %bitcast.22, bf16[1,272,512]{2,1,0:T(8,128)(2,1)} %copy-done.1, f32[]{:T(128)} %bitcast.27, ...), kind=kOutput, calls=%fused_computation.85 | convolution fusion | flops 1211235584 | bytes 5121536 | tf_op jit(solution)/shard_map/dot_general | solution.py:82
  212.3 0.2 multiply_reduce_fusion
  212.5 3.4 %all-gather.5.cloned.1.call-done = bf16[4096,512]{0,1:T(8,128)(2,1)} async-done(((bf16[128,512]{0,1:T(8,128)(2,1)}), bf16[4096,512]{0,1:T(8,128)(2,1)}) %all-gather.5.cloned.1.call-update) | async-done | bytes 4194320 | tf_op jit(solution)/shard_map/all_gather | solution.py:143
  215.9 7.7 %convolution_convert_fusion = bf16[768,4096]{1,0:T(8,128)(2,1)} fusion(bf16[4096,512]{0,1:T(8,128)(2,1)} %all-gather.5.cloned.1.call-done, f32[768,512]{0,1:T(8,128)S(1)} %get-tuple-element.157, f32[512]{0:T(512)S(1)} %copy-done.7, f32[768]{0:T(1024)S(1)} %add_rsqrt_fusion, f32[768]{0:T(1024)S(1)} %broadcast_multiply_fusion), kind=kOutput, calls=%fused_computation | convolution fusion | flops 3225944064 | bytes 12066816 | tf_op jit(solution)/shard_map/dot_general | solution.py:144
  223.6 49.0 %reduce-scatter.2.cloned.1.call-done = bf16[96,4096]{1,0:T(8,128)(2,1)} async-done(((bf16[768,4096]{1,0:T(8,128)(2,1)}), bf16[96,4096]{1,0:T(8,128)(2,1)}) %reduce-scatter.2.cloned.1.call-update) | async-done | bytes 786448 | tf_op jit(solution)/shard_map/reduce_scatter | solution.py:147
  272.7 2.2 fusion.4
  (45 shorter events, 0.9 us)
Async XLA Ops:
  6.5 2.1 copy-start
  6.5 100.3 %all-gather.3.cloned.1.call-start = ((), (), s32[]{:S(2)}) async-start(), calls=%async_computation.2 | async-start | bytes 8650752 | tf_op jit(solution)/shard_map/all_gather | solution.py:109
  13.0 6.4 %copy-start.6 = (s32[1,768]{1,0:T(1,128)S(1)}, s32[1,768]{1,0:T(1,128)}, u32[]{:S(2)}) copy-start(s32[1,768]{1,0:T(1,128)} %param.39) | copy-start | bytes 9220
  13.0 6.8 %copy-start.4 = (s32[768]{0:T(1024)S(1)}, s32[768]{0:T(1024)}, u32[]{:S(2)}) copy-start(s32[768]{0:T(1024)} %param.41) | copy-start | bytes 9220
  13.0 12.0 %copy-start.5 = (s32[1,768]{1,0:T(1,128)S(1)}, s32[1,768]{1,0:T(1,128)}, u32[]{:S(2)}) copy-start(s32[1,768]{1,0:T(1,128)} %param.38) | copy-start | bytes 9220
  13.0 77.1 %all-to-all-start = ((bf16[8,96,4096]{2,1,0:T(8,128)(2,1)}), bf16[8,96,4096]{2,1,0:T(8,128)(2,1)}, u32[]{:S(2)}, u32[]{:S(2)}) async-start(bf16[8,96,4096]{2,1,0:T(8,128)(2,1)} %broadcast_in_dim.5), calls=%async_computation | async-start | bytes 12582912 | tf_op jit(solution)/shard_map/all_to_all | solution.py:108
  17.9 197.9 %all-gather.5.cloned.1.call-start = ((), (), s32[]{:S(2)}) async-start(), calls=%async_computation.3 | async-start | bytes 4325376 | tf_op jit(solution)/shard_map/all_gather | solution.py:143
  18.7 254.0 %reduce-scatter.2.cloned.1.call-start = ((), (), s32[]{:S(2)}) async-start(), calls=%async_computation.4 | async-start | bytes 7077888 | tf_op jit(solution)/shard_map/reduce_scatter | solution.py:147
  117.8 20.4 %copy-start.3 = (bf16[768,1024]{1,0:T(8,128)(2,1)}, bf16[768,1024]{1,0:T(8,128)(2,1)S(1)}, u32[]{:S(2)}) copy-start(bf16[768,1024]{1,0:T(8,128)(2,1)S(1)} %convolution_convert_fusion.1) | copy-start | bytes 4718596
  118.4 17.9 %collective-permute-start = (bf16[1,272,512]{2,1,0:T(8,128)(2,1)S(1)}, bf16[1,272,512]{2,1,0:T(8,128)(2,1)S(1)}, u32[]{:S(2)}, u32[]{:S(2)}) collective-permute-start(bf16[1,272,512]{2,1,0:T(8,128)(2,1)S(1)} %pad_maximum_fusion), channel_id=1, source_target_pairs={{0,8},{8,16},{16,24},{24,32},{32,40},{40,48},{48,56},{56,64},{64,7... | collective-permute-start | bytes 835592 | tf_op jit(solution)/shard_map/ppermute | solution.py:29
  120.5 17.6 %collective-permute-start.1 = (bf16[1,272,512]{2,1,0:T(8,128)(2,1)S(1)}, bf16[1,272,512]{2,1,0:T(8,128)(2,1)S(1)}, u32[]{:S(2)}, u32[]{:S(2)}) collective-permute-start(bf16[1,272,512]{2,1,0:T(8,128)(2,1)S(1)} %pad_maximum_fusion), channel_id=1, source_target_pairs={{0,16},{8,24},{16,32},{24,40},{32,48},{40,56},{48,64},{56,72},{64,... | collective-permute-start | bytes 835592 | tf_op jit(solution)/shard_map/ppermute | solution.py:29
  141.4 11.9 %collective-permute-start.2 = (bf16[1,272,512]{2,1,0:T(8,128)(2,1)S(1)}, bf16[1,272,512]{2,1,0:T(8,128)(2,1)S(1)}, u32[]{:S(2)}, u32[]{:S(2)}) collective-permute-start(bf16[1,272,512]{2,1,0:T(8,128)(2,1)S(1)} %pad_maximum_fusion.1), channel_id=1, source_target_pairs={{0,16},{8,24},{16,32},{24,40},{32,48},{40,56},{48,64},{56,72},{64,... | collective-permute-start | bytes 835592 | tf_op jit(solution)/shard_map/ppermute | solution.py:29
  156.7 8.4 %collective-permute-start.3 = (bf16[1,272,512]{2,1,0:T(8,128)(2,1)S(1)}, bf16[1,272,512]{2,1,0:T(8,128)(2,1)S(1)}, u32[]{:S(2)}, u32[]{:S(2)}) collective-permute-start(bf16[1,272,512]{2,1,0:T(8,128)(2,1)S(1)} %pad_maximum_fusion.2), channel_id=1, source_target_pairs={{0,32},{8,40},{16,48},{24,56},{32,64},{40,72},{48,80},{56,88},{64,... | collective-permute-start | bytes 835592 | tf_op jit(solution)/shard_map/ppermute | solution.py:29
  168.5 16.9 %collective-permute-start.4 = (bf16[1,272,512]{2,1,0:T(8,128)(2,1)S(1)}, bf16[1,272,512]{2,1,0:T(8,128)(2,1)S(1)}, u32[]{:S(2)}, u32[]{:S(2)}) collective-permute-start(bf16[1,272,512]{2,1,0:T(8,128)(2,1)S(1)} %pad_maximum_fusion.3), channel_id=1, source_target_pairs={{0,64},{8,72},{16,80},{24,88},{32,96},{40,104},{48,112},{56,120},{... | collective-permute-start | bytes 835592 | tf_op jit(solution)/shard_map/ppermute | solution.py:29
  185.4 9.0 %copy-start.1 = (bf16[1,272,512]{2,1,0:T(8,128)(2,1)}, bf16[1,272,512]{2,1,0:T(8,128)(2,1)S(1)}, u32[]{:S(2)}) copy-start(bf16[1,272,512]{2,1,0:T(8,128)(2,1)S(1)} %collective-permute-done.4) | copy-start | bytes 835588
  189.0 19.0 %collective-permute-start.5 = (bf16[1,272,512]{2,1,0:T(8,128)(2,1)S(1)}, bf16[1,272,512]{2,1,0:T(8,128)(2,1)S(1)}, u32[]{:S(2)}, u32[]{:S(2)}) collective-permute-start(bf16[1,272,512]{2,1,0:T(8,128)(2,1)S(1)} %pad_maximum_fusion.4), channel_id=1, source_target_pairs={{0,128},{8,136},{16,144},{24,152},{32,160},{40,168},{48,176},{56,1... | collective-permute-start | bytes 835592 | tf_op jit(solution)/shard_map/ppermute | solution.py:29
  207.9 0.7 copy-start.2
  212.2 3.6 %copy-start.7 = (f32[512]{0:T(512)S(1)}, f32[512]{0:T(512)}, u32[]{:S(2)}) copy-start(f32[512]{0:T(512)} %param.37) | copy-start | bytes 6148
Sparse Core Ops, SparseCore 0:
  9.9 96.8 all-gather.2
  109.3 106.5 all-gather.4
  223.8 48.8 reduce-scatter.1

commit v5 on v4

--- a/solution.py
+++ b/solution.py
@@ -140,7 +140,9 @@
         incoming[attention_slot_number],
     )
     normed_heads = head_norm(head_out, head_gain)
-    out_rows = lax.all_gather(w_out.T, "ctx", axis=0, tiled=True)
+    blocks = lax.axis_size("ctx")
+    out_copies = jnp.broadcast_to(w_out.T[None], (blocks,) + w_out.T.shape)
+    out_rows = lax.all_to_all(out_copies, "ctx", 0, 0, tiled=True).reshape(-1, w_out.shape[0])
     projected = lax.dot_general(
         normed_heads, out_rows, (((1,), (1,)), ((), ())), preferred_element_type=jnp.float32
     )

time: 285 us -> 353 us (1.24)
  waiting for transfers between devices: 192 us -> 249 us
  starting transfers between devices: 17.9 us -> 24.2 us
    ppermute x6, waiting for transfers between devices: 57.1 us -> 119 us  [shifted(): got = lax.ppermute(message, axis, pairs)]
    all_gather x1, waiting for transfers between devices: 16.7 us -> 3.62 us  [local(): parameter_collection = lax.all_gather(w_qkv, 'ctx', axis=0, tiled=True)]
    all_to_all x0 -> x1, starting transfers between devices: none -> 8.89 us  [local(): lax.all_to_all(out_copies, 'ctx', 0, 0, tiled=True)]
    all_to_all x1, waiting for transfers between devices: 63.8 us -> 72 us  [local(): lax.all_to_all(copies, 'tp', 0, 0, tiled=True).reshape(-1, normed.shape[1])]
    reduce_scatter x1, waiting for transfers between devices: 49 us -> 53.3 us  [local(): lax.psum_scatter(projected.astype(jnp.bfloat16), 'tp', scatter_dimension=...]
  transfers between devices with their start and end apart: 10 -> 10, of which waited for: 9 -> 8; matrix products, arithmetic and copies ran while one was open for 14% -> 12% of each run, Pallas kernels for 0% -> 0%
where the time goes in v5:
time: 353 us; the launch traced here: 349 us
  waiting for transfers between devices  249 us (71%)
  matrix products  26.9 us (8%)
  starting transfers between devices  24.2 us (7%)
  between operations  22.3 us (6%)
  local copies, waits for them, and re-layouts  18.9 us (5%)
  other arithmetic  7.54 us (2%)
    ppermute x6, waiting for transfers between devices, shifted(): got = lax.ppermute(message, axis, pairs)  119 us
    all_to_all x1, waiting for transfers between devices, local(): lax.all_to_all(copies, 'tp', 0, 0, tiled=True).reshape(-1, normed.shape[1])  72 us
    reduce_scatter x1, waiting for transfers between devices, local(): lax.psum_scatter(projected.astype(jnp.bfloat16), 'tp', scatter_dimension=...  53.3 us
    dot_general x1, matrix products, local(): jnp.dot(every_row_list, parameter_collection, preferred_element_type=jnp....  10.9 us
    ppermute x6, starting transfers between devices, shifted(): got = lax.ppermute(message, axis, pairs)  10.4 us
    all_to_all x1, starting transfers between devices, local(): lax.all_to_all(out_copies, 'ctx', 0, 0, tiled=True)  8.89 us
    dot_general x1, matrix products, local(): lax.dot_general(normed_heads, out_rows, (((1,), (1,)), ((), ())), preferr...  7.91 us
  transfers between devices with their start and end apart: 10, of which 8 were waited for; matrix products, arithmetic and copies ran while one was open for 12% of the time, Pallas kernels for 0%

profile of v5, /device:TPU:224, one launch (start us, length us, event | category | flops | bytes accessed | tf_op | source)
XLA Modules:
  0.0 348.9 jit_solution(16439991329450018250)
XLA Ops:
  6.5 0.7 all-gather.2.cloned.1.call-update
  7.3 1.4 fusion.1
  8.7 1.0 fusion.3
  9.7 3.3 broadcast_in_dim.7
  13.0 4.9 %all-to-all-start = ((bf16[8,96,4096]{2,1,0:T(8,128)(2,1)}), bf16[8,96,4096]{2,1,0:T(8,128)(2,1)}, u32[]{:S(2)}, u32[]{:S(2)}) async-start(bf16[8,96,4096]{2,1,0:T(8,128)(2,1)} %broadcast_in_dim.7), calls=%async_computation | async-start | bytes 12582912 | tf_op jit(solution)/shard_map/all_to_all | solution.py:108
  18.1 72.0 %all-to-all-done = bf16[8,96,4096]{2,1,0:T(8,128)(2,1)} async-done(((bf16[8,96,4096]{2,1,0:T(8,128)(2,1)}), bf16[8,96,4096]{2,1,0:T(8,128)(2,1)}, u32[]{:S(2)}, u32[]{:S(2)}) %all-to-all-start) | async-done | bytes 6291488 | tf_op jit(solution)/shard_map/all_to_all | solution.py:108
  90.1 2.5 broadcast_in_dim.8
  92.6 8.9 %all-to-all-start.1 = ((bf16[32,128,512]{2,1,0:T(8,128)(2,1)}), bf16[32,128,512]{2,1,0:T(8,128)(2,1)}, u32[]{:S(2)}, u32[]{:S(2)}) async-start(bf16[32,128,512]{2,1,0:T(8,128)(2,1)} %broadcast_in_dim.8), calls=%async_computation.1 | async-start | bytes 8388608 | tf_op jit(solution)/shard_map/all_to_all | solution.py:145
  102.2 0.3 reduce-window.24
  102.6 0.3 reduce-window.16
  103.3 0.6 slice.305
  104.6 0.6 slice.306
  105.9 0.6 fusion.51
  106.5 1.3 scatter.35
  107.9 1.3 exponential_select_fusion
  109.2 3.6 %all-gather.2.cloned.1.call-done = bf16[4096,1024]{1,0:T(8,128)(2,1)} async-done(((bf16[128,1024]{1,0:T(8,128)(2,1)}), bf16[4096,1024]{1,0:T(8,128)(2,1)}) %all-gather.2.cloned.1.call-update) | async-done | bytes 8388624 | tf_op jit(solution)/shard_map/all_gather | solution.py:109
  112.8 10.9 %convolution_convert_fusion.1 = bf16[768,1024]{1,0:T(8,128)(2,1)S(1)} fusion(bf16[768,4096]{1,0:T(8,128)(2,1)} %bitcast, bf16[4096,1024]{1,0:T(8,128)(2,1)} %all-gather.2.cloned.1.call-done), kind=kOutput, calls=%fused_computation.7 | convolution fusion | flops 6443237376 | bytes 16252928 | tf_op jit(solution)/shard_map/dot_general | solution.py:110
  123.7 0.6 fusion.13
  124.3 1.9 collective-permute-start
  126.2 2.5 collective-permute-start.1
  128.7 79.8 %collective-permute-done = bf16[1,272,512]{2,1,0:T(8,128)(2,1)S(1)} collective-permute-done((bf16[1,272,512]{2,1,0:T(8,128)(2,1)S(1)}, bf16[1,272,512]{2,1,0:T(8,128)(2,1)S(1)}, u32[]{:S(2)}, u32[]{:S(2)}) %collective-permute-start) | collective-permute-done | bytes 278560 | tf_op jit(solution)/shard_map/ppermute | solution.py:29
  208.5 0.6 fusion.50
  210.4 0.6 fusion.49
  212.3 1.3 scatter.39
  213.7 1.9 collective-permute-start.2
  215.6 10.2 %collective-permute-done.2 = bf16[1,272,512]{2,1,0:T(8,128)(2,1)S(1)} collective-permute-done((bf16[1,272,512]{2,1,0:T(8,128)(2,1)S(1)}, bf16[1,272,512]{2,1,0:T(8,128)(2,1)S(1)}, u32[]{:S(2)}, u32[]{:S(2)}) %collective-permute-start.2) | collective-permute-done | bytes 278560 | tf_op jit(solution)/shard_map/ppermute | solution.py:29
  225.9 0.6 fusion.48
  227.8 1.3 scatter.41
  229.3 1.3 collective-permute-start.3
  230.6 7.5 %collective-permute-done.3 = bf16[1,272,512]{2,1,0:T(8,128)(2,1)S(1)} collective-permute-done((bf16[1,272,512]{2,1,0:T(8,128)(2,1)S(1)}, bf16[1,272,512]{2,1,0:T(8,128)(2,1)S(1)}, u32[]{:S(2)}, u32[]{:S(2)}) %collective-permute-start.3) | collective-permute-done | bytes 278560 | tf_op jit(solution)/shard_map/ppermute | solution.py:29
  238.1 0.6 fusion.47
  240.0 1.3 scatter.45
  241.3 0.2 fusion.34
  241.6 1.3 collective-permute-start.4
  242.9 13.5 %collective-permute-done.4 = bf16[1,272,512]{2,1,0:T(8,128)(2,1)S(1)} collective-permute-done((bf16[1,272,512]{2,1,0:T(8,128)(2,1)S(1)}, bf16[1,272,512]{2,1,0:T(8,128)(2,1)S(1)}, u32[]{:S(2)}, u32[]{:S(2)}) %collective-permute-start.4) | collective-permute-done | bytes 278560 | tf_op jit(solution)/shard_map/ppermute | solution.py:29
  256.3 0.6 fusion.46
  258.3 1.3 scatter.49
  259.6 0.2 fusion.37
  259.9 1.5 collective-permute-start.5
  261.4 3.9 %fusion.5 = f32[768,512]{0,1:T(8,128)} fusion(f32[768]{0:T(1024)S(1)} %multiply_reduce_fusion.1, f32[768]{0:T(1024)S(1)} %get-tuple-element.143, s32[768]{0:T(1024)S(1)} %get-tuple-element.142, bf16[768,1024]{1,0:T(8,128)(2,1)} %copy-done.4), kind=kOutput, calls=%fused_computation.15 | convolution fusion | flops 911867904 | bytes 3166208 | tf_op jit(solution)/shard_map/dot_general | solution.py:67
  265.3 8.4 %collective-permute-done.5 = bf16[1,272,512]{2,1,0:T(8,128)(2,1)S(1)} collective-permute-done((bf16[1,272,512]{2,1,0:T(8,128)(2,1)S(1)}, bf16[1,272,512]{2,1,0:T(8,128)(2,1)S(1)}, u32[]{:S(2)}, u32[]{:S(2)}) %collective-permute-start.5) | collective-permute-done | bytes 278560 | tf_op jit(solution)/shard_map/ppermute | solution.py:29
  273.7 0.7 copy-done.2
  274.4 3.6 %fusion.52 = (f32[768]{0:T(1024)S(1)}, f32[768,512]{0,1:T(8,128)S(1)}) fusion(f32[768,512]{0,1:T(8,128)} %fusion.5, bf16[1,272,512]{2,1,0:T(8,128)(2,1)} %copy-done.2, f32[]{:T(128)} %bitcast.26, bf16[1,272,512]{2,1,0:T(8,128)(2,1)S(1)} %collective-permute-done.3, f32[]{:T(128)} %bitcast.22, bf16[1,272,512]{2,1,0:T(8,128)(2,1)} %copy-done.1, f32[]{:T(128)} %bitcast.27, ...), kind=kOutput, calls=%fused_computation.85 | convolution fusion | flops 1211235584 | bytes 5121536 | tf_op jit(solution)/shard_map/dot_general | solution.py:82
  278.0 0.2 multiply_reduce_fusion
  278.2 0.4 copy-done.8
  278.7 7.9 %convolution_convert_fusion = bf16[768,4096]{1,0:T(8,128)(2,1)} fusion(bf16[4096,512]{1,0:T(8,128)(2,1)} %bitcast.32, f32[768,512]{0,1:T(8,128)S(1)} %get-tuple-element.157, f32[512]{0:T(512)S(1)} %copy-done.8, f32[768]{0:T(1024)S(1)} %add_rsqrt_fusion, f32[768]{0:T(1024)S(1)} %broadcast_multiply_fusion), kind=kOutput, calls=%fused_computation | convolution fusion | flops 3225944064 | bytes 12066816 | tf_op jit(solution)/shard_map/dot_general | solution.py:146
  286.6 53.3 %reduce-scatter.2.cloned.1.call-done = bf16[96,4096]{1,0:T(8,128)(2,1)} async-done(((bf16[768,4096]{1,0:T(8,128)(2,1)}), bf16[96,4096]{1,0:T(8,128)(2,1)}) %reduce-scatter.2.cloned.1.call-update) | async-done | bytes 786448 | tf_op jit(solution)/shard_map/reduce_scatter | solution.py:149
  339.9 2.2 fusion.4
  (48 shorter events, 1.1 us)
Async XLA Ops:
  6.5 2.1 copy-start
  6.5 106.2 %all-gather.2.cloned.1.call-start = ((), (), s32[]{:S(2)}) async-start(), calls=%async_computation.3 | async-start | bytes 8650752 | tf_op jit(solution)/shard_map/all_gather | solution.py:109
  13.0 4.9 %copy-start.3 = (bf16[512,128]{1,0:T(8,128)(2,1)S(1)}, bf16[512,128]{1,0:T(8,128)(2,1)}, u32[]{:S(2)}) copy-start(bf16[512,128]{1,0:T(8,128)(2,1)} %param.36) | copy-start | bytes 393220
  13.0 77.1 %all-to-all-start = ((bf16[8,96,4096]{2,1,0:T(8,128)(2,1)}), bf16[8,96,4096]{2,1,0:T(8,128)(2,1)}, u32[]{:S(2)}, u32[]{:S(2)}) async-start(bf16[8,96,4096]{2,1,0:T(8,128)(2,1)} %broadcast_in_dim.7), calls=%async_computation | async-start | bytes 12582912 | tf_op jit(solution)/shard_map/all_to_all | solution.py:108
  92.6 9.6 %copy-start.7 = (s32[1,768]{1,0:T(1,128)S(1)}, s32[1,768]{1,0:T(1,128)}, u32[]{:S(2)}) copy-start(s32[1,768]{1,0:T(1,128)} %param.39) | copy-start | bytes 9220
  92.6 10.0 %copy-start.5 = (s32[768]{0:T(1024)S(1)}, s32[768]{0:T(1024)}, u32[]{:S(2)}) copy-start(s32[768]{0:T(1024)} %param.41) | copy-start | bytes 9220
  92.6 15.2 %copy-start.6 = (s32[1,768]{1,0:T(1,128)S(1)}, s32[1,768]{1,0:T(1,128)}, u32[]{:S(2)}) copy-start(s32[1,768]{1,0:T(1,128)} %param.38) | copy-start | bytes 9220
  92.6 185.6 %all-to-all-start.1 = ((bf16[32,128,512]{2,1,0:T(8,128)(2,1)}), bf16[32,128,512]{2,1,0:T(8,128)(2,1)}, u32[]{:S(2)}, u32[]{:S(2)}) async-start(bf16[32,128,512]{2,1,0:T(8,128)(2,1)} %broadcast_in_dim.8), calls=%async_computation.1 | async-start | bytes 8388608 | tf_op jit(solution)/shard_map/all_to_all | solution.py:145
  101.5 238.4 %reduce-scatter.2.cloned.1.call-start = ((), (), s32[]{:S(2)}) async-start(), calls=%async_computation.4 | async-start | bytes 7077888 | tf_op jit(solution)/shard_map/reduce_scatter | solution.py:149
  123.7 86.7 %copy-start.4 = (bf16[768,1024]{1,0:T(8,128)(2,1)}, bf16[768,1024]{1,0:T(8,128)(2,1)S(1)}, u32[]{:S(2)}) copy-start(bf16[768,1024]{1,0:T(8,128)(2,1)S(1)} %convolution_convert_fusion.1) | copy-start | bytes 4718596
  124.3 84.2 %collective-permute-start = (bf16[1,272,512]{2,1,0:T(8,128)(2,1)S(1)}, bf16[1,272,512]{2,1,0:T(8,128)(2,1)S(1)}, u32[]{:S(2)}, u32[]{:S(2)}) collective-permute-start(bf16[1,272,512]{2,1,0:T(8,128)(2,1)S(1)} %pad_maximum_fusion), channel_id=1, source_target_pairs={{0,8},{8,16},{16,24},{24,32},{32,40},{40,48},{48,56},{56,64},{64,7... | collective-permute-start | bytes 835592 | tf_op jit(solution)/shard_map/ppermute | solution.py:29
  126.2 84.1 %collective-permute-start.1 = (bf16[1,272,512]{2,1,0:T(8,128)(2,1)S(1)}, bf16[1,272,512]{2,1,0:T(8,128)(2,1)S(1)}, u32[]{:S(2)}, u32[]{:S(2)}) collective-permute-start(bf16[1,272,512]{2,1,0:T(8,128)(2,1)S(1)} %pad_maximum_fusion), channel_id=1, source_target_pairs={{0,16},{8,24},{16,32},{24,40},{32,48},{40,56},{48,64},{56,72},{64,... | collective-permute-start | bytes 835592 | tf_op jit(solution)/shard_map/ppermute | solution.py:29
  213.7 12.2 %collective-permute-start.2 = (bf16[1,272,512]{2,1,0:T(8,128)(2,1)S(1)}, bf16[1,272,512]{2,1,0:T(8,128)(2,1)S(1)}, u32[]{:S(2)}, u32[]{:S(2)}) collective-permute-start(bf16[1,272,512]{2,1,0:T(8,128)(2,1)S(1)} %pad_maximum_fusion.1), channel_id=1, source_target_pairs={{0,16},{8,24},{16,32},{24,40},{32,48},{40,56},{48,64},{56,72},{64,... | collective-permute-start | bytes 835592 | tf_op jit(solution)/shard_map/ppermute | solution.py:29
  229.3 8.8 %collective-permute-start.3 = (bf16[1,272,512]{2,1,0:T(8,128)(2,1)S(1)}, bf16[1,272,512]{2,1,0:T(8,128)(2,1)S(1)}, u32[]{:S(2)}, u32[]{:S(2)}) collective-permute-start(bf16[1,272,512]{2,1,0:T(8,128)(2,1)S(1)} %pad_maximum_fusion.2), channel_id=1, source_target_pairs={{0,32},{8,40},{16,48},{24,56},{32,64},{40,72},{48,80},{56,88},{64,... | collective-permute-start | bytes 835592 | tf_op jit(solution)/shard_map/ppermute | solution.py:29
  241.6 14.8 %collective-permute-start.4 = (bf16[1,272,512]{2,1,0:T(8,128)(2,1)S(1)}, bf16[1,272,512]{2,1,0:T(8,128)(2,1)S(1)}, u32[]{:S(2)}, u32[]{:S(2)}) collective-permute-start(bf16[1,272,512]{2,1,0:T(8,128)(2,1)S(1)} %pad_maximum_fusion.3), channel_id=1, source_target_pairs={{0,64},{8,72},{16,80},{24,88},{32,96},{40,104},{48,112},{56,120},{... | collective-permute-start | bytes 835592 | tf_op jit(solution)/shard_map/ppermute | solution.py:29
  256.3 9.0 %copy-start.1 = (bf16[1,272,512]{2,1,0:T(8,128)(2,1)}, bf16[1,272,512]{2,1,0:T(8,128)(2,1)S(1)}, u32[]{:S(2)}) copy-start(bf16[1,272,512]{2,1,0:T(8,128)(2,1)S(1)} %collective-permute-done.4) | copy-start | bytes 835588
  259.9 13.8 %collective-permute-start.5 = (bf16[1,272,512]{2,1,0:T(8,128)(2,1)S(1)}, bf16[1,272,512]{2,1,0:T(8,128)(2,1)S(1)}, u32[]{:S(2)}, u32[]{:S(2)}) collective-permute-start(bf16[1,272,512]{2,1,0:T(8,128)(2,1)S(1)} %pad_maximum_fusion.4), channel_id=1, source_target_pairs={{0,128},{8,136},{16,144},{24,152},{32,160},{40,168},{48,176},{56,1... | collective-permute-start | bytes 835592 | tf_op jit(solution)/shard_map/ppermute | solution.py:29
  273.7 0.7 copy-start.2
  278.0 0.7 copy-start.8
Sparse Core Ops, SparseCore 0:
  9.9 102.7 all-gather.1
  286.7 53.1 reduce-scatter.1

commit v6 on v4

--- a/solution.py
+++ b/solution.py
@@ -1,6 +1,10 @@
+import functools
+
 import jax
 import jax.numpy as jnp
 from jax import lax
+from jax.experimental import pallas as pl
+from jax.experimental.pallas import tpu as pltpu
 from jax.sharding import PartitionSpec as P
 
 DK = 256
@@ -10,38 +14,109 @@
 EPSILON = 1e-06
 FORGET_STEP = 0.5
 INPUT_STEP = 0.5
+
+
+MESH_ID = pl.DeviceIdType.MESH
+DECAY_ROWS = 16
+
+
+def scan_shifts(count):
+    shifts = [1] + ([2] if count > 2 else [])
+    k = 2
+    while k < count:
+        shifts.append(k)
+        k *= 2
+    return shifts
+
+
+def scan_kernel(count, shifts, state_ref, decay_ref, out_ref, send_buf, recv_buf, acc_total, acc_decay, send_sems, recv_sems):
+    me = lax.axis_index("ctx")
+    tp = lax.axis_index("tp")
+    rows = state_ref.shape[0]
+
+    barrier = pltpu.get_barrier_semaphore()
+    partners = sorted(set(shifts))
+    for s in partners:
+        for peer in (lax.rem(me + s, count), lax.rem(me + count - s, count)):
+            pl.semaphore_signal(barrier, 1, device_id=(peer, tp), device_id_type=MESH_ID)
+    pl.semaphore_wait(barrier, 2 * len(partners))
+
+    def pack(slot, total, decay):
+        high = decay.astype(jnp.bfloat16)
+        send_buf[slot, :rows, :] = total.astype(jnp.bfloat16)
+        send_buf[slot, rows : rows + DECAY_ROWS, :] = high
+        send_buf[slot, rows + DECAY_ROWS :, :] = (decay - high.astype(jnp.float32)).astype(jnp.bfloat16)
+
+    def copy(j, source_slot, peer):
+        return pltpu.make_async_remote_copy(
+            src_ref=send_buf.at[source_slot],
+            dst_ref=recv_buf.at[j],
+            send_sem=send_sems.at[j],
+            recv_sem=recv_sems.at[j],
+            device_id=(peer, tp),
+            device_id_type=MESH_ID,
+        )
+
+    def send(j, source_slot):
+        @pl.when(me + shifts[j] < count)
+        def _():
+            copy(j, source_slot, me + shifts[j]).start()
+
+    def absorb(j, source_slot):
+        @pl.when(me - shifts[j] >= 0)
+        def _():
+            copy(j, source_slot, me - shifts[j]).wait_recv()
+            got = recv_buf[j]
+            far_total = got[:rows].astype(jnp.float32)
+            far_decay = got[rows : rows + DECAY_ROWS].astype(jnp.float32) + got[
+                rows + DECAY_ROWS :
+            ].astype(jnp.float32)
+            decay = acc_decay[...]
+            acc_total[...] = decay[0:1, :] * far_total + acc_total[...]
+            acc_decay[...] = decay * far_decay
+
+    acc_total[...] = jnp.zeros_like(acc_total)
+    acc_decay[...] = jnp.ones_like(acc_decay)
+    pack(0, state_ref[...], decay_ref[...])
+    first = min(2, len(shifts))
+    for j in range(first):
+        send(j, 0)
+    for j in range(first):
+        absorb(j, 0)
+    for j in range(first, len(shifts)):
+        pack(j - 1, acc_total[...], acc_decay[...])
+        send(j, j - 1)
+        absorb(j, j - 1)
+    out_ref[...] = acc_total[...]
+    for j in range(len(shifts)):
+        @pl.when(me + shifts[j] < count)
+        def _():
+            copy(j, 0 if j < first else j - 1, me + shifts[j]).wait_send()
 
 
 def carried_in(passing, state, axis):
     count = lax.axis_size(axis)
     if count == 1:
         return jnp.zeros_like(state)
-    heads, rows, width = state.shape
-    pad = 16
-
-    def shifted(decay, total, k):
-        high = decay.astype(jnp.bfloat16)
-        low = (decay - high.astype(jnp.float32)).astype(jnp.bfloat16)
-        extra = jnp.zeros((heads, pad, width), jnp.bfloat16)
-        extra = extra.at[:, 0, 0].set(high).at[:, 0, 1].set(low)
-        message = jnp.concatenate([total.astype(jnp.bfloat16), extra], axis=1)
-        pairs = [(i, i + k) for i in range(count - k)]
-        got = lax.ppermute(message, axis, pairs)
-        got_decay = got[:, rows, 0].astype(jnp.float32) + got[:, rows, 1].astype(jnp.float32)
-        return got_decay, got[:, :rows].astype(jnp.float32)
-
-    decay, total = shifted(passing, state, 1)
-    if count > 2:
-        decay_far, total_far = shifted(passing, state, 2)
-        total = decay[:, None, None] * total_far + total
-        decay = decay * decay_far
-    k = 2
-    while k < count:
-        decay_far, total_far = shifted(decay, total, k)
-        total = decay[:, None, None] * total_far + total
-        decay = decay * decay_far
-        k *= 2
-    return total
+    shifts = scan_shifts(count)
+    rows, width = state.shape
+    decay = jnp.broadcast_to(passing.reshape(1, 1), (DECAY_ROWS, width)).astype(jnp.float32)
+    message = (len(shifts), rows + 2 * DECAY_ROWS, width)
+    return pl.pallas_call(
+        functools.partial(scan_kernel, count, shifts),
+        out_shape=jax.ShapeDtypeStruct((rows, width), jnp.float32),
+        in_specs=[pl.BlockSpec(memory_space=pltpu.VMEM)] * 2,
+        out_specs=pl.BlockSpec(memory_space=pltpu.VMEM),
+        scratch_shapes=[
+            pltpu.VMEM(message, jnp.bfloat16),
+            pltpu.VMEM(message, jnp.bfloat16),
+            pltpu.VMEM((rows, width), jnp.float32),
+            pltpu.VMEM((DECAY_ROWS, width), jnp.float32),
+            pltpu.SemaphoreType.DMA((len(shifts),)),
+            pltpu.SemaphoreType.DMA((len(shifts),)),
+        ],
+        compiler_params=pltpu.CompilerParams(collective_id=0, has_side_effects=True),
+    )(state.astype(jnp.float32), decay)
 
 
 def rms_rows(embedded_entries, norm_gain):
@@ -106,7 +181,10 @@
     group = lax.axis_size("tp")
     copies = jnp.broadcast_to(normed[None], (group,) + normed.shape)
     every_row_list = lax.all_to_all(copies, "tp", 0, 0, tiled=True).reshape(-1, normed.shape[1])
-    parameter_collection = lax.all_gather(w_qkv, "ctx", axis=0, tiled=True)
+    width = w_qkv.shape[1]
+    both = lax.all_gather(jnp.concatenate([w_qkv, w_out.T], axis=1), "ctx", axis=0, tiled=True)
+    parameter_collection = both[:, :width]
+    out_rows = both[:, width:]
     rows_combined = jnp.dot(
         every_row_list, parameter_collection, preferred_element_type=jnp.float32
     )
@@ -132,7 +210,7 @@
     state_list.append(local_state)
     passing_list.append(passing)
     carried_list.append(carried)
-    incoming = carried_in(jnp.stack(passing_list), jnp.stack(state_list), "ctx")
+    incoming = carried_in(passing_list[0], state_list[0], "ctx")[None]
     attention_slot_number = 0
     head_out = inner_list[attention_slot_number] + apply_state(
         query_list[attention_slot_number],
@@ -140,7 +218,6 @@
         incoming[attention_slot_number],
     )
     normed_heads = head_norm(head_out, head_gain)
-    out_rows = lax.all_gather(w_out.T, "ctx", axis=0, tiled=True)
     projected = lax.dot_general(
         normed_heads, out_rows, (((1,), (1,)), ((), ())), preferred_element_type=jnp.float32
     )

time: 285 us -> 278 us (0.975)
  Pallas kernels: 0 us -> 55.9 us
  waiting for transfers between devices: 192 us -> 157 us
  starting transfers between devices: 17.9 us -> 4.96 us
  local copies, waits for them, and re-layouts: 15.7 us -> 7.09 us
  between operations: 21.9 us -> 15.4 us
    ppermute x6 -> x0, waiting for transfers between devices: 57.1 us -> none  [shifted(): got = lax.ppermute(message, axis, pairs)]
    pallas_call x0 -> x1, Pallas kernels: none -> 55.9 us  [carried_in(): pl.pallas_call(functools.partial(scan_kernel, count, shifts), out_shape=j...]
    all_gather x2 -> x1, waiting for transfers between devices: 20.2 us -> 37.8 us  [local(): lax.all_gather(jnp.concatenate([w_qkv, w_out.T], axis=1), 'ctx', axis=0,...]
    ppermute x6 -> x0, starting transfers between devices: 12.9 us -> none  [shifted(): got = lax.ppermute(message, axis, pairs)]
    scatter x10 -> x0, local copies, waits for them, and re-layouts: 6.5 us -> none  [shifted(): extra = extra.at[:, 0, 0].set(high).at[:, 0, 1].set(low)]
    reduce_scatter x1, waiting for transfers between devices: 49 us -> 52.4 us  [local(): lax.psum_scatter(projected.astype(jnp.bfloat16), 'tp', scatter_dimension=...]
    all_to_all x1, waiting for transfers between devices: 63.8 us -> 66.7 us  [local(): lax.all_to_all(copies, 'tp', 0, 0, tiled=True).reshape(-1, normed.shape[1])]
    slice x5 -> x1, local copies, waits for them, and re-layouts: 2.96 us -> 0.07 us  [shifted(): got[:, rows, 1].astype(jnp.float32)]
  transfers between devices with their start and end apart: 10 -> 3, of which waited for: 9 -> 3; matrix products, arithmetic and copies ran while one was open for 14% -> 3% of each run, Pallas kernels for 0% -> 0%
where the time goes in v6:
time: 278 us; the launch traced here: 275 us
  waiting for transfers between devices  157 us (56%)
  Pallas kernels  55.9 us (20%)
  matrix products  28.2 us (10%)
  between operations  15.4 us (6%)
  local copies, waits for them, and re-layouts  7.09 us (3%)
  other arithmetic  6.58 us (2%)
  starting transfers between devices  4.96 us (2%)
    all_to_all x1, waiting for transfers between devices, local(): lax.all_to_all(copies, 'tp', 0, 0, tiled=True).reshape(-1, normed.shape[1])  66.7 us
    pallas_call x1, Pallas kernels, carried_in(): pl.pallas_call(functools.partial(scan_kernel, count, shifts), out_shape=j...  55.9 us
    reduce_scatter x1, waiting for transfers between devices, local(): lax.psum_scatter(projected.astype(jnp.bfloat16), 'tp', scatter_dimension=...  52.4 us
    all_gather x1, waiting for transfers between devices, local(): lax.all_gather(jnp.concatenate([w_qkv, w_out.T], axis=1), 'ctx', axis=0,...  37.8 us
    dot_general x1, matrix products, local(): jnp.dot(every_row_list, parameter_collection, preferred_element_type=jnp....  12 us
    dot_general x1, matrix products, local(): lax.dot_general(normed_heads, out_rows, (((1,), (1,)), ((), ())), preferr...  7.86 us
  transfers between devices with their start and end apart: 3, of which 3 were waited for; matrix products, arithmetic and copies ran while one was open for 3% of the time, Pallas kernels for 0%

profile of v6, /device:TPU:224, one launch (start us, length us, event | category | flops | bytes accessed | tf_op | source)
XLA Modules:
  0.0 275.1 jit_solution(16461451227619351306)
XLA Ops:
  6.5 0.0 copy-start
  6.5 0.0 copy-start.1
  6.5 0.0 all-gather.2.cloned.1.call-start
  6.5 1.1 copy.11
  7.6 1.7 pad_maximum_fusion
  9.3 0.0 all-gather.2.cloned.1.call-update
  9.4 0.0 copy-done
  9.4 0.3 fusion.7
  9.6 0.0 copy-done.1
  9.7 0.3 fusion.9
  9.9 3.4 %broadcast_in_dim.7 = bf16[8,96,4096]{2,1,0:T(8,128)(2,1)} broadcast(bf16[96,4096]{1,0:T(8,128)(2,1)S(1)} %fusion.9), dimensions={1,2} | broadcast | bytes 7077888 | tf_op jit(solution)/shard_map/broadcast_in_dim | solution.py:182
  13.3 0.0 copy-start.2
  13.3 0.0 copy-start.4
  13.3 0.0 copy-start.3
  13.3 4.9 %all-to-all-start = ((bf16[8,96,4096]{2,1,0:T(8,128)(2,1)}), bf16[8,96,4096]{2,1,0:T(8,128)(2,1)}, u32[]{:S(2)}, u32[]{:S(2)}) async-start(bf16[8,96,4096]{2,1,0:T(8,128)(2,1)} %broadcast_in_dim.7), calls=%async_computation | async-start | bytes 12582912 | tf_op jit(solution)/shard_map/all_to_all | solution.py:183
  18.2 0.0 reduce-scatter.2.cloned.1.call-start
  18.3 0.0 copy-done.2
  18.3 0.3 reduce-window.16
  18.6 0.1 slice.38
  19.3 0.0 copy-done.4
  19.4 0.3 reduce-window.24
  19.7 0.1 slice.40
  19.8 0.1 slice_reduce_fusion.1
  19.9 0.1 slice_reduce_fusion
  20.0 0.1 select_multiply_fusion
  20.1 0.6 slice.44
  20.7 0.6 slice.43
  22.5 0.0 copy-done.3
  22.5 1.2 exponential_select_fusion
  23.7 66.7 %all-to-all-done = bf16[8,96,4096]{2,1,0:T(8,128)(2,1)} async-done(((bf16[8,96,4096]{2,1,0:T(8,128)(2,1)}), bf16[8,96,4096]{2,1,0:T(8,128)(2,1)}, u32[]{:S(2)}, u32[]{:S(2)}) %all-to-all-start) | async-done | bytes 6291488 | tf_op jit(solution)/shard_map/all_to_all | solution.py:183
  90.4 37.8 %all-gather.2.cloned.1.call-done = bf16[4096,1536]{1,0:T(8,128)(2,1)} async-done(((bf16[128,1536]{1,0:T(8,128)(2,1)}), bf16[4096,1536]{1,0:T(8,128)(2,1)}) %all-gather.2.cloned.1.call-update) | async-done | bytes 12582928 | tf_op jit(solution)/shard_map/all_gather | solution.py:185
  128.2 12.0 %fusion.4 = bf16[768,1024]{1,0:T(8,128)(2,1)} fusion(bf16[768,4096]{1,0:T(8,128)(2,1)} %bitcast, bf16[4096,1536]{1,0:T(8,128)(2,1)} %all-gather.2.cloned.1.call-done), kind=kOutput, calls=%fused_computation.10 | convolution fusion | flops 6443237376 | bytes 16252928 | tf_op jit(solution)/shard_map/dot_general | solution.py:188
  140.2 2.8 %fusion.11 = f32[768,512]{0,1:T(8,128)S(1)} fusion(f32[768]{0:T(1024)S(1)} %multiply_reduce_fusion.1, f32[768]{0:T(1024)S(1)} %get-tuple-element.7, s32[768]{0:T(1024)S(1)} %get-tuple-element.6, bf16[768,1024]{1,0:T(8,128)(2,1)} %fusion.4), kind=kOutput, calls=%fused_computation.18 | convolution fusion | flops 911867904 | bytes 3166208 | tf_op jit(solution)/shard_map/dot_general | solution.py:142
  143.0 2.6 fusion.24.state_ref
  145.6 0.6 broadcast_in_dim.8.decay_ref
  146.2 55.9 %shard_map.91 = f32[256,512]{1,0:T(8,128)} custom-call(f32[256,512]{1,0:T(8,128)} %fusion.24.state_ref, f32[16,512]{1,0:T(8,128)} %broadcast_in_dim.8.decay_ref), custom_call_target="tpu_custom_call" | custom-call | tf_op jit(solution)/shard_map/pallas_call | solution.py:105
  202.1 2.9 %fusion.42 = (f32[768]{0:T(1024)S(1)}, f32[768,512]{0,1:T(8,128)S(1)}) fusion(f32[768,512]{0,1:T(8,128)S(1)} %fusion.11, f32[256,512]{1,0:T(8,128)} %shard_map.91, f32[768]{0:T(1024)S(1)} %get-tuple-element.5, bf16[768,1024]{1,0:T(8,128)(2,1)} %fusion.4), kind=kOutput, calls=%fused_computation.63 | convolution fusion | flops 1209138432 | bytes 4069376 | tf_op jit(solution)/shard_map/dot_general | solution.py:157
  205.1 0.0 copy-start.5
  205.1 0.2 multiply_reduce_fusion
  205.3 0.5 copy-done.5
  205.7 7.9 %convolution_convert_fusion = bf16[768,4096]{1,0:T(8,128)(2,1)} fusion(bf16[4096,1536]{1,0:T(8,128)(2,1)} %all-gather.2.cloned.1.call-done, f32[768,512]{0,1:T(8,128)S(1)} %get-tuple-element.9, f32[512]{0:T(512)S(1)} %copy-done.5, f32[768]{0:T(1024)S(1)} %add_rsqrt_fusion, f32[768]{0:T(1024)S(1)} %broadcast_multiply_fusion), kind=kOutput, calls=%fused_computation.2 | convolution fusion | flops 3225944064 | bytes 12066816 | tf_op jit(solution)/shard_map/dot_general | solution.py:221
  213.6 0.0 reduce-scatter.2.cloned.1.call-update
  213.6 52.4 %reduce-scatter.2.cloned.1.call-done = bf16[96,4096]{1,0:T(8,128)(2,1)} async-done(((bf16[768,4096]{1,0:T(8,128)(2,1)}), bf16[96,4096]{1,0:T(8,128)(2,1)}) %reduce-scatter.2.cloned.1.call-update) | async-done | bytes 786448 | tf_op jit(solution)/shard_map/reduce_scatter | solution.py:224
  266.1 2.2 fusion.10
  (8 shorter events, 0.1 us)
Async XLA Ops:
  6.5 2.8 %copy-start = (bf16[96,4096]{1,0:T(8,128)(2,1)S(1)}, bf16[96,4096]{1,0:T(8,128)(2,1)}, u32[]{:S(2)}) copy-start(bf16[96,4096]{1,0:T(8,128)(2,1)} %param.9) | copy-start | bytes 2359300
  6.5 3.1 %copy-start.1 = (f32[4096]{0:T(1024)S(1)}, f32[4096]{0:T(1024)}, u32[]{:S(2)}) copy-start(f32[4096]{0:T(1024)} %param.10) | copy-start | bytes 49156
  6.5 121.6 %all-gather.2.cloned.1.call-start = ((), (), s32[]{:S(2)}) async-start(), calls=%async_computation.2 | async-start | bytes 12976128 | tf_op jit(solution)/shard_map/all_gather | solution.py:185
  13.3 5.0 %copy-start.2 = (s32[768]{0:T(1024)S(1)}, s32[768]{0:T(1024)}, u32[]{:S(2)}) copy-start(s32[768]{0:T(1024)} %param.17) | copy-start | bytes 9220
  13.3 6.0 %copy-start.4 = (s32[1,768]{1,0:T(1,128)S(1)}, s32[1,768]{1,0:T(1,128)}, u32[]{:S(2)}) copy-start(s32[1,768]{1,0:T(1,128)} %param.15) | copy-start | bytes 9220
  13.3 9.2 %copy-start.3 = (s32[1,768]{1,0:T(1,128)S(1)}, s32[1,768]{1,0:T(1,128)}, u32[]{:S(2)}) copy-start(s32[1,768]{1,0:T(1,128)} %param.14) | copy-start | bytes 9220
  13.3 77.1 %all-to-all-start = ((bf16[8,96,4096]{2,1,0:T(8,128)(2,1)}), bf16[8,96,4096]{2,1,0:T(8,128)(2,1)}, u32[]{:S(2)}, u32[]{:S(2)}) async-start(bf16[8,96,4096]{2,1,0:T(8,128)(2,1)} %broadcast_in_dim.7), calls=%async_computation | async-start | bytes 12582912 | tf_op jit(solution)/shard_map/all_to_all | solution.py:183
  18.2 247.8 %reduce-scatter.2.cloned.1.call-start = ((), (), s32[]{:S(2)}) async-start(), calls=%async_computation.3 | async-start | bytes 7077888 | tf_op jit(solution)/shard_map/reduce_scatter | solution.py:224
  205.1 0.7 copy-start.5
Sparse Core Ops, SparseCore 0:
  9.9 118.1 all-gather.1
  213.7 52.2 reduce-scatter.1

commit v7 on v6

--- a/solution.py
+++ b/solution.py
@@ -30,15 +30,19 @@
 
 
 def scan_kernel(count, shifts, state_ref, decay_ref, out_ref, send_buf, recv_buf, acc_total, acc_decay, send_sems, recv_sems):
-    me = lax.axis_index("ctx")
+    rows_of_z = lax.axis_size("cy")
+    me = lax.axis_index("cz") * rows_of_z + lax.axis_index("cy")
     tp = lax.axis_index("tp")
     rows = state_ref.shape[0]
+
+    def place(peer):
+        return (peer // rows_of_z, peer % rows_of_z, tp)
 
     barrier = pltpu.get_barrier_semaphore()
     partners = sorted(set(shifts))
     for s in partners:
         for peer in (lax.rem(me + s, count), lax.rem(me + count - s, count)):
-            pl.semaphore_signal(barrier, 1, device_id=(peer, tp), device_id_type=MESH_ID)
+            pl.semaphore_signal(barrier, 1, device_id=place(peer), device_id_type=MESH_ID)
     pl.semaphore_wait(barrier, 2 * len(partners))
 
     def pack(slot, total, decay):
@@ -53,7 +57,7 @@
             dst_ref=recv_buf.at[j],
             send_sem=send_sems.at[j],
             recv_sem=recv_sems.at[j],
-            device_id=(peer, tp),
+            device_id=place(peer),
             device_id_type=MESH_ID,
         )
 
@@ -94,8 +98,8 @@
             copy(j, 0 if j < first else j - 1, me + shifts[j]).wait_send()
 
 
-def carried_in(passing, state, axis):
-    count = lax.axis_size(axis)
+def carried_in(passing, state):
+    count = lax.axis_size("cz") * lax.axis_size("cy")
     if count == 1:
         return jnp.zeros_like(state)
     shifts = scan_shifts(count)
@@ -182,7 +186,8 @@
     copies = jnp.broadcast_to(normed[None], (group,) + normed.shape)
     every_row_list = lax.all_to_all(copies, "tp", 0, 0, tiled=True).reshape(-1, normed.shape[1])
     width = w_qkv.shape[1]
-    both = lax.all_gather(jnp.concatenate([w_qkv, w_out.T], axis=1), "ctx", axis=0, tiled=True)
+    pieces = jnp.concatenate([w_qkv, w_out.T], axis=1)
+    both = lax.all_gather(lax.all_gather(pieces, "cy", axis=0, tiled=True), "cz", axis=0, tiled=True)
     parameter_collection = both[:, :width]
     out_rows = both[:, width:]
     rows_combined = jnp.dot(
@@ -210,7 +215,7 @@
     state_list.append(local_state)
     passing_list.append(passing)
     carried_list.append(carried)
-    incoming = carried_in(passing_list[0], state_list[0], "ctx")[None]
+    incoming = carried_in(passing_list[0], state_list[0])[None]
     attention_slot_number = 0
     head_out = inner_list[attention_slot_number] + apply_state(
         query_list[attention_slot_number],
@@ -231,17 +236,22 @@
 
 
 def solution(mesh):
+    z_rows = 4 if mesh.shape["ctx"] % 4 == 0 else 1
+    split = jax.sharding.Mesh(
+        mesh.devices.reshape(mesh.shape["ctx"] // z_rows, z_rows, mesh.shape["tp"]), ("cz", "cy", "tp")
+    )
+    blocks = ("cz", "cy")
     placed = (
-        P(("ctx", "tp"), None),
+        P(blocks + ("tp",), None),
         P(),
-        P("ctx", "tp"),
-        P("tp", "ctx"),
+        P(blocks, "tp"),
+        P("tp", blocks),
         P("tp"),
-        P("tp", "ctx"),
-        P("tp", "ctx"),
+        P("tp", blocks),
+        P("tp", blocks),
         P("tp"),
-        P("ctx"),
+        P(blocks),
     )
     return jax.shard_map(
-        local, mesh=mesh, in_specs=placed, out_specs=P(("ctx", "tp"), None), check_vma=False
-    )
+        local, mesh=split, in_specs=placed, out_specs=P(blocks + ("tp",), None), check_vma=False
+    )

time: 278 us -> 326 us (1.17)
  waiting for transfers between devices: 157 us -> 207 us
    all_gather x1 -> x2, waiting for transfers between devices: 37.8 us -> 82 us  [the longest x1 52.4 us: local(): lax.all_gather(lax.all_gather(pieces, 'cy', axis=0, tiled=True), 'cz', ax...]
    reduce_scatter x1, waiting for transfers between devices: 52.4 us -> 58.6 us  [local(): lax.psum_scatter(projected.astype(jnp.bfloat16), 'tp', scatter_dimension=...]
  transfers between devices with their start and end apart: 3 -> 4, of which waited for: 3 -> 4; matrix products, arithmetic and copies ran while one was open for 3% -> 2% of each run, Pallas kernels for 0% -> 0%
where the time goes in v7:
time: 326 us; the launch traced here: 323 us
  waiting for transfers between devices  207 us (63%)
  Pallas kernels  53.3 us (16%)
  matrix products  28.2 us (9%)
  between operations  15.2 us (5%)
  local copies, waits for them, and re-layouts  7.1 us (2%)
  other arithmetic  6.63 us (2%)
  starting transfers between devices  5 us (2%)
    all_to_all x1, waiting for transfers between devices, local(): lax.all_to_all(copies, 'tp', 0, 0, tiled=True).reshape(-1, normed.shape[1])  66.6 us
    reduce_scatter x1, waiting for transfers between devices, local(): lax.psum_scatter(projected.astype(jnp.bfloat16), 'tp', scatter_dimension=...  58.6 us
    pallas_call x1, Pallas kernels, carried_in(): pl.pallas_call(functools.partial(scan_kernel, count, shifts), out_shape=j...  53.3 us
    all_gather x1, waiting for transfers between devices, local(): lax.all_gather(lax.all_gather(pieces, 'cy', axis=0, tiled=True), 'cz', ax...  52.4 us
    all_gather x1, waiting for transfers between devices, local(): lax.all_gather(pieces, 'cy', axis=0, tiled=True)  29.6 us
    dot_general x1, matrix products, local(): jnp.dot(every_row_list, parameter_collection, preferred_element_type=jnp....  12 us
    dot_general x1, matrix products, local(): lax.dot_general(normed_heads, out_rows, (((1,), (1,)), ((), ())), preferr...  7.86 us
  transfers between devices with their start and end apart: 4, of which 4 were waited for; matrix products, arithmetic and copies ran while one was open for 2% of the time, Pallas kernels for 0%

profile of v7, /device:TPU:224, one launch (start us, length us, event | category | flops | bytes accessed | tf_op | source)
XLA Modules:
  0.0 322.6 jit_solution(5242302045425467063)
XLA Ops:
  6.5 0.0 copy-start
  6.5 0.0 all-gather.3.cloned.1.call-start
  6.5 1.1 copy.11
  7.6 1.7 pad_maximum_fusion
  9.3 0.0 copy-start.1
  9.3 0.0 all-gather.3.cloned.1.call-update
  9.4 0.0 all-gather.5.cloned.1.call-start
  9.4 29.6 %all-gather.3.cloned.1.call-done = bf16[512,1536]{1,0:T(8,128)(2,1)} async-done(((bf16[128,1536]{1,0:T(8,128)(2,1)}), bf16[512,1536]{1,0:T(8,128)(2,1)}) %all-gather.3.cloned.1.call-update) | async-done | bytes 1572880 | tf_op jit(solution)/shard_map/all_gather | solution.py:190
  39.1 0.0 all-gather.5.cloned.1.call-update
  39.1 0.0 copy-done
  39.1 0.3 fusion.7
  39.4 0.0 copy-done.1
  39.4 0.3 fusion.9
  39.6 3.4 %broadcast_in_dim.7 = bf16[8,96,4096]{2,1,0:T(8,128)(2,1)} broadcast(bf16[96,4096]{1,0:T(8,128)(2,1)S(1)} %fusion.9), dimensions={1,2} | broadcast | bytes 7077888 | tf_op jit(solution)/shard_map/broadcast_in_dim | solution.py:186
  43.0 0.0 copy-start.2
  43.0 0.0 copy-start.4
  43.0 0.0 copy-start.3
  43.0 4.9 %all-to-all-start = ((bf16[8,96,4096]{2,1,0:T(8,128)(2,1)}), bf16[8,96,4096]{2,1,0:T(8,128)(2,1)}, u32[]{:S(2)}, u32[]{:S(2)}) async-start(bf16[8,96,4096]{2,1,0:T(8,128)(2,1)} %broadcast_in_dim.7), calls=%async_computation | async-start | bytes 12582912 | tf_op jit(solution)/shard_map/all_to_all | solution.py:187
  47.9 0.0 reduce-scatter.2.cloned.1.call-start
  48.0 0.0 copy-done.2
  48.0 0.3 reduce-window.16
  48.3 0.1 slice.38
  49.0 0.0 copy-done.4
  49.1 0.3 reduce-window.24
  49.4 0.1 slice.40
  49.5 0.1 slice_reduce_fusion.1
  49.6 0.1 slice_reduce_fusion
  49.7 0.1 select_multiply_fusion
  49.8 0.6 slice.44
  50.4 0.6 slice.43
  52.2 0.0 copy-done.3
  52.3 1.2 exponential_select_fusion
  53.5 66.6 %all-to-all-done = bf16[8,96,4096]{2,1,0:T(8,128)(2,1)} async-done(((bf16[8,96,4096]{2,1,0:T(8,128)(2,1)}), bf16[8,96,4096]{2,1,0:T(8,128)(2,1)}, u32[]{:S(2)}, u32[]{:S(2)}) %all-to-all-start) | async-done | bytes 6291488 | tf_op jit(solution)/shard_map/all_to_all | solution.py:187
  120.1 52.4 %all-gather.5.cloned.1.call-done = bf16[4096,1536]{1,0:T(8,128)(2,1)} async-done(((bf16[512,1536]{1,0:T(8,128)(2,1)}), bf16[4096,1536]{1,0:T(8,128)(2,1)}) %all-gather.5.cloned.1.call-update) | async-done | bytes 12582928 | tf_op jit(solution)/shard_map/all_gather | solution.py:190
  172.5 12.0 %fusion.4 = bf16[768,1024]{1,0:T(8,128)(2,1)} fusion(bf16[768,4096]{1,0:T(8,128)(2,1)} %bitcast, bf16[4096,1536]{1,0:T(8,128)(2,1)} %all-gather.5.cloned.1.call-done), kind=kOutput, calls=%fused_computation.10 | convolution fusion | flops 6443237376 | bytes 16252928 | tf_op jit(solution)/shard_map/dot_general | solution.py:193
  184.5 2.8 fusion.11
  187.3 2.6 fusion.24.state_ref
  190.0 0.6 broadcast_in_dim.8.decay_ref
  190.6 53.3 %shard_map.91 = f32[256,512]{1,0:T(8,128)} custom-call(f32[256,512]{1,0:T(8,128)} %fusion.24.state_ref, f32[16,512]{1,0:T(8,128)} %broadcast_in_dim.8.decay_ref), custom_call_target="tpu_custom_call" | custom-call | tf_op jit(solution)/shard_map/pallas_call | solution.py:109
  243.8 2.9 fusion.42
  246.8 0.0 copy-start.5
  246.8 0.2 multiply_reduce_fusion
  247.0 0.5 copy-done.5
  247.4 7.9 %convolution_convert_fusion = bf16[768,4096]{1,0:T(8,128)(2,1)} fusion(bf16[4096,1536]{1,0:T(8,128)(2,1)} %all-gather.5.cloned.1.call-done, f32[768,512]{0,1:T(8,128)S(1)} %get-tuple-element.9, f32[512]{0:T(512)S(1)} %copy-done.5, f32[768]{0:T(1024)S(1)} %add_rsqrt_fusion, f32[768]{0:T(1024)S(1)} %broadcast_multiply_fusion), kind=kOutput, calls=%fused_computation.2 | convolution fusion | flops 3225944064 | bytes 12066816 | tf_op jit(solution)/shard_map/dot_general | solution.py:226
  255.3 0.0 reduce-scatter.2.cloned.1.call-update
  255.3 58.6 %reduce-scatter.2.cloned.1.call-done = bf16[96,4096]{1,0:T(8,128)(2,1)} async-done(((bf16[768,4096]{1,0:T(8,128)(2,1)}), bf16[96,4096]{1,0:T(8,128)(2,1)}) %reduce-scatter.2.cloned.1.call-update) | async-done | bytes 786448 | tf_op jit(solution)/shard_map/reduce_scatter | solution.py:229
  313.9 2.2 fusion.10
  (8 shorter events, 0.1 us)
Async XLA Ops:
  6.5 32.6 %copy-start = (bf16[96,4096]{1,0:T(8,128)(2,1)S(1)}, bf16[96,4096]{1,0:T(8,128)(2,1)}, u32[]{:S(2)}) copy-start(bf16[96,4096]{1,0:T(8,128)(2,1)} %param.9) | copy-start | bytes 2359300
  6.5 32.5 %all-gather.3.cloned.1.call-start = ((), (), s32[]{:S(2)}) async-start(), calls=%async_computation.2 | async-start | bytes 1966080 | tf_op jit(solution)/shard_map/all_gather | solution.py:190
  9.3 30.0 %copy-start.1 = (f32[4096]{0:T(1024)S(1)}, f32[4096]{0:T(1024)}, u32[]{:S(2)}) copy-start(f32[4096]{0:T(1024)} %param.10) | copy-start | bytes 49156
  9.4 163.1 %all-gather.5.cloned.1.call-start = ((), (), s32[]{:S(2)}) async-start(), calls=%async_computation.3 | async-start | bytes 14155776 | tf_op jit(solution)/shard_map/all_gather | solution.py:190
  43.0 5.0 %copy-start.2 = (s32[768]{0:T(1024)S(1)}, s32[768]{0:T(1024)}, u32[]{:S(2)}) copy-start(s32[768]{0:T(1024)} %param.17) | copy-start | bytes 9220
  43.0 6.0 %copy-start.4 = (s32[1,768]{1,0:T(1,128)S(1)}, s32[1,768]{1,0:T(1,128)}, u32[]{:S(2)}) copy-start(s32[1,768]{1,0:T(1,128)} %param.15) | copy-start | bytes 9220
  43.0 9.2 %copy-start.3 = (s32[1,768]{1,0:T(1,128)S(1)}, s32[1,768]{1,0:T(1,128)}, u32[]{:S(2)}) copy-start(s32[1,768]{1,0:T(1,128)} %param.14) | copy-start | bytes 9220
  43.0 77.1 %all-to-all-start = ((bf16[8,96,4096]{2,1,0:T(8,128)(2,1)}), bf16[8,96,4096]{2,1,0:T(8,128)(2,1)}, u32[]{:S(2)}, u32[]{:S(2)}) async-start(bf16[8,96,4096]{2,1,0:T(8,128)(2,1)} %broadcast_in_dim.7), calls=%async_computation | async-start | bytes 12582912 | tf_op jit(solution)/shard_map/all_to_all | solution.py:187
  47.9 266.0 %reduce-scatter.2.cloned.1.call-start = ((), (), s32[]{:S(2)}) async-start(), calls=%async_computation.4 | async-start | bytes 7077888 | tf_op jit(solution)/shard_map/reduce_scatter | solution.py:229
  246.8 0.7 copy-start.5
Sparse Core Ops, SparseCore 0:
  9.5 29.5 all-gather.2
  40.8 131.5 all-gather.4
  255.4 58.4 reduce-scatter.1

commit v8 on v7

--- a/solution.py
+++ b/solution.py
@@ -29,95 +29,172 @@
     return shifts
 
 
-def scan_kernel(count, shifts, state_ref, decay_ref, out_ref, send_buf, recv_buf, acc_total, acc_decay, send_sems, recv_sems):
-    rows_of_z = lax.axis_size("cy")
-    me = lax.axis_index("cz") * rows_of_z + lax.axis_index("cy")
+def pack(ref, total, decay):
+    rows = total.shape[0]
+    high = decay.astype(jnp.bfloat16)
+    ref[:rows, :] = total.astype(jnp.bfloat16)
+    ref[rows : rows + DECAY_ROWS, :] = high
+    ref[rows + DECAY_ROWS :, :] = (decay - high.astype(jnp.float32)).astype(jnp.bfloat16)
+
+
+def absorb(got, rows, acc_total, acc_decay):
+    far_total = got[:rows].astype(jnp.float32)
+    far_decay = got[rows : rows + DECAY_ROWS].astype(jnp.float32) + got[rows + DECAY_ROWS :].astype(jnp.float32)
+    decay = acc_decay[...]
+    acc_total[...] = decay[0:1, :] * far_total + acc_total[...]
+    acc_decay[...] = decay * far_decay
+
+
+def scan_kernel(
+    ny, nz, zshifts, state_ref, decay_ref, out_ref,
+    row_send, row_recv, z_send, z_recv, p_send, p_recv,
+    acc_total, acc_decay, quarter_total, quarter_decay, z_total, z_decay,
+    row_send_sems, row_recv_sems, z_send_sems, z_recv_sems, p_send_sems, p_recv_sems,
+):
+    yi = lax.axis_index("cy")
+    zi = lax.axis_index("cz")
     tp = lax.axis_index("tp")
-    rows = state_ref.shape[0]
-
-    def place(peer):
-        return (peer // rows_of_z, peer % rows_of_z, tp)
+    rows, width = state_ref.shape
+    quarter = width // ny
+    mine = pl.ds(pl.multiple_of(yi * quarter, quarter), quarter)
 
     barrier = pltpu.get_barrier_semaphore()
-    partners = sorted(set(shifts))
-    for s in partners:
-        for peer in (lax.rem(me + s, count), lax.rem(me + count - s, count)):
-            pl.semaphore_signal(barrier, 1, device_id=place(peer), device_id_type=MESH_ID)
-    pl.semaphore_wait(barrier, 2 * len(partners))
-
-    def pack(slot, total, decay):
-        high = decay.astype(jnp.bfloat16)
-        send_buf[slot, :rows, :] = total.astype(jnp.bfloat16)
-        send_buf[slot, rows : rows + DECAY_ROWS, :] = high
-        send_buf[slot, rows + DECAY_ROWS :, :] = (decay - high.astype(jnp.float32)).astype(jnp.bfloat16)
-
-    def copy(j, source_slot, peer):
+    z_partners = sorted(set(zshifts))
+    for d in range(1, ny):
+        pl.semaphore_signal(barrier, 1, device_id=(zi, lax.rem(yi + d, ny), tp), device_id_type=MESH_ID)
+    for s in z_partners:
+        for peer in (lax.rem(zi + s, nz), lax.rem(zi + nz - s, nz)):
+            pl.semaphore_signal(barrier, 1, device_id=(peer, yi, tp), device_id_type=MESH_ID)
+    pl.semaphore_wait(barrier, (ny - 1) + 2 * len(z_partners))
+
+    def row_copy(d, target, slot):
         return pltpu.make_async_remote_copy(
-            src_ref=send_buf.at[source_slot],
-            dst_ref=recv_buf.at[j],
-            send_sem=send_sems.at[j],
-            recv_sem=recv_sems.at[j],
-            device_id=place(peer),
-            device_id_type=MESH_ID,
+            src_ref=row_send, dst_ref=row_recv.at[slot], send_sem=row_send_sems.at[d],
+            recv_sem=row_recv_sems.at[slot], device_id=(zi, target, tp), device_id_type=MESH_ID,
         )
 
-    def send(j, source_slot):
-        @pl.when(me + shifts[j] < count)
-        def _():
-            copy(j, source_slot, me + shifts[j]).start()
-
-    def absorb(j, source_slot):
-        @pl.when(me - shifts[j] >= 0)
-        def _():
-            copy(j, source_slot, me - shifts[j]).wait_recv()
-            got = recv_buf[j]
-            far_total = got[:rows].astype(jnp.float32)
-            far_decay = got[rows : rows + DECAY_ROWS].astype(jnp.float32) + got[
-                rows + DECAY_ROWS :
-            ].astype(jnp.float32)
-            decay = acc_decay[...]
-            acc_total[...] = decay[0:1, :] * far_total + acc_total[...]
-            acc_decay[...] = decay * far_decay
+    pack(row_send, state_ref[...], decay_ref[...])
+    for d in range(1, ny):
+        row_copy(d, lax.rem(yi + d, ny), yi).start()
+    for d in range(1, ny):
+        source = lax.rem(yi + ny - d, ny)
+        row_copy(d, yi, source).wait_recv()
 
     acc_total[...] = jnp.zeros_like(acc_total)
     acc_decay[...] = jnp.ones_like(acc_decay)
-    pack(0, state_ref[...], decay_ref[...])
-    first = min(2, len(shifts))
+    for d in range(1, ny):
+        @pl.when(yi - d >= 0)
+        def _():
+            absorb(row_recv[yi - d], rows, acc_total, acc_decay)
+
+    quarter_total[...] = jnp.zeros_like(quarter_total)
+    quarter_decay[...] = jnp.ones_like(quarter_decay)
+    for y in reversed(range(ny)):
+        @pl.when(yi == y)
+        def _():
+            absorb(row_send[:, mine], rows, quarter_total, quarter_decay)
+
+        @pl.when(yi != y)
+        def _():
+            absorb(row_recv[y, :, mine], rows, quarter_total, quarter_decay)
+
+    def z_copy(j, slot, peer):
+        return pltpu.make_async_remote_copy(
+            src_ref=z_send.at[slot], dst_ref=z_recv.at[j], send_sem=z_send_sems.at[j],
+            recv_sem=z_recv_sems.at[j], device_id=(peer, yi, tp), device_id_type=MESH_ID,
+        )
+
+    def z_send_round(j, slot):
+        @pl.when(zi + zshifts[j] < nz)
+        def _():
+            z_copy(j, slot, zi + zshifts[j]).start()
+
+    def z_absorb(j, slot):
+        @pl.when(zi - zshifts[j] >= 0)
+        def _():
+            z_copy(j, slot, zi - zshifts[j]).wait_recv()
+            absorb(z_recv[j], rows, z_total, z_decay)
+
+    z_total[...] = jnp.zeros_like(z_total)
+    z_decay[...] = jnp.ones_like(z_decay)
+    first = min(2, len(zshifts))
+    if zshifts:
+        pack(z_send.at[0], quarter_total[...], quarter_decay[...])
     for j in range(first):
-        send(j, 0)
+        z_send_round(j, 0)
     for j in range(first):
-        absorb(j, 0)
-    for j in range(first, len(shifts)):
-        pack(j - 1, acc_total[...], acc_decay[...])
-        send(j, j - 1)
-        absorb(j, j - 1)
-    out_ref[...] = acc_total[...]
-    for j in range(len(shifts)):
-        @pl.when(me + shifts[j] < count)
-        def _():
-            copy(j, 0 if j < first else j - 1, me + shifts[j]).wait_send()
+        z_absorb(j, 0)
+    for j in range(first, len(zshifts)):
+        pack(z_send.at[j - 1], z_total[...], z_decay[...])
+        z_send_round(j, j - 1)
+        z_absorb(j, j - 1)
+
+    def p_copy(d, target, slot):
+        return pltpu.make_async_remote_copy(
+            src_ref=p_send, dst_ref=p_recv.at[slot], send_sem=p_send_sems.at[d],
+            recv_sem=p_recv_sems.at[slot], device_id=(zi, target, tp), device_id_type=MESH_ID,
+        )
+
+    p_send[...] = z_total[...].astype(jnp.bfloat16)
+    for d in range(1, ny):
+        p_copy(d, lax.rem(yi + d, ny), yi).start()
+    for d in range(1, ny):
+        p_copy(d, yi, lax.rem(yi + ny - d, ny)).wait_recv()
+    decay = acc_decay[0:1, :]
+    for y in range(ny):
+        cols = slice(y * quarter, (y + 1) * quarter)
+
+        @pl.when(yi == y)
+        def _():
+            out_ref[:, cols] = decay[:, cols] * p_send[...].astype(jnp.float32) + acc_total[:, cols]
+
+        @pl.when(yi != y)
+        def _():
+            out_ref[:, cols] = decay[:, cols] * p_recv[y].astype(jnp.float32) + acc_total[:, cols]
+
+    for d in range(1, ny):
+        row_copy(d, lax.rem(yi + d, ny), yi).wait_send()
+        p_copy(d, lax.rem(yi + d, ny), yi).wait_send()
+    for j in range(len(zshifts)):
+        @pl.when(zi + zshifts[j] < nz)
+        def _():
+            z_copy(j, 0 if j < first else j - 1, zi + zshifts[j]).wait_send()
 
 
 def carried_in(passing, state):
-    count = lax.axis_size("cz") * lax.axis_size("cy")
-    if count == 1:
+    ny, nz = lax.axis_size("cy"), lax.axis_size("cz")
+    if ny * nz == 1:
         return jnp.zeros_like(state)
-    shifts = scan_shifts(count)
+    zshifts = scan_shifts(nz) if nz > 1 else []
     rows, width = state.shape
+    quarter = width // ny
     decay = jnp.broadcast_to(passing.reshape(1, 1), (DECAY_ROWS, width)).astype(jnp.float32)
-    message = (len(shifts), rows + 2 * DECAY_ROWS, width)
+    message = rows + 2 * DECAY_ROWS
+    slots = max(len(zshifts), 1)
     return pl.pallas_call(
-        functools.partial(scan_kernel, count, shifts),
+        functools.partial(scan_kernel, ny, nz, zshifts),
         out_shape=jax.ShapeDtypeStruct((rows, width), jnp.float32),
         in_specs=[pl.BlockSpec(memory_space=pltpu.VMEM)] * 2,
         out_specs=pl.BlockSpec(memory_space=pltpu.VMEM),
         scratch_shapes=[
-            pltpu.VMEM(message, jnp.bfloat16),
-            pltpu.VMEM(message, jnp.bfloat16),
+            pltpu.VMEM((message, width), jnp.bfloat16),
+            pltpu.VMEM((ny, message, width), jnp.bfloat16),
+            pltpu.VMEM((slots, message, quarter), jnp.bfloat16),
+            pltpu.VMEM((slots, message, quarter), jnp.bfloat16),
+            pltpu.VMEM((rows, quarter), jnp.bfloat16),
+            pltpu.VMEM((ny, rows, quarter), jnp.bfloat16),
             pltpu.VMEM((rows, width), jnp.float32),
             pltpu.VMEM((DECAY_ROWS, width), jnp.float32),
-            pltpu.SemaphoreType.DMA((len(shifts),)),
-            pltpu.SemaphoreType.DMA((len(shifts),)),
+            pltpu.VMEM((rows, quarter), jnp.float32),
+            pltpu.VMEM((DECAY_ROWS, quarter), jnp.float32),
+            pltpu.VMEM((rows, quarter), jnp.float32),
+            pltpu.VMEM((DECAY_ROWS, quarter), jnp.float32),
+            pltpu.SemaphoreType.DMA((ny,)),
+            pltpu.SemaphoreType.DMA((ny,)),
+            pltpu.SemaphoreType.DMA((slots,)),
+            pltpu.SemaphoreType.DMA((slots,)),
+            pltpu.SemaphoreType.DMA((ny,)),
+            pltpu.SemaphoreType.DMA((ny,)),
         ],
         compiler_params=pltpu.CompilerParams(collective_id=0, has_side_effects=True),
     )(state.astype(jnp.float32), decay)
@@ -186,8 +263,7 @@
     copies = jnp.broadcast_to(normed[None], (group,) + normed.shape)
     every_row_list = lax.all_to_all(copies, "tp", 0, 0, tiled=True).reshape(-1, normed.shape[1])
     width = w_qkv.shape[1]
-    pieces = jnp.concatenate([w_qkv, w_out.T], axis=1)
-    both = lax.all_gather(lax.all_gather(pieces, "cy", axis=0, tiled=True), "cz", axis=0, tiled=True)
+    both = lax.all_gather(jnp.concatenate([w_qkv, w_out.T], axis=1), ("cz", "cy"), axis=0, tiled=True)
     parameter_collection = both[:, :width]
     out_rows = both[:, width:]
     rows_combined = jnp.dot(

time: 326 us -> 255 us (0.78)
  waiting for transfers between devices: 207 us -> 147 us
  Pallas kernels: 53.3 us -> 41.8 us
    all_gather x2 -> x1, waiting for transfers between devices: 82 us -> 37.8 us  [local(): lax.all_gather(jnp.concatenate([w_qkv, w_out.T], axis=1), ('cz', 'cy'), a...]
    reduce_scatter x1, waiting for transfers between devices: 58.6 us -> 42.8 us  [local(): lax.psum_scatter(projected.astype(jnp.bfloat16), 'tp', scatter_dimension=...]
    pallas_call x1, Pallas kernels: 53.3 us -> 41.8 us  [carried_in(): pl.pallas_call(functools.partial(scan_kernel, ny, nz, zshifts), out_shape...]
  transfers between devices with their start and end apart: 4 -> 3, of which waited for: 4 -> 3; matrix products, arithmetic and copies ran while one was open for 2% -> 3% of each run, Pallas kernels for 0% -> 0%
where the time goes in v8:
time: 255 us; the launch traced here: 251 us
  waiting for transfers between devices  147 us (58%)
  Pallas kernels  41.8 us (16%)
  matrix products  28.2 us (11%)
  between operations  15.4 us (6%)
  local copies, waits for them, and re-layouts  7.09 us (3%)
  other arithmetic  6.58 us (3%)
  starting transfers between devices  4.96 us (2%)
    all_to_all x1, waiting for transfers between devices, local(): lax.all_to_all(copies, 'tp', 0, 0, tiled=True).reshape(-1, normed.shape[1])  66.7 us
    reduce_scatter x1, waiting for transfers between devices, local(): lax.psum_scatter(projected.astype(jnp.bfloat16), 'tp', scatter_dimension=...  42.8 us
    pallas_call x1, Pallas kernels, carried_in(): pl.pallas_call(functools.partial(scan_kernel, ny, nz, zshifts), out_shape...  41.8 us
    all_gather x1, waiting for transfers between devices, local(): lax.all_gather(jnp.concatenate([w_qkv, w_out.T], axis=1), ('cz', 'cy'), a...  37.8 us
    dot_general x1, matrix products, local(): jnp.dot(every_row_list, parameter_collection, preferred_element_type=jnp....  12 us
    dot_general x1, matrix products, local(): lax.dot_general(normed_heads, out_rows, (((1,), (1,)), ((), ())), preferr...  7.86 us
  transfers between devices with their start and end apart: 3, of which 3 were waited for; matrix products, arithmetic and copies ran while one was open for 3% of the time, Pallas kernels for 0%

profile of v8, /device:TPU:224, one launch (start us, length us, event | category | flops | bytes accessed | tf_op | source)
XLA Modules:
  0.0 251.4 jit_solution(10309291934833659802)
XLA Ops:
  6.5 0.0 copy-start
  6.5 0.0 copy-start.1
  6.5 0.0 all-gather.2.cloned.1.call-start
  6.5 1.1 copy.11
  7.6 1.7 pad_maximum_fusion
  9.3 0.0 all-gather.2.cloned.1.call-update
  9.4 0.0 copy-done
  9.4 0.3 fusion.7
  9.6 0.0 copy-done.1
  9.7 0.3 fusion.9
  9.9 3.4 %broadcast_in_dim.7 = bf16[8,96,4096]{2,1,0:T(8,128)(2,1)} broadcast(bf16[96,4096]{1,0:T(8,128)(2,1)S(1)} %fusion.9), dimensions={1,2} | broadcast | bytes 7077888 | tf_op jit(solution)/shard_map/broadcast_in_dim | solution.py:263
  13.3 0.0 copy-start.2
  13.3 0.0 copy-start.4
  13.3 0.0 copy-start.3
  13.3 4.9 %all-to-all-start = ((bf16[8,96,4096]{2,1,0:T(8,128)(2,1)}), bf16[8,96,4096]{2,1,0:T(8,128)(2,1)}, u32[]{:S(2)}, u32[]{:S(2)}) async-start(bf16[8,96,4096]{2,1,0:T(8,128)(2,1)} %broadcast_in_dim.7), calls=%async_computation | async-start | bytes 12582912 | tf_op jit(solution)/shard_map/all_to_all | solution.py:264
  18.2 0.0 reduce-scatter.2.cloned.1.call-start
  18.3 0.0 copy-done.2
  18.3 0.3 reduce-window.16
  18.6 0.1 slice.38
  19.3 0.0 copy-done.4
  19.4 0.3 reduce-window.24
  19.7 0.1 slice.40
  19.8 0.1 slice_reduce_fusion.1
  19.9 0.1 slice_reduce_fusion
  20.0 0.1 select_multiply_fusion
  20.1 0.6 slice.44
  20.7 0.6 slice.43
  22.5 0.0 copy-done.3
  22.5 1.2 exponential_select_fusion
  23.7 66.7 %all-to-all-done = bf16[8,96,4096]{2,1,0:T(8,128)(2,1)} async-done(((bf16[8,96,4096]{2,1,0:T(8,128)(2,1)}), bf16[8,96,4096]{2,1,0:T(8,128)(2,1)}, u32[]{:S(2)}, u32[]{:S(2)}) %all-to-all-start) | async-done | bytes 6291488 | tf_op jit(solution)/shard_map/all_to_all | solution.py:264
  90.4 37.8 %all-gather.2.cloned.1.call-done = bf16[4096,1536]{1,0:T(8,128)(2,1)} async-done(((bf16[128,1536]{1,0:T(8,128)(2,1)}), bf16[4096,1536]{1,0:T(8,128)(2,1)}) %all-gather.2.cloned.1.call-update) | async-done | bytes 12582928 | tf_op jit(solution)/shard_map/all_gather | solution.py:266
  128.2 12.0 %fusion.4 = bf16[768,1024]{1,0:T(8,128)(2,1)} fusion(bf16[768,4096]{1,0:T(8,128)(2,1)} %bitcast, bf16[4096,1536]{1,0:T(8,128)(2,1)} %all-gather.2.cloned.1.call-done), kind=kOutput, calls=%fused_computation.10 | convolution fusion | flops 6443237376 | bytes 16252928 | tf_op jit(solution)/shard_map/dot_general | solution.py:269
  140.2 2.8 %fusion.11 = f32[768,512]{0,1:T(8,128)S(1)} fusion(f32[768]{0:T(1024)S(1)} %multiply_reduce_fusion.1, f32[768]{0:T(1024)S(1)} %get-tuple-element.7, s32[768]{0:T(1024)S(1)} %get-tuple-element.6, bf16[768,1024]{1,0:T(8,128)(2,1)} %fusion.4), kind=kOutput, calls=%fused_computation.18 | convolution fusion | flops 911867904 | bytes 3166208 | tf_op jit(solution)/shard_map/dot_general | solution.py:223
  143.0 2.6 %fusion.24.state_ref = f32[256,512]{1,0:T(8,128)} fusion(bf16[768,1024]{1,0:T(8,128)(2,1)} %fusion.4, f32[768]{0:T(1024)S(1)} %exponential_select_fusion), kind=kOutput, calls=%fused_computation.32 | convolution fusion | flops 201916416 | bytes 1707008 | tf_op jit(solution)/shard_map/dot_general | solution.py:228
  145.6 0.6 broadcast_in_dim.8.decay_ref
  146.2 41.8 %shard_map.91 = f32[256,512]{1,0:T(8,128)} custom-call(f32[256,512]{1,0:T(8,128)} %fusion.24.state_ref, f32[16,512]{1,0:T(8,128)} %broadcast_in_dim.8.decay_ref), custom_call_target="tpu_custom_call" | custom-call | tf_op jit(solution)/shard_map/pallas_call | solution.py:174
  188.0 2.9 %fusion.42 = (f32[768]{0:T(1024)S(1)}, f32[768,512]{0,1:T(8,128)S(1)}) fusion(f32[768,512]{0,1:T(8,128)S(1)} %fusion.11, f32[256,512]{1,0:T(8,128)} %shard_map.91, f32[768]{0:T(1024)S(1)} %get-tuple-element.5, bf16[768,1024]{1,0:T(8,128)(2,1)} %fusion.4), kind=kOutput, calls=%fused_computation.63 | convolution fusion | flops 1209138432 | bytes 4069376 | tf_op jit(solution)/shard_map/dot_general | solution.py:238
  190.9 0.0 copy-start.5
  191.0 0.2 multiply_reduce_fusion
  191.2 0.5 copy-done.5
  191.6 7.9 %convolution_convert_fusion = bf16[768,4096]{1,0:T(8,128)(2,1)} fusion(bf16[4096,1536]{1,0:T(8,128)(2,1)} %all-gather.2.cloned.1.call-done, f32[768,512]{0,1:T(8,128)S(1)} %get-tuple-element.9, f32[512]{0:T(512)S(1)} %copy-done.5, f32[768]{0:T(1024)S(1)} %add_rsqrt_fusion, f32[768]{0:T(1024)S(1)} %broadcast_multiply_fusion), kind=kOutput, calls=%fused_computation.2 | convolution fusion | flops 3225944064 | bytes 12066816 | tf_op jit(solution)/shard_map/dot_general | solution.py:302
  199.5 0.0 reduce-scatter.2.cloned.1.call-update
  199.5 42.8 %reduce-scatter.2.cloned.1.call-done = bf16[96,4096]{1,0:T(8,128)(2,1)} async-done(((bf16[768,4096]{1,0:T(8,128)(2,1)}), bf16[96,4096]{1,0:T(8,128)(2,1)}) %reduce-scatter.2.cloned.1.call-update) | async-done | bytes 786448 | tf_op jit(solution)/shard_map/reduce_scatter | solution.py:305
  242.3 2.2 fusion.10
  (8 shorter events, 0.1 us)
Async XLA Ops:
  6.5 2.8 %copy-start = (bf16[96,4096]{1,0:T(8,128)(2,1)S(1)}, bf16[96,4096]{1,0:T(8,128)(2,1)}, u32[]{:S(2)}) copy-start(bf16[96,4096]{1,0:T(8,128)(2,1)} %param.9) | copy-start | bytes 2359300
  6.5 3.1 %copy-start.1 = (f32[4096]{0:T(1024)S(1)}, f32[4096]{0:T(1024)}, u32[]{:S(2)}) copy-start(f32[4096]{0:T(1024)} %param.10) | copy-start | bytes 49156
  6.5 121.6 %all-gather.2.cloned.1.call-start = ((), (), s32[]{:S(2)}) async-start(), calls=%async_computation.2 | async-start | bytes 12976128 | tf_op jit(solution)/shard_map/all_gather | solution.py:266
  13.3 5.0 %copy-start.2 = (s32[768]{0:T(1024)S(1)}, s32[768]{0:T(1024)}, u32[]{:S(2)}) copy-start(s32[768]{0:T(1024)} %param.17) | copy-start | bytes 9220
  13.3 6.0 %copy-start.4 = (s32[1,768]{1,0:T(1,128)S(1)}, s32[1,768]{1,0:T(1,128)}, u32[]{:S(2)}) copy-start(s32[1,768]{1,0:T(1,128)} %param.15) | copy-start | bytes 9220
  13.3 9.2 %copy-start.3 = (s32[1,768]{1,0:T(1,128)S(1)}, s32[1,768]{1,0:T(1,128)}, u32[]{:S(2)}) copy-start(s32[1,768]{1,0:T(1,128)} %param.14) | copy-start | bytes 9220
  13.3 77.1 %all-to-all-start = ((bf16[8,96,4096]{2,1,0:T(8,128)(2,1)}), bf16[8,96,4096]{2,1,0:T(8,128)(2,1)}, u32[]{:S(2)}, u32[]{:S(2)}) async-start(bf16[8,96,4096]{2,1,0:T(8,128)(2,1)} %broadcast_in_dim.7), calls=%async_computation | async-start | bytes 12582912 | tf_op jit(solution)/shard_map/all_to_all | solution.py:264
  18.2 224.1 %reduce-scatter.2.cloned.1.call-start = ((), (), s32[]{:S(2)}) async-start(), calls=%async_computation.3 | async-start | bytes 7077888 | tf_op jit(solution)/shard_map/reduce_scatter | solution.py:305
  190.9 0.7 copy-start.5
Sparse Core Ops, SparseCore 0:
  9.9 118.1 all-gather.1
  199.6 42.6 reduce-scatter.1

commit v9 on v8

--- a/solution.py
+++ b/solution.py
@@ -159,6 +159,109 @@
         @pl.when(zi + zshifts[j] < nz)
         def _():
             z_copy(j, 0 if j < first else j - 1, zi + zshifts[j]).wait_send()
+
+
+def ring_steps(n):
+    steps = [(s, True) for s in range(1, (n - 1) // 2 + 1)]
+    if n % 2 == 0 and n > 1:
+        steps.append((n // 2, False))
+    return steps
+
+
+def gather_kernel(ny, nz, piece_ref, out_ref, local_sem, send_sems, recv_sems):
+    yi = lax.axis_index("cy")
+    zi = lax.axis_index("cz")
+    tp = lax.axis_index("tp")
+    half = piece_ref.shape[1] // 2
+    cols = (pl.ds(0, half), pl.ds(half, half))
+
+    barrier = pltpu.get_barrier_semaphore()
+    neighbours = [
+        (zi, lax.rem(yi + 1, ny), tp),
+        (zi, lax.rem(yi + ny - 1, ny), tp),
+        (lax.rem(zi + 1, nz), yi, tp),
+        (lax.rem(zi + nz - 1, nz), yi, tp),
+    ]
+    for peer in neighbours:
+        pl.semaphore_signal(barrier, 1, device_id=peer, device_id_type=MESH_ID)
+    pl.semaphore_wait(barrier, len(neighbours))
+
+    own = pltpu.make_async_copy(piece_ref, out_ref.at[zi, yi], local_sem.at[0])
+    own.start()
+    sends = []
+
+    def ring(along_y, group_of, first_src):
+        n, me = (ny, yi) if along_y else (nz, zi)
+        return dict(n=n, me=me, along_y=along_y, group_of=group_of, first_src=first_src, steps=ring_steps(n), last={})
+
+    def device(r, k):
+        return (zi, k, tp) if r["along_y"] else (k, yi, tp)
+
+    def step(r, t):
+        if t > len(r["steps"]):
+            return
+        n, me, group_of = r["n"], r["me"], r["group_of"]
+        hop, both = r["steps"][t - 1]
+        for sign in (1, -1) if both else (1,):
+            if t > 1:
+                r["last"].pop(sign).wait_recv()
+            origin = lax.rem(me + n - sign * (hop - 1), n)
+            target = lax.rem(me + n + sign, n)
+            source = lax.rem(me + n - sign, n)
+            arrived = lax.rem(me + 2 * n - sign * hop, n)
+            idx = len(sends)
+            send = pltpu.make_async_remote_copy(
+                src_ref=r["first_src"] if t == 1 else group_of(origin), dst_ref=group_of(origin),
+                send_sem=send_sems.at[idx], recv_sem=recv_sems.at[idx],
+                device_id=device(r, target), device_id_type=MESH_ID,
+            )
+            incoming = pltpu.make_async_remote_copy(
+                src_ref=group_of(arrived), dst_ref=group_of(arrived),
+                send_sem=send_sems.at[idx], recv_sem=recv_sems.at[idx],
+                device_id=device(r, source), device_id_type=MESH_ID,
+            )
+            send.start()
+            sends.append(send)
+            r["last"][sign] = incoming
+
+    def stage(rings):
+        for t in range(1, max(len(r["steps"]) for r in rings) + 1):
+            for r in rings:
+                step(r, t)
+        for r in rings:
+            for incoming in r["last"].values():
+                incoming.wait_recv()
+
+    stage([
+        ring(True, lambda k: out_ref.at[zi, k, :, cols[0]], piece_ref.at[:, cols[0]]),
+        ring(False, lambda k: out_ref.at[k, yi, :, cols[1]], piece_ref.at[:, cols[1]]),
+    ])
+    own.wait()
+    stage([
+        ring(False, lambda k: out_ref.at[k, :, :, cols[0]], out_ref.at[zi, :, :, cols[0]]),
+        ring(True, lambda k: out_ref.at[:, k, :, cols[1]], out_ref.at[:, yi, :, cols[1]]),
+    ])
+    for send in sends:
+        send.wait_send()
+
+
+def gather_blocks(piece):
+    ny, nz = lax.axis_size("cy"), lax.axis_size("cz")
+    rows, width = piece.shape
+    count = sum(2 if both else 1 for _, both in ring_steps(ny)) * 2 + sum(2 if both else 1 for _, both in ring_steps(nz)) * 2
+    out = pl.pallas_call(
+        functools.partial(gather_kernel, ny, nz),
+        out_shape=jax.ShapeDtypeStruct((nz, ny, rows, width), piece.dtype),
+        in_specs=[pl.BlockSpec(memory_space=pltpu.VMEM)],
+        out_specs=pl.BlockSpec(memory_space=pl.ANY),
+        scratch_shapes=[
+            pltpu.SemaphoreType.DMA((1,)),
+            pltpu.SemaphoreType.DMA((count,)),
+            pltpu.SemaphoreType.DMA((count,)),
+        ],
+        compiler_params=pltpu.CompilerParams(collective_id=1, has_side_effects=True),
+    )(piece)
+    return out.reshape(nz * ny * rows, width)
 
 
 def carried_in(passing, state):
@@ -263,7 +366,7 @@
     copies = jnp.broadcast_to(normed[None], (group,) + normed.shape)
     every_row_list = lax.all_to_all(copies, "tp", 0, 0, tiled=True).reshape(-1, normed.shape[1])
     width = w_qkv.shape[1]
-    both = lax.all_gather(jnp.concatenate([w_qkv, w_out.T], axis=1), ("cz", "cy"), axis=0, tiled=True)
+    both = gather_blocks(jnp.concatenate([w_qkv, w_out.T], axis=1))
     parameter_collection = both[:, :width]
     out_rows = both[:, width:]
     rows_combined = jnp.dot(

time: 255 us -> 237 us (0.929)
  waiting for transfers between devices: 147 us -> 43 us
  Pallas kernels: 41.8 us -> 132 us
  matrix products: 28.2 us -> 24.3 us
    pallas_call x0 -> x1, Pallas kernels: none -> 96.1 us  [gather_blocks(): pl.pallas_call(functools.partial(gather_kernel, ny, nz), out_shape=jax.Sh...]
    all_to_all x1, waiting for transfers between devices: 66.7 us -> 0.01 us  [local(): lax.all_to_all(copies, 'tp', 0, 0, tiled=True).reshape(-1, normed.shape[1])]
    all_gather x1 -> x0, waiting for transfers between devices: 37.8 us -> none  [local(): lax.all_gather(jnp.concatenate([w_qkv, w_out.T], axis=1), ('cz', 'cy'), a...]
    pallas_call x1, Pallas kernels: 41.8 us -> 36 us  [carried_in(): pl.pallas_call(functools.partial(scan_kernel, ny, nz, zshifts), out_shape...]
  transfers between devices with their start and end apart: 3 -> 2, of which waited for: 3 -> 1; matrix products, arithmetic and copies ran while one was open for 3% -> 2% of each run, Pallas kernels for 0% -> 41%
where the time goes in v9:
time: 237 us; the launch traced here: 234 us
  Pallas kernels  132 us (56%)
  waiting for transfers between devices  43 us (18%)
  matrix products  24.3 us (10%)
  between operations  15.5 us (7%)
  other arithmetic  7.9 us (3%)
  local copies, waits for them, and re-layouts  6.13 us (3%)
  starting transfers between devices  4.97 us (2%)
    pallas_call x1, Pallas kernels, gather_blocks(): pl.pallas_call(functools.partial(gather_kernel, ny, nz), out_shape=jax.Sh...  96.1 us
    reduce_scatter x1, waiting for transfers between devices, local(): lax.psum_scatter(projected.astype(jnp.bfloat16), 'tp', scatter_dimension=...  43 us
    pallas_call x1, Pallas kernels, carried_in(): pl.pallas_call(functools.partial(scan_kernel, ny, nz, zshifts), out_shape...  36 us
    dot_general x1, matrix products, local(): jnp.dot(every_row_list, parameter_collection, preferred_element_type=jnp....  10.9 us
    dot_general x1, matrix products, local(): lax.dot_general(normed_heads, out_rows, (((1,), (1,)), ((), ())), preferr...  7.86 us
    all_to_all x1, starting transfers between devices, local(): lax.all_to_all(copies, 'tp', 0, 0, tiled=True).reshape(-1, normed.shape[1])  4.93 us
  transfers between devices with their start and end apart: 2, of which 1 were waited for; matrix products, arithmetic and copies ran while one was open for 2% of the time, Pallas kernels for 41%

profile of v9, /device:TPU:224, one launch (start us, length us, event | category | flops | bytes accessed | tf_op | source)
XLA Modules:
  0.0 233.9 jit_solution(16570041115753747243)
XLA Ops:
  6.5 1.4 fusion.7
  7.9 1.4 fusion.9
  9.3 3.4 %broadcast_in_dim.7 = bf16[8,96,4096]{2,1,0:T(8,128)(2,1)} broadcast(bf16[96,4096]{1,0:T(8,128)(2,1)S(1)} %fusion.9), dimensions={1,2} | broadcast | bytes 7077888 | tf_op jit(solution)/shard_map/broadcast_in_dim | solution.py:366
  12.7 0.0 copy-start.3
  12.7 0.0 copy-start.5
  12.7 0.0 copy-start.2
  12.7 0.0 copy-start.1
  12.7 4.9 %all-to-all-start = ((bf16[8,96,4096]{2,1,0:T(8,128)(2,1)}), bf16[8,96,4096]{2,1,0:T(8,128)(2,1)}, u32[]{:S(2)}, u32[]{:S(2)}) async-start(bf16[8,96,4096]{2,1,0:T(8,128)(2,1)} %broadcast_in_dim.7), calls=%async_computation | async-start | bytes 12582912 | tf_op jit(solution)/shard_map/all_to_all | solution.py:367
  17.7 0.0 reduce-scatter.2.cloned.1.call-start
  18.4 0.0 copy-done.3
  18.4 0.3 reduce-window.16
  18.7 0.1 slice.38
  18.8 0.0 copy-done.5
  18.8 0.3 reduce-window.24
  19.1 0.1 slice.40
  19.2 0.1 slice_reduce_fusion.1
  19.3 0.1 slice_reduce_fusion
  19.4 0.1 select_multiply_fusion
  19.5 0.6 slice.44
  20.8 0.6 slice.43
  21.9 0.0 copy-done.2
  21.9 0.1 copy.11
  22.0 0.0 copy-done.1
  22.0 0.8 pad_maximum_fusion.piece_ref
  22.8 0.0 copy-start.4
  22.8 96.1 %shard_map.91 = bf16[8,4,128,1536]{3,2,1,0:T(8,128)(2,1)} custom-call(bf16[128,1536]{1,0:T(8,128)(2,1)} %pad_maximum_fusion.piece_ref), custom_call_target="tpu_custom_call" | custom-call | tf_op jit(solution)/shard_map/pallas_call | solution.py:252
  118.9 0.0 copy-done.4
  119.0 1.2 exponential_select_fusion
  120.2 0.0 all-to-all-done
  120.2 10.9 %fusion.4 = bf16[768,1024]{1,0:T(8,128)(2,1)S(1)} fusion(bf16[768,4096]{1,0:T(8,128)(2,1)} %bitcast, bf16[4096,1536]{1,0:T(8,128)(2,1)} %bitcast.32), kind=kOutput, calls=%fused_computation.10 | convolution fusion | flops 6443237376 | bytes 16252928 | tf_op jit(solution)/shard_map/dot_general | solution.py:372
  131.1 1.4 fusion.11
  132.5 1.4 fusion.24.state_ref
  133.9 0.6 broadcast_in_dim.8.decay_ref
  134.5 36.0 %shard_map.92 = f32[256,512]{1,0:T(8,128)} custom-call(f32[256,512]{1,0:T(8,128)} %fusion.24.state_ref, f32[16,512]{1,0:T(8,128)} %broadcast_in_dim.8.decay_ref), custom_call_target="tpu_custom_call" | custom-call | tf_op jit(solution)/shard_map/pallas_call | solution.py:277
  170.5 2.7 %fusion.42 = (f32[768]{0:T(1024)S(1)}, f32[768,512]{0,1:T(8,128)S(1)}) fusion(f32[768,512]{0,1:T(8,128)S(1)} %fusion.11, f32[256,512]{1,0:T(8,128)} %shard_map.92, f32[768]{0:T(1024)S(1)} %get-tuple-element.5, bf16[768,1024]{1,0:T(8,128)(2,1)S(1)} %fusion.4), kind=kOutput, calls=%fused_computation.63 | convolution fusion | flops 1209138432 | bytes 4070400 | tf_op jit(solution)/shard_map/dot_general | solution.py:341
  173.2 0.0 copy-start.6
  173.3 0.2 multiply_reduce_fusion
  173.5 0.5 copy-done.6
  173.9 7.9 %convolution_convert_fusion = bf16[768,4096]{1,0:T(8,128)(2,1)} fusion(bf16[4096,1536]{1,0:T(8,128)(2,1)} %bitcast.33, f32[768,512]{0,1:T(8,128)S(1)} %get-tuple-element.9, f32[512]{0:T(512)S(1)} %copy-done.6, f32[768]{0:T(1024)S(1)} %add_rsqrt_fusion, f32[768]{0:T(1024)S(1)} %broadcast_multiply_fusion), kind=kOutput, calls=%fused_computation.2 | convolution fusion | flops 3225944064 | bytes 12066816 | tf_op jit(solution)/shard_map/dot_general | solution.py:405
  181.8 0.0 copy-start
  181.8 0.0 reduce-scatter.2.cloned.1.call-update
  181.8 43.0 %reduce-scatter.2.cloned.1.call-done = bf16[96,4096]{1,0:T(8,128)(2,1)} async-done(((bf16[768,4096]{1,0:T(8,128)(2,1)}), bf16[96,4096]{1,0:T(8,128)(2,1)}) %reduce-scatter.2.cloned.1.call-update) | async-done | bytes 786448 | tf_op jit(solution)/shard_map/reduce_scatter | solution.py:408
  224.8 0.0 copy-done
  224.8 2.2 fusion.10
  (8 shorter events, 0.1 us)
Async XLA Ops:
  12.7 5.6 %copy-start.3 = (s32[768]{0:T(1024)S(1)}, s32[768]{0:T(1024)}, u32[]{:S(2)}) copy-start(s32[768]{0:T(1024)} %param.17) | copy-start | bytes 9220
  12.7 6.0 %copy-start.5 = (s32[1,768]{1,0:T(1,128)S(1)}, s32[1,768]{1,0:T(1,128)}, u32[]{:S(2)}) copy-start(s32[1,768]{1,0:T(1,128)} %param.15) | copy-start | bytes 9220
  12.7 9.2 %copy-start.2 = (bf16[512,128]{1,0:T(8,128)(2,1)S(1)}, bf16[512,128]{1,0:T(8,128)(2,1)}, u32[]{:S(2)}) copy-start(bf16[512,128]{1,0:T(8,128)(2,1)} %param.12) | copy-start | bytes 393220
  12.7 9.3 %copy-start.1 = (bf16[128,1024]{1,0:T(8,128)(2,1)S(1)}, bf16[128,1024]{1,0:T(8,128)(2,1)}, u32[]{:S(2)}) copy-start(bf16[128,1024]{1,0:T(8,128)(2,1)} %param.11) | copy-start | bytes 786436
  12.7 107.4 %all-to-all-start = ((bf16[8,96,4096]{2,1,0:T(8,128)(2,1)}), bf16[8,96,4096]{2,1,0:T(8,128)(2,1)}, u32[]{:S(2)}, u32[]{:S(2)}) async-start(bf16[8,96,4096]{2,1,0:T(8,128)(2,1)} %broadcast_in_dim.7), calls=%async_computation | async-start | bytes 12582912 | tf_op jit(solution)/shard_map/all_to_all | solution.py:367
  17.7 207.1 %reduce-scatter.2.cloned.1.call-start = ((), (), s32[]{:S(2)}) async-start(), calls=%async_computation.2 | async-start | bytes 7077888 | tf_op jit(solution)/shard_map/reduce_scatter | solution.py:408
  22.8 96.1 %copy-start.4 = (s32[1,768]{1,0:T(1,128)S(1)}, s32[1,768]{1,0:T(1,128)}, u32[]{:S(2)}) copy-start(s32[1,768]{1,0:T(1,128)} %param.14) | copy-start | bytes 9220
  173.2 0.7 copy-start.6
  181.8 43.0 %copy-start = (bf16[96,4096]{1,0:T(8,128)(2,1)S(1)}, bf16[96,4096]{1,0:T(8,128)(2,1)}, u32[]{:S(2)}) copy-start(bf16[96,4096]{1,0:T(8,128)(2,1)} %param.9) | copy-start | bytes 2359300
Sparse Core Ops, SparseCore 0:
  181.9 42.8 reduce-scatter.1

commit v10 on v9

--- a/solution.py
+++ b/solution.py
@@ -168,7 +168,7 @@
     return steps
 
 
-def gather_kernel(ny, nz, piece_ref, out_ref, local_sem, send_sems, recv_sems):
+def gather_kernel(ny, nz, nt, piece_ref, rows_ref, out_ref, rows_out, local_sem, send_sems, recv_sems):
     yi = lax.axis_index("cy")
     zi = lax.axis_index("cz")
     tp = lax.axis_index("tp")
@@ -181,6 +181,8 @@
         (zi, lax.rem(yi + ny - 1, ny), tp),
         (lax.rem(zi + 1, nz), yi, tp),
         (lax.rem(zi + nz - 1, nz), yi, tp),
+        (zi, yi, lax.rem(tp + 1, nt)),
+        (zi, yi, lax.rem(tp + nt - 1, nt)),
     ]
     for peer in neighbours:
         pl.semaphore_signal(barrier, 1, device_id=peer, device_id_type=MESH_ID)
@@ -188,14 +190,16 @@
 
     own = pltpu.make_async_copy(piece_ref, out_ref.at[zi, yi], local_sem.at[0])
     own.start()
+    own_rows = pltpu.make_async_copy(rows_ref, rows_out.at[tp], local_sem.at[1])
+    own_rows.start()
     sends = []
 
-    def ring(along_y, group_of, first_src):
-        n, me = (ny, yi) if along_y else (nz, zi)
-        return dict(n=n, me=me, along_y=along_y, group_of=group_of, first_src=first_src, steps=ring_steps(n), last={})
+    def ring(along, group_of, first_src):
+        n, me = {"y": (ny, yi), "z": (nz, zi), "t": (nt, tp)}[along]
+        return dict(n=n, me=me, along=along, group_of=group_of, first_src=first_src, steps=ring_steps(n), last={})
 
     def device(r, k):
-        return (zi, k, tp) if r["along_y"] else (k, yi, tp)
+        return {"y": (zi, k, tp), "z": (k, yi, tp), "t": (zi, yi, k)}[r["along"]]
 
     def step(r, t):
         if t > len(r["steps"]):
@@ -233,35 +237,40 @@
                 incoming.wait_recv()
 
     stage([
-        ring(True, lambda k: out_ref.at[zi, k, :, cols[0]], piece_ref.at[:, cols[0]]),
-        ring(False, lambda k: out_ref.at[k, yi, :, cols[1]], piece_ref.at[:, cols[1]]),
+        ring("y", lambda k: out_ref.at[zi, k, :, cols[0]], piece_ref.at[:, cols[0]]),
+        ring("z", lambda k: out_ref.at[k, yi, :, cols[1]], piece_ref.at[:, cols[1]]),
     ])
     own.wait()
     stage([
-        ring(False, lambda k: out_ref.at[k, :, :, cols[0]], out_ref.at[zi, :, :, cols[0]]),
-        ring(True, lambda k: out_ref.at[:, k, :, cols[1]], out_ref.at[:, yi, :, cols[1]]),
+        ring("z", lambda k: out_ref.at[k, :, :, cols[0]], out_ref.at[zi, :, :, cols[0]]),
+        ring("y", lambda k: out_ref.at[:, k, :, cols[1]], out_ref.at[:, yi, :, cols[1]]),
+        ring("t", lambda k: rows_out.at[k], rows_ref),
     ])
+    own_rows.wait()
     for send in sends:
         send.wait_send()
 
 
-def gather_blocks(piece):
-    ny, nz = lax.axis_size("cy"), lax.axis_size("cz")
-    rows, width = piece.shape
-    count = sum(2 if both else 1 for _, both in ring_steps(ny)) * 2 + sum(2 if both else 1 for _, both in ring_steps(nz)) * 2
-    out = pl.pallas_call(
-        functools.partial(gather_kernel, ny, nz),
-        out_shape=jax.ShapeDtypeStruct((nz, ny, rows, width), piece.dtype),
-        in_specs=[pl.BlockSpec(memory_space=pltpu.VMEM)],
-        out_specs=pl.BlockSpec(memory_space=pl.ANY),
+def gather_blocks(piece, rows):
+    ny, nz, nt = lax.axis_size("cy"), lax.axis_size("cz"), lax.axis_size("tp")
+    height, width = piece.shape
+    count = sum(sum(2 if both else 1 for _, both in ring_steps(n)) for n in (ny, nz, nz, ny, nt))
+    out, rows_out = pl.pallas_call(
+        functools.partial(gather_kernel, ny, nz, nt),
+        out_shape=(
+            jax.ShapeDtypeStruct((nz, ny, height, width), piece.dtype),
+            jax.ShapeDtypeStruct((nt,) + rows.shape, rows.dtype),
+        ),
+        in_specs=[pl.BlockSpec(memory_space=pltpu.VMEM)] * 2,
+        out_specs=(pl.BlockSpec(memory_space=pl.ANY), pl.BlockSpec(memory_space=pl.ANY)),
         scratch_shapes=[
-            pltpu.SemaphoreType.DMA((1,)),
+            pltpu.SemaphoreType.DMA((2,)),
             pltpu.SemaphoreType.DMA((count,)),
             pltpu.SemaphoreType.DMA((count,)),
         ],
         compiler_params=pltpu.CompilerParams(collective_id=1, has_side_effects=True),
-    )(piece)
-    return out.reshape(nz * ny * rows, width)
+    )(piece, rows)
+    return out.reshape(nz * ny * height, width), rows_out.reshape(nt * rows.shape[0], rows.shape[1])
 
 
 def carried_in(passing, state):
@@ -362,11 +371,8 @@
     document_begin_flags,
 ):
     normed = rms_rows(tokens, norm_gain)
-    group = lax.axis_size("tp")
-    copies = jnp.broadcast_to(normed[None], (group,) + normed.shape)
-    every_row_list = lax.all_to_all(copies, "tp", 0, 0, tiled=True).reshape(-1, normed.shape[1])
     width = w_qkv.shape[1]
-    both = gather_blocks(jnp.concatenate([w_qkv, w_out.T], axis=1))
+    both, every_row_list = gather_blocks(jnp.concatenate([w_qkv, w_out.T], axis=1), normed)
     parameter_collection = both[:, :width]
     out_rows = both[:, width:]
     rows_combined = jnp.dot(

time: 237 us -> 242 us (1.021)
  Pallas kernels: 132 us -> 139 us
  starting transfers between devices: 4.97 us -> 0.01 us
  matrix products: 24.3 us -> 28.2 us
  other arithmetic: 7.9 us -> 10.8 us
    all_to_all x1 -> x0, starting transfers between devices: 4.93 us -> none  [local(): lax.all_to_all(copies, 'tp', 0, 0, tiled=True).reshape(-1, normed.shape[1])]
    pallas_call x1, Pallas kernels: 36 us -> 40.9 us  [carried_in(): pl.pallas_call(functools.partial(scan_kernel, ny, nz, zshifts), out_shape...]
    broadcast_in_dim x1 -> x0, local copies, waits for them, and re-layouts: 3.38 us -> none  [local(): copies = jnp.broadcast_to(normed[None], (group,) + normed.shape)]
  transfers between devices with their start and end apart: 2 -> 1, of which waited for: 1 -> 1; matrix products, arithmetic and copies ran while one was open for 2% -> 0% of each run, Pallas kernels for 41% -> 0%
where the time goes in v10:
time: 242 us; the launch traced here: 239 us
  Pallas kernels  139 us (57%)
  waiting for transfers between devices  42.1 us (17%)
  matrix products  28.2 us (12%)
  between operations  15.5 us (6%)
  other arithmetic  10.8 us (4%)
  local copies, waits for them, and re-layouts  3.79 us (2%)
    pallas_call x1, Pallas kernels, gather_blocks(): pl.pallas_call(functools.partial(gather_kernel, ny, nz, nt), out_shape=(j...  97.6 us
    reduce_scatter x1, waiting for transfers between devices, local(): lax.psum_scatter(projected.astype(jnp.bfloat16), 'tp', scatter_dimension=...  42.1 us
    pallas_call x1, Pallas kernels, carried_in(): pl.pallas_call(functools.partial(scan_kernel, ny, nz, zshifts), out_shape...  40.9 us
    dot_general x1, matrix products, local(): jnp.dot(every_row_list, parameter_collection, preferred_element_type=jnp....  12.1 us
    dot_general x1, matrix products, local(): lax.dot_general(normed_heads, out_rows, (((1,), (1,)), ((), ())), preferr...  7.85 us
  transfers between devices with their start and end apart: 1, of which 1 were waited for; matrix products, arithmetic and copies ran while one was open for 0% of the time, Pallas kernels for 0%

profile of v10, /device:TPU:224, one launch (start us, length us, event | category | flops | bytes accessed | tf_op | source)
XLA Modules:
  0.0 239.0 jit_solution(687241341258437044)
XLA Ops:
  6.5 0.0 copy-start
  6.5 0.0 copy-start.1
  6.5 0.0 reduce-scatter.2.cloned.1.call-start
  6.5 1.1 copy.11
  7.6 1.4 fusion.7
  9.0 0.7 multiply_reduce_fusion.1
  9.7 1.0 reduce-window.16
  10.7 0.1 slice.38
  10.8 0.1 slice_reduce_fusion.1
  11.6 0.7 negate_reduce_fusion
  12.3 0.3 reduce-window.24
  12.6 0.1 slice.40
  12.7 0.1 slice_reduce_fusion
  12.8 0.1 select_multiply_fusion
  12.9 0.6 slice.44
  13.5 0.7 slice.43
  15.5 1.3 exponential_select_fusion
  16.9 1.7 pad_maximum_fusion.piece_ref
  18.6 0.0 copy-done
  18.6 0.0 copy-done.1
  18.6 1.1 fusion.9.rows_ref
  19.7 97.6 %shard_map.91 = (bf16[8,4,128,1536]{3,2,1,0:T(8,128)(2,1)}, bf16[8,96,4096]{2,1,0:T(8,128)(2,1)}) custom-call(bf16[128,1536]{1,0:T(8,128)(2,1)} %pad_maximum_fusion.piece_ref, bf16[96,4096]{1,0:T(8,128)(2,1)} %fusion.9.rows_ref), custom_call_target="tpu_custom_call" | custom-call | tf_op jit(solution)/shard_map/pallas_call | solution.py:258
  117.4 12.1 %fusion.4 = bf16[768,1024]{1,0:T(8,128)(2,1)} fusion(bf16[768,4096]{1,0:T(8,128)(2,1)} %bitcast.36, bf16[4096,1536]{1,0:T(8,128)(2,1)} %bitcast.34), kind=kOutput, calls=%fused_computation.10 | convolution fusion | flops 6443237376 | bytes 16252928 | tf_op jit(solution)/shard_map/dot_general | solution.py:378
  129.5 2.8 %fusion.11 = f32[768,512]{0,1:T(8,128)S(1)} fusion(f32[768]{0:T(1024)S(1)} %multiply_reduce_fusion.1, f32[768]{0:T(1024)S(1)} %get-tuple-element.11, s32[768]{0:T(1024)S(1)} %get-tuple-element.10, bf16[768,1024]{1,0:T(8,128)(2,1)} %fusion.4), kind=kOutput, calls=%fused_computation.18 | convolution fusion | flops 911867904 | bytes 3166208 | tf_op jit(solution)/shard_map/dot_general | solution.py:335
  132.3 2.6 %fusion.24.state_ref = f32[256,512]{1,0:T(8,128)} fusion(bf16[768,1024]{1,0:T(8,128)(2,1)} %fusion.4, f32[768]{0:T(1024)S(1)} %exponential_select_fusion), kind=kOutput, calls=%fused_computation.32 | convolution fusion | flops 201916416 | bytes 1707008 | tf_op jit(solution)/shard_map/dot_general | solution.py:340
  134.9 0.6 broadcast_in_dim.5.decay_ref
  135.5 40.9 %shard_map.92 = f32[256,512]{1,0:T(8,128)} custom-call(f32[256,512]{1,0:T(8,128)} %fusion.24.state_ref, f32[16,512]{1,0:T(8,128)} %broadcast_in_dim.5.decay_ref), custom_call_target="tpu_custom_call" | custom-call | tf_op jit(solution)/shard_map/pallas_call | solution.py:286
  176.4 2.9 %fusion.42 = (f32[768]{0:T(1024)S(1)}, f32[768,512]{0,1:T(8,128)S(1)}) fusion(f32[768,512]{0,1:T(8,128)S(1)} %fusion.11, f32[256,512]{1,0:T(8,128)} %shard_map.92, f32[768]{0:T(1024)S(1)} %get-tuple-element.9, bf16[768,1024]{1,0:T(8,128)(2,1)} %fusion.4), kind=kOutput, calls=%fused_computation.63 | convolution fusion | flops 1209138432 | bytes 4069376 | tf_op jit(solution)/shard_map/dot_general | solution.py:350
  179.3 0.0 copy-start.2
  179.4 0.2 multiply_reduce_fusion
  179.6 0.5 copy-done.2
  180.0 7.8 %convolution_convert_fusion = bf16[768,4096]{1,0:T(8,128)(2,1)} fusion(bf16[4096,1536]{1,0:T(8,128)(2,1)} %bitcast.35, f32[768,512]{0,1:T(8,128)S(1)} %get-tuple-element.13, f32[512]{0:T(512)S(1)} %copy-done.2, f32[768]{0:T(1024)S(1)} %add_rsqrt_fusion, f32[768]{0:T(1024)S(1)} %broadcast_multiply_fusion), kind=kOutput, calls=%fused_computation.2 | convolution fusion | flops 3225944064 | bytes 12066816 | tf_op jit(solution)/shard_map/dot_general | solution.py:411
  187.9 0.0 reduce-scatter.2.cloned.1.call-update
  187.9 42.1 %reduce-scatter.2.cloned.1.call-done = bf16[96,4096]{1,0:T(8,128)(2,1)} async-done(((bf16[768,4096]{1,0:T(8,128)(2,1)}), bf16[96,4096]{1,0:T(8,128)(2,1)}) %reduce-scatter.2.cloned.1.call-update) | async-done | bytes 786448 | tf_op jit(solution)/shard_map/reduce_scatter | solution.py:414
  230.0 2.2 fusion.10
  (6 shorter events, 0.1 us)
Async XLA Ops:
  6.5 12.1 %copy-start = (bf16[96,4096]{1,0:T(8,128)(2,1)S(1)}, bf16[96,4096]{1,0:T(8,128)(2,1)}, u32[]{:S(2)}) copy-start(bf16[96,4096]{1,0:T(8,128)(2,1)} %param.9) | copy-start | bytes 2359300
  6.5 12.1 %copy-start.1 = (f32[4096]{0:T(1024)S(1)}, f32[4096]{0:T(1024)}, u32[]{:S(2)}) copy-start(f32[4096]{0:T(1024)} %param.10) | copy-start | bytes 49156
  6.5 223.4 %reduce-scatter.2.cloned.1.call-start = ((), (), s32[]{:S(2)}) async-start(), calls=%async_computation.1 | async-start | bytes 7077888 | tf_op jit(solution)/shard_map/reduce_scatter | solution.py:414
  179.3 0.7 copy-start.2
Sparse Core Ops, SparseCore 0:
  188.0 41.9 reduce-scatter.1

commit v11 on v10

--- a/solution.py
+++ b/solution.py
@@ -271,6 +271,68 @@
         compiler_params=pltpu.CompilerParams(collective_id=1, has_side_effects=True),
     )(piece, rows)
     return out.reshape(nz * ny * height, width), rows_out.reshape(nt * rows.shape[0], rows.shape[1])
+
+
+def scatter_kernel(nt, part_ref, out_ref, send_buf, recv_buf, send_sems, recv_sems):
+    tp = lax.axis_index("tp")
+    rows = out_ref.shape[0]
+    half = out_ref.shape[1] // 2
+
+    barrier = pltpu.get_barrier_semaphore()
+    for peer in (lax.rem(tp + 1, nt), lax.rem(tp + nt - 1, nt)):
+        pl.semaphore_signal(barrier, 1, device_id=(lax.axis_index("cz"), lax.axis_index("cy"), peer), device_id_type=MESH_ID)
+    pl.semaphore_wait(barrier, 2)
+
+    def own(chunk, side):
+        start = pl.multiple_of(chunk * rows, 16)
+        return part_ref[pl.ds(start, rows), pl.ds(side * half, half)].astype(jnp.float32)
+
+    def copy(side, step, peer):
+        slot = side * nt + step
+        return pltpu.make_async_remote_copy(
+            src_ref=send_buf.at[slot], dst_ref=recv_buf.at[slot], send_sem=send_sems.at[slot],
+            recv_sem=recv_sems.at[slot],
+            device_id=(lax.axis_index("cz"), lax.axis_index("cy"), peer), device_id_type=MESH_ID,
+        )
+
+    sides = ((0, 1), (1, -1))
+    for step in range(1, nt):
+        for side, sign in sides:
+            chunk = lax.rem(tp + nt * nt - sign * step, nt)
+            total = own(chunk, side)
+            if step > 1:
+                copy(side, step - 1, lax.rem(tp + nt - sign, nt)).wait_recv()
+                total = total + recv_buf[side * nt + step - 1].astype(jnp.float32)
+            send_buf[side * nt + step] = total.astype(jnp.bfloat16)
+            copy(side, step, lax.rem(tp + nt + sign, nt)).start()
+    for side, sign in sides:
+        copy(side, nt - 1, lax.rem(tp + nt - sign, nt)).wait_recv()
+        total = own(tp, side) + recv_buf[side * nt + nt - 1].astype(jnp.float32)
+        out_ref[:, side * half : (side + 1) * half] = total.astype(out_ref.dtype)
+    for step in range(1, nt):
+        for side, sign in sides:
+            copy(side, step, lax.rem(tp + nt + sign, nt)).wait_send()
+
+
+def scatter_rows(part):
+    nt = lax.axis_size("tp")
+    rows = part.shape[0] // nt
+    width = part.shape[1]
+    return pl.pallas_call(
+        functools.partial(scatter_kernel, nt),
+        out_shape=jax.ShapeDtypeStruct((rows, width), part.dtype),
+        in_specs=[pl.BlockSpec(memory_space=pltpu.VMEM)],
+        out_specs=pl.BlockSpec(memory_space=pltpu.VMEM),
+        scratch_shapes=[
+            pltpu.VMEM((2 * nt, rows, width // 2), jnp.bfloat16),
+            pltpu.VMEM((2 * nt, rows, width // 2), jnp.bfloat16),
+            pltpu.SemaphoreType.DMA((2 * nt,)),
+            pltpu.SemaphoreType.DMA((2 * nt,)),
+        ],
+        compiler_params=pltpu.CompilerParams(
+            collective_id=2, has_side_effects=True, vmem_limit_bytes=48 * 1024 * 1024
+        ),
+    )(part)
 
 
 def carried_in(passing, state):
@@ -411,12 +473,7 @@
     projected = lax.dot_general(
         normed_heads, out_rows, (((1,), (1,)), ((), ())), preferred_element_type=jnp.float32
     )
-    summed = lax.psum_scatter(
-        projected.astype(jnp.bfloat16),
-        "tp",
-        scatter_dimension=0,
-        tiled=True,
-    ).astype(jnp.float32)
+    summed = scatter_rows(projected.astype(jnp.bfloat16)).astype(jnp.float32)
     return (tokens.astype(jnp.float32) + summed).astype(jnp.bfloat16)
 
 

time: 242 us -> 221 us (0.913)
  waiting for transfers between devices: 42.1 us -> 0 us
  Pallas kernels: 139 us -> 179 us
  between operations: 15.5 us -> 2.13 us
  other arithmetic: 10.8 us -> 6.43 us
    reduce_scatter x1 -> x0, waiting for transfers between devices: 42.1 us -> none  [local(): lax.psum_scatter(projected.astype(jnp.bfloat16), 'tp', scatter_dimension=...]
    pallas_call x0 -> x1, Pallas kernels: none -> 40.3 us  [scatter_rows(): pl.pallas_call(functools.partial(scatter_kernel, nt), out_shape=jax.Shape...]
  transfers between devices with their start and end apart: 1 -> 0, of which waited for: 1 -> 0; matrix products, arithmetic and copies ran while one was open for 0% -> 0% of each run, Pallas kernels for 0% -> 0%
where the time goes in v11:
time: 221 us; the launch traced here: 220 us
  Pallas kernels  179 us (81%)
  matrix products  28.2 us (13%)
  other arithmetic  6.43 us (3%)
  local copies, waits for them, and re-layouts  3.81 us (2%)
    pallas_call x1, Pallas kernels, gather_blocks(): pl.pallas_call(functools.partial(gather_kernel, ny, nz, nt), out_shape=(j...  97.6 us
    pallas_call x1, Pallas kernels, carried_in(): pl.pallas_call(functools.partial(scan_kernel, ny, nz, zshifts), out_shape...  41.1 us
    pallas_call x1, Pallas kernels, scatter_rows(): pl.pallas_call(functools.partial(scatter_kernel, nt), out_shape=jax.Shape...  40.3 us
    dot_general x1, matrix products, local(): jnp.dot(every_row_list, parameter_collection, preferred_element_type=jnp....  12.1 us
    dot_general x1, matrix products, local(): lax.dot_general(normed_heads, out_rows, (((1,), (1,)), ((), ())), preferr...  7.86 us

profile of v11, /device:TPU:224, one launch (start us, length us, event | category | flops | bytes accessed | tf_op | source)
XLA Modules:
  0.0 219.6 jit_solution(17594843739236962786)
XLA Ops:
  0.0 0.0 copy-start
  0.0 0.0 copy-start.1
  0.0 1.1 copy.11
  1.1 1.7 pad_maximum_fusion.piece_ref
  2.8 0.0 copy-done
  2.8 0.3 fusion.7
  3.1 0.0 copy-start.3
  3.1 0.0 copy-start.2
  3.1 0.0 copy-start.4
  3.1 0.0 copy-done.1
  3.1 1.1 fusion.9.rows_ref
  4.3 97.6 %shard_map.91 = (bf16[8,4,128,1536]{3,2,1,0:T(8,128)(2,1)}, bf16[8,96,4096]{2,1,0:T(8,128)(2,1)}) custom-call(bf16[128,1536]{1,0:T(8,128)(2,1)} %pad_maximum_fusion.piece_ref, bf16[96,4096]{1,0:T(8,128)(2,1)} %fusion.9.rows_ref), custom_call_target="tpu_custom_call" | custom-call | tf_op jit(solution)/shard_map/pallas_call | solution.py:258
  101.9 0.0 copy-done.3
  102.0 0.0 copy-done.2
  102.0 0.3 reduce-window.16
  102.2 0.1 slice.38
  102.3 0.1 slice_reduce_fusion.1
  103.1 0.0 copy-done.4
  103.2 0.3 reduce-window.24
  103.5 0.1 slice.40
  103.6 0.1 slice_reduce_fusion
  103.7 0.1 select_multiply_fusion
  103.7 12.1 %fusion.4 = bf16[768,1024]{1,0:T(8,128)(2,1)} fusion(bf16[768,4096]{1,0:T(8,128)(2,1)} %bitcast.36, bf16[4096,1536]{1,0:T(8,128)(2,1)} %bitcast.34), kind=kOutput, calls=%fused_computation.10 | convolution fusion | flops 6443237376 | bytes 16252928 | tf_op jit(solution)/shard_map/dot_general | solution.py:440
  115.8 2.8 %fusion.11 = f32[768,512]{0,1:T(8,128)S(1)} fusion(f32[768]{0:T(1024)S(1)} %multiply_reduce_fusion.1, f32[768]{0:T(1024)S(1)} %get-tuple-element.11, s32[768]{0:T(1024)S(1)} %get-tuple-element.10, bf16[768,1024]{1,0:T(8,128)(2,1)} %fusion.4), kind=kOutput, calls=%fused_computation.18 | convolution fusion | flops 911867904 | bytes 3166208 | tf_op jit(solution)/shard_map/dot_general | solution.py:397
  118.6 0.6 slice.44
  119.2 0.6 slice.43
  119.9 1.3 exponential_select_fusion
  121.2 2.6 %fusion.24.state_ref = f32[256,512]{1,0:T(8,128)} fusion(bf16[768,1024]{1,0:T(8,128)(2,1)} %fusion.4, f32[768]{0:T(1024)S(1)} %exponential_select_fusion), kind=kOutput, calls=%fused_computation.32 | convolution fusion | flops 201916416 | bytes 1707008 | tf_op jit(solution)/shard_map/dot_general | solution.py:402
  125.1 0.6 broadcast_in_dim.5.decay_ref
  125.7 41.1 %shard_map.92 = f32[256,512]{1,0:T(8,128)} custom-call(f32[256,512]{1,0:T(8,128)} %fusion.24.state_ref, f32[16,512]{1,0:T(8,128)} %broadcast_in_dim.5.decay_ref), custom_call_target="tpu_custom_call" | custom-call | tf_op jit(solution)/shard_map/pallas_call | solution.py:348
  166.8 2.9 %fusion.42 = (f32[768]{0:T(1024)S(1)}, f32[768,512]{0,1:T(8,128)S(1)}) fusion(f32[768,512]{0,1:T(8,128)S(1)} %fusion.11, f32[256,512]{1,0:T(8,128)} %shard_map.92, f32[768]{0:T(1024)S(1)} %get-tuple-element.9, bf16[768,1024]{1,0:T(8,128)(2,1)} %fusion.4), kind=kOutput, calls=%fused_computation.63 | convolution fusion | flops 1209138432 | bytes 4069376 | tf_op jit(solution)/shard_map/dot_general | solution.py:412
  169.7 0.0 copy-start.5
  169.8 0.2 multiply_reduce_fusion
  170.0 0.5 copy-done.5
  170.4 7.9 %convolution_convert_fusion.part_ref = bf16[768,4096]{1,0:T(8,128)(2,1)} fusion(bf16[4096,1536]{1,0:T(8,128)(2,1)} %bitcast.35, f32[768,512]{0,1:T(8,128)S(1)} %get-tuple-element.13, f32[512]{0:T(512)S(1)} %copy-done.5, f32[768]{0:T(1024)S(1)} %add_rsqrt_fusion, f32[768]{0:T(1024)S(1)} %broadcast_multiply_fusion), kind=kOutput, calls=%fused_computation.2 | convolution fusion | flops 3225944064 | bytes 12066816 | tf_op jit(solution)/shard_map/dot_general | solution.py:473
  178.3 40.3 %shard_map.93 = bf16[96,4096]{1,0:T(8,128)(2,1)S(1)} custom-call(bf16[768,4096]{1,0:T(8,128)(2,1)} %convolution_convert_fusion.part_ref), custom_call_target="tpu_custom_call" | custom-call | tf_op jit(solution)/shard_map/pallas_call | solution.py:321
  218.6 1.1 fusion.10
  (8 shorter events, 0.1 us)
Async XLA Ops:
  0.0 2.8 %copy-start = (bf16[96,4096]{1,0:T(8,128)(2,1)S(1)}, bf16[96,4096]{1,0:T(8,128)(2,1)}, u32[]{:S(2)}) copy-start(bf16[96,4096]{1,0:T(8,128)(2,1)} %param.9) | copy-start | bytes 2359300
  0.0 3.1 %copy-start.1 = (f32[4096]{0:T(1024)S(1)}, f32[4096]{0:T(1024)}, u32[]{:S(2)}) copy-start(f32[4096]{0:T(1024)} %param.10) | copy-start | bytes 49156
  3.1 98.9 %copy-start.3 = (s32[1,768]{1,0:T(1,128)S(1)}, s32[1,768]{1,0:T(1,128)}, u32[]{:S(2)}) copy-start(s32[1,768]{1,0:T(1,128)} %param.14) | copy-start | bytes 9220
  3.1 98.9 %copy-start.2 = (s32[768]{0:T(1024)S(1)}, s32[768]{0:T(1024)}, u32[]{:S(2)}) copy-start(s32[768]{0:T(1024)} %param.17) | copy-start | bytes 9220
  3.1 100.0 %copy-start.4 = (s32[1,768]{1,0:T(1,128)S(1)}, s32[1,768]{1,0:T(1,128)}, u32[]{:S(2)}) copy-start(s32[1,768]{1,0:T(1,128)} %param.15) | copy-start | bytes 9220
  169.7 0.7 copy-start.5

commit v12 on v11

--- a/solution.py
+++ b/solution.py
@@ -273,7 +273,7 @@
     return out.reshape(nz * ny * height, width), rows_out.reshape(nt * rows.shape[0], rows.shape[1])
 
 
-def scatter_kernel(nt, part_ref, out_ref, send_buf, recv_buf, send_sems, recv_sems):
+def scatter_kernel(nt, heads_ref, weight_ref, out_ref, send_buf, recv_buf, send_sems, recv_sems):
     tp = lax.axis_index("tp")
     rows = out_ref.shape[0]
     half = out_ref.shape[1] // 2
@@ -285,7 +285,13 @@
 
     def own(chunk, side):
         start = pl.multiple_of(chunk * rows, 16)
-        return part_ref[pl.ds(start, rows), pl.ds(side * half, half)].astype(jnp.float32)
+        part = lax.dot_general(
+            heads_ref[pl.ds(start, rows), :],
+            weight_ref[side * half : (side + 1) * half, :],
+            (((1,), (1,)), ((), ())),
+            preferred_element_type=jnp.float32,
+        )
+        return part.astype(jnp.bfloat16).astype(jnp.float32)
 
     def copy(side, step, peer):
         slot = side * nt + step
@@ -314,14 +320,14 @@
             copy(side, step, lax.rem(tp + nt + sign, nt)).wait_send()
 
 
-def scatter_rows(part):
+def scatter_rows(heads, weight):
     nt = lax.axis_size("tp")
-    rows = part.shape[0] // nt
-    width = part.shape[1]
+    rows = heads.shape[0] // nt
+    width = weight.shape[0]
     return pl.pallas_call(
         functools.partial(scatter_kernel, nt),
-        out_shape=jax.ShapeDtypeStruct((rows, width), part.dtype),
-        in_specs=[pl.BlockSpec(memory_space=pltpu.VMEM)],
+        out_shape=jax.ShapeDtypeStruct((rows, width), jnp.bfloat16),
+        in_specs=[pl.BlockSpec(memory_space=pltpu.VMEM)] * 2,
         out_specs=pl.BlockSpec(memory_space=pltpu.VMEM),
         scratch_shapes=[
             pltpu.VMEM((2 * nt, rows, width // 2), jnp.bfloat16),
@@ -332,7 +338,7 @@
         compiler_params=pltpu.CompilerParams(
             collective_id=2, has_side_effects=True, vmem_limit_bytes=48 * 1024 * 1024
         ),
-    )(part)
+    )(heads, weight)
 
 
 def carried_in(passing, state):
@@ -470,10 +476,7 @@
         incoming[attention_slot_number],
     )
     normed_heads = head_norm(head_out, head_gain)
-    projected = lax.dot_general(
-        normed_heads, out_rows, (((1,), (1,)), ((), ())), preferred_element_type=jnp.float32
-    )
-    summed = scatter_rows(projected.astype(jnp.bfloat16)).astype(jnp.float32)
+    summed = scatter_rows(normed_heads, out_rows).astype(jnp.float32)
     return (tokens.astype(jnp.float32) + summed).astype(jnp.bfloat16)
 
 

time: 221 us -> 219 us (level)
  matrix products: 28.2 us -> 20.2 us
  Pallas kernels: 179 us -> 182 us
  other arithmetic: 6.43 us -> 8.99 us
  local copies, waits for them, and re-layouts: 3.81 us -> 6.05 us
    dot_general x1 -> x0, matrix products: 7.86 us -> none  [local(): lax.dot_general(normed_heads, out_rows, (((1,), (1,)), ((), ())), preferr...]
    pallas_call x1, Pallas kernels: 40.3 us -> 43 us  [scatter_rows(): pl.pallas_call(functools.partial(scatter_kernel, nt), out_shape=jax.Shape...]
    slice x1 -> x2, local copies, waits for them, and re-layouts: 0.07 us -> 2.53 us  [the longest x1 2.46 us: local(): out_rows = both[:, width:]]
where the time goes in v12:
time: 219 us
  Pallas kernels  182 us (83%)
  matrix products  20.2 us (9%)
  other arithmetic  8.99 us (4%)
  local copies, waits for them, and re-layouts  6.05 us (3%)
    pallas_call x1, Pallas kernels, gather_blocks(): pl.pallas_call(functools.partial(gather_kernel, ny, nz, nt), out_shape=(j...  97.6 us
    pallas_call x1, Pallas kernels, scatter_rows(): pl.pallas_call(functools.partial(scatter_kernel, nt), out_shape=jax.Shape...  43 us
    pallas_call x1, Pallas kernels, carried_in(): pl.pallas_call(functools.partial(scan_kernel, ny, nz, zshifts), out_shape...  41.1 us
    dot_general x1, matrix products, local(): jnp.dot(every_row_list, parameter_collection, preferred_element_type=jnp....  12.1 us

profile of v12, /device:TPU:224, one launch (start us, length us, event | category | flops | bytes accessed | tf_op | source)
XLA Modules:
  0.0 219.0 jit_solution(5681943916346173708)
XLA Ops:
  0.0 0.0 copy-start
  0.0 0.0 copy-start.1
  0.0 0.8 multiply_reduce_fusion.1
  0.8 1.0 reduce-window.16
  1.7 0.1 slice.38
  1.8 0.1 slice_reduce_fusion.1
  2.6 0.7 negate_reduce_fusion
  3.3 0.3 reduce-window.24
  3.6 0.1 slice.40
  3.7 0.1 slice_reduce_fusion
  3.8 0.1 select_multiply_fusion
  3.9 1.0 copy.13
  4.9 1.7 pad_maximum_fusion.piece_ref
  6.7 0.0 copy-done
  6.7 0.3 fusion.6
  6.9 0.0 copy-done.1
  6.9 1.1 fusion.8.rows_ref
  8.1 97.6 %shard_map.91 = (bf16[8,4,128,1536]{3,2,1,0:T(8,128)(2,1)}, bf16[8,96,4096]{2,1,0:T(8,128)(2,1)}) custom-call(bf16[128,1536]{1,0:T(8,128)(2,1)} %pad_maximum_fusion.piece_ref, bf16[96,4096]{1,0:T(8,128)(2,1)} %fusion.8.rows_ref), custom_call_target="tpu_custom_call" | custom-call | tf_op jit(solution)/shard_map/pallas_call | solution.py:258
  105.7 12.1 %fusion.3 = bf16[768,1024]{1,0:T(8,128)(2,1)} fusion(bf16[768,4096]{1,0:T(8,128)(2,1)} %bitcast.36, bf16[4096,1536]{1,0:T(8,128)(2,1)} %bitcast.32), kind=kOutput, calls=%fused_computation.8 | convolution fusion | flops 6443237376 | bytes 16252928 | tf_op jit(solution)/shard_map/dot_general | solution.py:446
  117.8 2.7 %fusion.10 = f32[768,512]{1,0:T(8,128)S(1)} fusion(f32[768]{0:T(1024)S(1)} %multiply_reduce_fusion.1, f32[768]{0:T(1024)S(1)} %get-tuple-element.11, s32[768]{0:T(1024)S(1)} %get-tuple-element.10, bf16[768,1024]{1,0:T(8,128)(2,1)} %fusion.3), kind=kOutput, calls=%fused_computation.16 | convolution fusion | flops 911867904 | bytes 3166208 | tf_op jit(solution)/shard_map/dot_general | solution.py:403
  120.6 0.6 slice.44
  121.2 0.6 slice.43
  121.8 1.3 exponential_select_fusion
  123.1 2.6 %fusion.20.state_ref = f32[256,512]{1,0:T(8,128)} fusion(bf16[768,1024]{1,0:T(8,128)(2,1)} %fusion.3, f32[768]{0:T(1024)S(1)} %exponential_select_fusion), kind=kOutput, calls=%fused_computation.27 | convolution fusion | flops 201916416 | bytes 1707008 | tf_op jit(solution)/shard_map/dot_general | solution.py:408
  127.1 0.6 broadcast_in_dim.5.decay_ref
  127.7 41.1 %shard_map.92 = f32[256,512]{1,0:T(8,128)} custom-call(f32[256,512]{1,0:T(8,128)} %fusion.20.state_ref, f32[16,512]{1,0:T(8,128)} %broadcast_in_dim.5.decay_ref), custom_call_target="tpu_custom_call" | custom-call | tf_op jit(solution)/shard_map/pallas_call | solution.py:354
  168.7 2.7 %fusion.38 = (f32[768]{0:T(1024)S(1)}, f32[768,512]{1,0:T(8,128)S(1)}) fusion(f32[768,512]{1,0:T(8,128)S(1)} %fusion.10, f32[256,512]{1,0:T(8,128)} %shard_map.92, f32[768]{0:T(1024)S(1)} %get-tuple-element.9, bf16[768,1024]{1,0:T(8,128)(2,1)} %fusion.3), kind=kOutput, calls=%fused_computation.58 | convolution fusion | flops 1209138432 | bytes 4069376 | tf_op jit(solution)/shard_map/dot_general | solution.py:418
  171.5 0.0 copy-start.2
  171.5 0.3 multiply_reduce_fusion
  171.8 0.3 copy-done.2
  172.2 0.3 multiply_convert_fusion.1.heads_ref
  172.4 2.5 %slice.50.weight_ref = bf16[4096,512]{1,0:T(8,128)(2,1)S(1)} slice(bf16[4096,1536]{1,0:T(8,128)(2,1)} %bitcast.33), slice={[0:4096], [1024:1536]} | slice | bytes 8388608 | tf_op jit(solution)/shard_map/slice | solution.py:445
  174.9 43.0 %shard_map.93 = bf16[96,4096]{1,0:T(8,128)(2,1)S(1)} custom-call(bf16[768,512]{1,0:T(8,128)(2,1)S(1)} %multiply_convert_fusion.1.heads_ref, bf16[4096,512]{1,0:T(8,128)(2,1)S(1)} %slice.50.weight_ref), custom_call_target="tpu_custom_call" | custom-call | tf_op jit(solution)/shard_map/pallas_call | solution.py:327
  217.9 1.1 fusion.9
  (6 shorter events, 0.1 us)
Async XLA Ops:
  0.0 6.7 %copy-start = (bf16[96,4096]{1,0:T(8,128)(2,1)S(1)}, bf16[96,4096]{1,0:T(8,128)(2,1)}, u32[]{:S(2)}) copy-start(bf16[96,4096]{1,0:T(8,128)(2,1)} %param.9) | copy-start | bytes 2359300
  0.0 6.9 %copy-start.1 = (f32[4096]{0:T(1024)S(1)}, f32[4096]{0:T(1024)}, u32[]{:S(2)}) copy-start(f32[4096]{0:T(1024)} %param.10) | copy-start | bytes 49156
  171.5 0.7 copy-start.2

commit v13 on v12

--- a/solution.py
+++ b/solution.py
@@ -281,7 +281,6 @@
     barrier = pltpu.get_barrier_semaphore()
     for peer in (lax.rem(tp + 1, nt), lax.rem(tp + nt - 1, nt)):
         pl.semaphore_signal(barrier, 1, device_id=(lax.axis_index("cz"), lax.axis_index("cy"), peer), device_id_type=MESH_ID)
-    pl.semaphore_wait(barrier, 2)
 
     def own(chunk, side):
         start = pl.multiple_of(chunk * rows, 16)
@@ -302,18 +301,21 @@
         )
 
     sides = ((0, 1), (1, -1))
+    first = [own(lax.rem(tp + nt * nt - sign, nt), side) for side, sign in sides]
+    pl.semaphore_wait(barrier, 2)
     for step in range(1, nt):
         for side, sign in sides:
             chunk = lax.rem(tp + nt * nt - sign * step, nt)
-            total = own(chunk, side)
+            total = first[side] if step == 1 else own(chunk, side)
             if step > 1:
                 copy(side, step - 1, lax.rem(tp + nt - sign, nt)).wait_recv()
                 total = total + recv_buf[side * nt + step - 1].astype(jnp.float32)
             send_buf[side * nt + step] = total.astype(jnp.bfloat16)
             copy(side, step, lax.rem(tp + nt + sign, nt)).start()
+    last = [own(tp, side) for side, _ in sides]
     for side, sign in sides:
         copy(side, nt - 1, lax.rem(tp + nt - sign, nt)).wait_recv()
-        total = own(tp, side) + recv_buf[side * nt + nt - 1].astype(jnp.float32)
+        total = last[side] + recv_buf[side * nt + nt - 1].astype(jnp.float32)
         out_ref[:, side * half : (side + 1) * half] = total.astype(out_ref.dtype)
     for step in range(1, nt):
         for side, sign in sides:

time: 219 us -> 217 us (level)
  no operation moved by 1% of the time
where the time goes in v13:
time: 217 us
  Pallas kernels  180 us (83%)
  matrix products  20.2 us (9%)
  other arithmetic  8.99 us (4%)
  local copies, waits for them, and re-layouts  6.05 us (3%)
    pallas_call x1, Pallas kernels, gather_blocks(): pl.pallas_call(functools.partial(gather_kernel, ny, nz, nt), out_shape=(j...  97.6 us
    pallas_call x1, Pallas kernels, carried_in(): pl.pallas_call(functools.partial(scan_kernel, ny, nz, zshifts), out_shape...  41.1 us
    pallas_call x1, Pallas kernels, scatter_rows(): pl.pallas_call(functools.partial(scatter_kernel, nt), out_shape=jax.Shape...  40.9 us
    dot_general x1, matrix products, local(): jnp.dot(every_row_list, parameter_collection, preferred_element_type=jnp....  12.1 us

profile of v13, /device:TPU:224, one launch (start us, length us, event | category | flops | bytes accessed | tf_op | source)
XLA Modules:
  0.0 216.9 jit_solution(6210190446869832260)
XLA Ops:
  0.0 0.0 copy-start
  0.0 0.0 copy-start.1
  0.0 0.8 multiply_reduce_fusion.1
  0.8 1.0 reduce-window.16
  1.7 0.1 slice.38
  1.8 0.1 slice_reduce_fusion.1
  2.6 0.7 negate_reduce_fusion
  3.3 0.3 reduce-window.24
  3.6 0.1 slice.40
  3.7 0.1 slice_reduce_fusion
  3.8 0.1 select_multiply_fusion
  3.9 1.0 copy.13
  4.9 1.7 pad_maximum_fusion.piece_ref
  6.7 0.0 copy-done
  6.7 0.3 fusion.6
  6.9 0.0 copy-done.1
  6.9 1.1 fusion.8.rows_ref
  8.1 97.6 %shard_map.91 = (bf16[8,4,128,1536]{3,2,1,0:T(8,128)(2,1)}, bf16[8,96,4096]{2,1,0:T(8,128)(2,1)}) custom-call(bf16[128,1536]{1,0:T(8,128)(2,1)} %pad_maximum_fusion.piece_ref, bf16[96,4096]{1,0:T(8,128)(2,1)} %fusion.8.rows_ref), custom_call_target="tpu_custom_call" | custom-call | tf_op jit(solution)/shard_map/pallas_call | solution.py:258
  105.7 12.1 %fusion.3 = bf16[768,1024]{1,0:T(8,128)(2,1)} fusion(bf16[768,4096]{1,0:T(8,128)(2,1)} %bitcast.36, bf16[4096,1536]{1,0:T(8,128)(2,1)} %bitcast.32), kind=kOutput, calls=%fused_computation.8 | convolution fusion | flops 6443237376 | bytes 16252928 | tf_op jit(solution)/shard_map/dot_general | solution.py:448
  117.8 2.7 %fusion.10 = f32[768,512]{1,0:T(8,128)S(1)} fusion(f32[768]{0:T(1024)S(1)} %multiply_reduce_fusion.1, f32[768]{0:T(1024)S(1)} %get-tuple-element.11, s32[768]{0:T(1024)S(1)} %get-tuple-element.10, bf16[768,1024]{1,0:T(8,128)(2,1)} %fusion.3), kind=kOutput, calls=%fused_computation.16 | convolution fusion | flops 911867904 | bytes 3166208 | tf_op jit(solution)/shard_map/dot_general | solution.py:405
  120.6 0.6 slice.44
  121.2 0.6 slice.43
  121.8 1.3 exponential_select_fusion
  123.1 2.6 %fusion.20.state_ref = f32[256,512]{1,0:T(8,128)} fusion(bf16[768,1024]{1,0:T(8,128)(2,1)} %fusion.3, f32[768]{0:T(1024)S(1)} %exponential_select_fusion), kind=kOutput, calls=%fused_computation.27 | convolution fusion | flops 201916416 | bytes 1707008 | tf_op jit(solution)/shard_map/dot_general | solution.py:410
  127.1 0.6 broadcast_in_dim.5.decay_ref
  127.7 41.1 %shard_map.92 = f32[256,512]{1,0:T(8,128)} custom-call(f32[256,512]{1,0:T(8,128)} %fusion.20.state_ref, f32[16,512]{1,0:T(8,128)} %broadcast_in_dim.5.decay_ref), custom_call_target="tpu_custom_call" | custom-call | tf_op jit(solution)/shard_map/pallas_call | solution.py:356
  168.7 2.7 %fusion.38 = (f32[768]{0:T(1024)S(1)}, f32[768,512]{1,0:T(8,128)S(1)}) fusion(f32[768,512]{1,0:T(8,128)S(1)} %fusion.10, f32[256,512]{1,0:T(8,128)} %shard_map.92, f32[768]{0:T(1024)S(1)} %get-tuple-element.9, bf16[768,1024]{1,0:T(8,128)(2,1)} %fusion.3), kind=kOutput, calls=%fused_computation.58 | convolution fusion | flops 1209138432 | bytes 4069376 | tf_op jit(solution)/shard_map/dot_general | solution.py:420
  171.5 0.0 copy-start.2
  171.5 0.3 multiply_reduce_fusion
  171.8 0.3 copy-done.2
  172.2 0.3 multiply_convert_fusion.1.heads_ref
  172.4 2.5 %slice.50.weight_ref = bf16[4096,512]{1,0:T(8,128)(2,1)S(1)} slice(bf16[4096,1536]{1,0:T(8,128)(2,1)} %bitcast.33), slice={[0:4096], [1024:1536]} | slice | bytes 8388608 | tf_op jit(solution)/shard_map/slice | solution.py:447
  174.9 40.9 %shard_map.93 = bf16[96,4096]{1,0:T(8,128)(2,1)S(1)} custom-call(bf16[768,512]{1,0:T(8,128)(2,1)S(1)} %multiply_convert_fusion.1.heads_ref, bf16[4096,512]{1,0:T(8,128)(2,1)S(1)} %slice.50.weight_ref), custom_call_target="tpu_custom_call" | custom-call | tf_op jit(solution)/shard_map/pallas_call | solution.py:329
  215.8 1.1 fusion.9
  (6 shorter events, 0.1 us)
Async XLA Ops:
  0.0 6.7 %copy-start = (bf16[96,4096]{1,0:T(8,128)(2,1)S(1)}, bf16[96,4096]{1,0:T(8,128)(2,1)}, u32[]{:S(2)}) copy-start(bf16[96,4096]{1,0:T(8,128)(2,1)} %param.9) | copy-start | bytes 2359300
  0.0 6.9 %copy-start.1 = (f32[4096]{0:T(1024)S(1)}, f32[4096]{0:T(1024)}, u32[]{:S(2)}) copy-start(f32[4096]{0:T(1024)} %param.10) | copy-start | bytes 49156
  171.5 0.7 copy-start.2

commit v14 on v13

--- a/solution.py
+++ b/solution.py
@@ -45,18 +45,24 @@
     acc_decay[...] = decay * far_decay
 
 
+def extend(got, rows, acc_total, acc_decay):
+    far_total = got[:rows].astype(jnp.float32)
+    far_decay = got[rows : rows + DECAY_ROWS].astype(jnp.float32) + got[rows + DECAY_ROWS :].astype(jnp.float32)
+    acc_total[...] = far_decay[0:1, :] * acc_total[...] + far_total
+    acc_decay[...] = far_decay * acc_decay[...]
+
+
 def scan_kernel(
     ny, nz, zshifts, state_ref, decay_ref, out_ref,
-    row_send, row_recv, z_send, z_recv, p_send, p_recv,
-    acc_total, acc_decay, quarter_total, quarter_decay, z_total, z_decay,
-    row_send_sems, row_recv_sems, z_send_sems, z_recv_sems, p_send_sems, p_recv_sems,
+    row_send, row_recv, z_send, z_recv, c_send, c_recv,
+    prefix_total, prefix_decay, quarter_total, quarter_decay, z_total, z_decay,
+    row_send_sems, row_recv_sems, z_send_sems, z_recv_sems, c_send_sems, c_recv_sems,
 ):
     yi = lax.axis_index("cy")
     zi = lax.axis_index("cz")
     tp = lax.axis_index("tp")
     rows, width = state_ref.shape
     quarter = width // ny
-    mine = pl.ds(pl.multiple_of(yi * quarter, quarter), quarter)
 
     barrier = pltpu.get_barrier_semaphore()
     z_partners = sorted(set(zshifts))
@@ -67,36 +73,33 @@
             pl.semaphore_signal(barrier, 1, device_id=(peer, yi, tp), device_id_type=MESH_ID)
     pl.semaphore_wait(barrier, (ny - 1) + 2 * len(z_partners))
 
-    def row_copy(d, target, slot):
+    def row_copy(d, target, slot, part):
         return pltpu.make_async_remote_copy(
-            src_ref=row_send, dst_ref=row_recv.at[slot], send_sem=row_send_sems.at[d],
+            src_ref=row_send.at[part], dst_ref=row_recv.at[slot], send_sem=row_send_sems.at[d],
             recv_sem=row_recv_sems.at[slot], device_id=(zi, target, tp), device_id_type=MESH_ID,
         )
 
-    pack(row_send, state_ref[...], decay_ref[...])
+    for y in range(ny):
+        pack(row_send.at[y], state_ref[:, y * quarter : (y + 1) * quarter], decay_ref[:, y * quarter : (y + 1) * quarter])
     for d in range(1, ny):
-        row_copy(d, lax.rem(yi + d, ny), yi).start()
+        target = lax.rem(yi + d, ny)
+        row_copy(d, target, yi, target).start()
     for d in range(1, ny):
-        source = lax.rem(yi + ny - d, ny)
-        row_copy(d, yi, source).wait_recv()
-
-    acc_total[...] = jnp.zeros_like(acc_total)
-    acc_decay[...] = jnp.ones_like(acc_decay)
-    for d in range(1, ny):
-        @pl.when(yi - d >= 0)
-        def _():
-            absorb(row_recv[yi - d], rows, acc_total, acc_decay)
+        row_copy(d, yi, lax.rem(yi + ny - d, ny), yi).wait_recv()
 
     quarter_total[...] = jnp.zeros_like(quarter_total)
     quarter_decay[...] = jnp.ones_like(quarter_decay)
-    for y in reversed(range(ny)):
+    for y in range(ny):
+        prefix_total[y] = quarter_total[...]
+        prefix_decay[y] = quarter_decay[...]
+
         @pl.when(yi == y)
         def _():
-            absorb(row_send[:, mine], rows, quarter_total, quarter_decay)
+            extend(row_send[y], rows, quarter_total, quarter_decay)
 
         @pl.when(yi != y)
         def _():
-            absorb(row_recv[y, :, mine], rows, quarter_total, quarter_decay)
+            extend(row_recv[y], rows, quarter_total, quarter_decay)
 
     def z_copy(j, slot, peer):
         return pltpu.make_async_remote_copy(
@@ -129,36 +132,80 @@
         z_send_round(j, j - 1)
         z_absorb(j, j - 1)
 
-    def p_copy(d, target, slot):
+    def c_copy(y, target, slot):
         return pltpu.make_async_remote_copy(
-            src_ref=p_send, dst_ref=p_recv.at[slot], send_sem=p_send_sems.at[d],
-            recv_sem=p_recv_sems.at[slot], device_id=(zi, target, tp), device_id_type=MESH_ID,
+            src_ref=c_send.at[y], dst_ref=c_recv.at[slot], send_sem=c_send_sems.at[y],
+            recv_sem=c_recv_sems.at[slot], device_id=(zi, target, tp), device_id_type=MESH_ID,
         )
 
-    p_send[...] = z_total[...].astype(jnp.bfloat16)
+    for y in range(ny):
+        done = prefix_decay[y][0:1, :] * z_total[...] + prefix_total[y]
+
+        @pl.when(yi == y)
+        def _():
+            out_ref[:, y * quarter : (y + 1) * quarter] = done
+
+        @pl.when(yi != y)
+        def _():
+            c_send[y] = done.astype(jnp.bfloat16)
+            c_copy(y, y, yi).start()
+
+    for y in range(ny):
+        @pl.when(yi != y)
+        def _():
+            c_copy(y, yi, y).wait_recv()
+            out_ref[:, y * quarter : (y + 1) * quarter] = c_recv[y].astype(jnp.float32)
+
     for d in range(1, ny):
-        p_copy(d, lax.rem(yi + d, ny), yi).start()
-    for d in range(1, ny):
-        p_copy(d, yi, lax.rem(yi + ny - d, ny)).wait_recv()
-    decay = acc_decay[0:1, :]
+        target = lax.rem(yi + d, ny)
+        row_copy(d, target, yi, target).wait_send()
     for y in range(ny):
-        cols = slice(y * quarter, (y + 1) * quarter)
-
-        @pl.when(yi == y)
-        def _():
-            out_ref[:, cols] = decay[:, cols] * p_send[...].astype(jnp.float32) + acc_total[:, cols]
-
         @pl.when(yi != y)
         def _():
-            out_ref[:, cols] = decay[:, cols] * p_recv[y].astype(jnp.float32) + acc_total[:, cols]
-
-    for d in range(1, ny):
-        row_copy(d, lax.rem(yi + d, ny), yi).wait_send()
-        p_copy(d, lax.rem(yi + d, ny), yi).wait_send()
+            c_copy(y, y, yi).wait_send()
     for j in range(len(zshifts)):
         @pl.when(zi + zshifts[j] < nz)
         def _():
             z_copy(j, 0 if j < first else j - 1, zi + zshifts[j]).wait_send()
+
+
+def carried_in(passing, state):
+    ny, nz = lax.axis_size("cy"), lax.axis_size("cz")
+    if ny * nz == 1:
+        return jnp.zeros_like(state)
+    zshifts = scan_shifts(nz) if nz > 1 else []
+    rows, width = state.shape
+    quarter = width // ny
+    decay = jnp.broadcast_to(passing.reshape(1, 1), (DECAY_ROWS, width)).astype(jnp.float32)
+    message = rows + 2 * DECAY_ROWS
+    slots = max(len(zshifts), 1)
+    return pl.pallas_call(
+        functools.partial(scan_kernel, ny, nz, zshifts),
+        out_shape=jax.ShapeDtypeStruct((rows, width), jnp.float32),
+        in_specs=[pl.BlockSpec(memory_space=pltpu.VMEM)] * 2,
+        out_specs=pl.BlockSpec(memory_space=pltpu.VMEM),
+        scratch_shapes=[
+            pltpu.VMEM((ny, message, quarter), jnp.bfloat16),
+            pltpu.VMEM((ny, message, quarter), jnp.bfloat16),
+            pltpu.VMEM((slots, message, quarter), jnp.bfloat16),
+            pltpu.VMEM((slots, message, quarter), jnp.bfloat16),
+            pltpu.VMEM((ny, rows, quarter), jnp.bfloat16),
+            pltpu.VMEM((ny, rows, quarter), jnp.bfloat16),
+            pltpu.VMEM((ny, rows, quarter), jnp.float32),
+            pltpu.VMEM((ny, DECAY_ROWS, quarter), jnp.float32),
+            pltpu.VMEM((rows, quarter), jnp.float32),
+            pltpu.VMEM((DECAY_ROWS, quarter), jnp.float32),
+            pltpu.VMEM((rows, quarter), jnp.float32),
+            pltpu.VMEM((DECAY_ROWS, quarter), jnp.float32),
+            pltpu.SemaphoreType.DMA((ny,)),
+            pltpu.SemaphoreType.DMA((ny,)),
+            pltpu.SemaphoreType.DMA((slots,)),
+            pltpu.SemaphoreType.DMA((slots,)),
+            pltpu.SemaphoreType.DMA((ny,)),
+            pltpu.SemaphoreType.DMA((ny,)),
+        ],
+        compiler_params=pltpu.CompilerParams(collective_id=0, has_side_effects=True),
+    )(state.astype(jnp.float32), decay)
 
 
 def ring_steps(n):
@@ -343,45 +390,6 @@
     )(heads, weight)
 
 
-def carried_in(passing, state):
-    ny, nz = lax.axis_size("cy"), lax.axis_size("cz")
-    if ny * nz == 1:
-        return jnp.zeros_like(state)
-    zshifts = scan_shifts(nz) if nz > 1 else []
-    rows, width = state.shape
-    quarter = width // ny
-    decay = jnp.broadcast_to(passing.reshape(1, 1), (DECAY_ROWS, width)).astype(jnp.float32)
-    message = rows + 2 * DECAY_ROWS
-    slots = max(len(zshifts), 1)
-    return pl.pallas_call(
-        functools.partial(scan_kernel, ny, nz, zshifts),
-        out_shape=jax.ShapeDtypeStruct((rows, width), jnp.float32),
-        in_specs=[pl.BlockSpec(memory_space=pltpu.VMEM)] * 2,
-        out_specs=pl.BlockSpec(memory_space=pltpu.VMEM),
-        scratch_shapes=[
-            pltpu.VMEM((message, width), jnp.bfloat16),
-            pltpu.VMEM((ny, message, width), jnp.bfloat16),
-            pltpu.VMEM((slots, message, quarter), jnp.bfloat16),
-            pltpu.VMEM((slots, message, quarter), jnp.bfloat16),
-            pltpu.VMEM((rows, quarter), jnp.bfloat16),
-            pltpu.VMEM((ny, rows, quarter), jnp.bfloat16),
-            pltpu.VMEM((rows, width), jnp.float32),
-            pltpu.VMEM((DECAY_ROWS, width), jnp.float32),
-            pltpu.VMEM((rows, quarter), jnp.float32),
-            pltpu.VMEM((DECAY_ROWS, quarter), jnp.float32),
-            pltpu.VMEM((rows, quarter), jnp.float32),
-            pltpu.VMEM((DECAY_ROWS, quarter), jnp.float32),
-            pltpu.SemaphoreType.DMA((ny,)),
-            pltpu.SemaphoreType.DMA((ny,)),
-            pltpu.SemaphoreType.DMA((slots,)),
-            pltpu.SemaphoreType.DMA((slots,)),
-            pltpu.SemaphoreType.DMA((ny,)),
-            pltpu.SemaphoreType.DMA((ny,)),
-        ],
-        compiler_params=pltpu.CompilerParams(collective_id=0, has_side_effects=True),
-    )(state.astype(jnp.float32), decay)
-
-
 def rms_rows(embedded_entries, norm_gain):
     token_float = embedded_entries.astype(jnp.float32)
     moment = jnp.mean(token_float * token_float, axis=1, keepdims=True)

time: 217 us -> 208 us (0.959)
  Pallas kernels: 180 us -> 169 us
    pallas_call x1, Pallas kernels: 41.1 us -> 30.8 us  [carried_in(): pl.pallas_call(functools.partial(scan_kernel, ny, nz, zshifts), out_shape...]
where the time goes in v14:
time: 208 us; the launch traced here: 207 us
  Pallas kernels  169 us (81%)
  matrix products  20.2 us (10%)
  other arithmetic  8.99 us (4%)
  local copies, waits for them, and re-layouts  6.05 us (3%)
  between operations  2.09 us (1%)
    pallas_call x1, Pallas kernels, gather_blocks(): pl.pallas_call(functools.partial(gather_kernel, ny, nz, nt), out_shape=(j...  97.6 us
    pallas_call x1, Pallas kernels, scatter_rows(): pl.pallas_call(functools.partial(scatter_kernel, nt), out_shape=jax.Shape...  40.9 us
    pallas_call x1, Pallas kernels, carried_in(): pl.pallas_call(functools.partial(scan_kernel, ny, nz, zshifts), out_shape...  30.8 us
    dot_general x1, matrix products, local(): jnp.dot(every_row_list, parameter_collection, preferred_element_type=jnp....  12.1 us

profile of v14, /device:TPU:224, one launch (start us, length us, event | category | flops | bytes accessed | tf_op | source)
XLA Modules:
  0.0 206.6 jit_solution(6908478438516806788)
XLA Ops:
  0.0 0.0 copy-start
  0.0 0.0 copy-start.1
  0.0 0.8 multiply_reduce_fusion.1
  0.8 1.0 reduce-window.16
  1.7 0.1 slice.38
  1.8 0.1 slice_reduce_fusion.1
  2.6 0.7 negate_reduce_fusion
  3.3 0.3 reduce-window.24
  3.6 0.1 slice.40
  3.7 0.1 slice_reduce_fusion
  3.8 0.1 select_multiply_fusion
  3.9 1.0 copy.13
  4.9 1.7 pad_maximum_fusion.piece_ref
  6.7 0.0 copy-done
  6.7 0.3 fusion.6
  6.9 0.0 copy-done.1
  6.9 1.1 fusion.8.rows_ref
  8.1 97.6 %shard_map.91 = (bf16[8,4,128,1536]{3,2,1,0:T(8,128)(2,1)}, bf16[8,96,4096]{2,1,0:T(8,128)(2,1)}) custom-call(bf16[128,1536]{1,0:T(8,128)(2,1)} %pad_maximum_fusion.piece_ref, bf16[96,4096]{1,0:T(8,128)(2,1)} %fusion.8.rows_ref), custom_call_target="tpu_custom_call" | custom-call | tf_op jit(solution)/shard_map/pallas_call | solution.py:305
  105.7 12.1 %fusion.3 = bf16[768,1024]{1,0:T(8,128)(2,1)} fusion(bf16[768,4096]{1,0:T(8,128)(2,1)} %bitcast.36, bf16[4096,1536]{1,0:T(8,128)(2,1)} %bitcast.32), kind=kOutput, calls=%fused_computation.8 | convolution fusion | flops 6443237376 | bytes 16252928 | tf_op jit(solution)/shard_map/dot_general | solution.py:456
  117.8 2.7 %fusion.10 = f32[768,512]{1,0:T(8,128)S(1)} fusion(f32[768]{0:T(1024)S(1)} %multiply_reduce_fusion.1, f32[768]{0:T(1024)S(1)} %get-tuple-element.11, s32[768]{0:T(1024)S(1)} %get-tuple-element.10, bf16[768,1024]{1,0:T(8,128)(2,1)} %fusion.3), kind=kOutput, calls=%fused_computation.16 | convolution fusion | flops 911867904 | bytes 3166208 | tf_op jit(solution)/shard_map/dot_general | solution.py:413
  120.6 0.6 slice.44
  121.2 0.6 slice.43
  121.8 1.3 exponential_select_fusion
  123.1 2.6 %fusion.20.state_ref = f32[256,512]{1,0:T(8,128)} fusion(bf16[768,1024]{1,0:T(8,128)(2,1)} %fusion.3, f32[768]{0:T(1024)S(1)} %exponential_select_fusion), kind=kOutput, calls=%fused_computation.27 | convolution fusion | flops 201916416 | bytes 1707008 | tf_op jit(solution)/shard_map/dot_general | solution.py:418
  127.1 0.6 broadcast_in_dim.5.decay_ref
  127.7 30.8 %shard_map.92 = f32[256,512]{1,0:T(8,128)} custom-call(f32[256,512]{1,0:T(8,128)} %fusion.20.state_ref, f32[16,512]{1,0:T(8,128)} %broadcast_in_dim.5.decay_ref), custom_call_target="tpu_custom_call" | custom-call | tf_op jit(solution)/shard_map/pallas_call | solution.py:182
  158.4 2.7 %fusion.38 = (f32[768]{0:T(1024)S(1)}, f32[768,512]{1,0:T(8,128)S(1)}) fusion(f32[768,512]{1,0:T(8,128)S(1)} %fusion.10, f32[256,512]{1,0:T(8,128)} %shard_map.92, f32[768]{0:T(1024)S(1)} %get-tuple-element.9, bf16[768,1024]{1,0:T(8,128)(2,1)} %fusion.3), kind=kOutput, calls=%fused_computation.58 | convolution fusion | flops 1209138432 | bytes 4069376 | tf_op jit(solution)/shard_map/dot_general | solution.py:428
  161.2 0.0 copy-start.2
  161.2 0.3 multiply_reduce_fusion
  161.5 0.3 copy-done.2
  161.9 0.3 multiply_convert_fusion.1.heads_ref
  162.1 2.5 %slice.50.weight_ref = bf16[4096,512]{1,0:T(8,128)(2,1)S(1)} slice(bf16[4096,1536]{1,0:T(8,128)(2,1)} %bitcast.33), slice={[0:4096], [1024:1536]} | slice | bytes 8388608 | tf_op jit(solution)/shard_map/slice | solution.py:455
  164.6 40.9 %shard_map.93 = bf16[96,4096]{1,0:T(8,128)(2,1)S(1)} custom-call(bf16[768,512]{1,0:T(8,128)(2,1)S(1)} %multiply_convert_fusion.1.heads_ref, bf16[4096,512]{1,0:T(8,128)(2,1)S(1)} %slice.50.weight_ref), custom_call_target="tpu_custom_call" | custom-call | tf_op jit(solution)/shard_map/pallas_call | solution.py:376
  205.5 1.1 fusion.9
  (6 shorter events, 0.1 us)
Async XLA Ops:
  0.0 6.7 %copy-start = (bf16[96,4096]{1,0:T(8,128)(2,1)S(1)}, bf16[96,4096]{1,0:T(8,128)(2,1)}, u32[]{:S(2)}) copy-start(bf16[96,4096]{1,0:T(8,128)(2,1)} %param.9) | copy-start | bytes 2359300
  0.0 6.9 %copy-start.1 = (f32[4096]{0:T(1024)S(1)}, f32[4096]{0:T(1024)}, u32[]{:S(2)}) copy-start(f32[4096]{0:T(1024)} %param.10) | copy-start | bytes 49156
  161.2 0.7 copy-start.2

commit v15 on v14

--- a/solution.py
+++ b/solution.py
@@ -241,9 +241,9 @@
     own_rows.start()
     sends = []
 
-    def ring(along, group_of, first_src):
+    def ring(along, group_of, first_src, height):
         n, me = {"y": (ny, yi), "z": (nz, zi), "t": (nt, tp)}[along]
-        return dict(n=n, me=me, along=along, group_of=group_of, first_src=first_src, steps=ring_steps(n), last={})
+        return dict(n=n, me=me, along=along, group_of=group_of, first_src=first_src, steps=ring_steps(n), last={}, height=height)
 
     def device(r, k):
         return {"y": (zi, k, tp), "z": (k, yi, tp), "t": (zi, yi, k)}[r["along"]]
@@ -253,21 +253,27 @@
             return
         n, me, group_of = r["n"], r["me"], r["group_of"]
         hop, both = r["steps"][t - 1]
-        for sign in (1, -1) if both else (1,):
+        whole = slice(None)
+        half_rows = r["height"] // 2
+        for sign in (1, -1):
+            if both:
+                part = whole
+            else:
+                part = pl.ds(0, half_rows) if sign == 1 else pl.ds(half_rows, half_rows)
             if t > 1:
                 r["last"].pop(sign).wait_recv()
-            origin = lax.rem(me + n - sign * (hop - 1), n)
+            origin = lax.rem(me + 2 * n - sign * (hop - 1), n)
             target = lax.rem(me + n + sign, n)
             source = lax.rem(me + n - sign, n)
             arrived = lax.rem(me + 2 * n - sign * hop, n)
             idx = len(sends)
             send = pltpu.make_async_remote_copy(
-                src_ref=r["first_src"] if t == 1 else group_of(origin), dst_ref=group_of(origin),
+                src_ref=r["first_src"](part) if t == 1 else group_of(origin, part), dst_ref=group_of(origin, part),
                 send_sem=send_sems.at[idx], recv_sem=recv_sems.at[idx],
                 device_id=device(r, target), device_id_type=MESH_ID,
             )
             incoming = pltpu.make_async_remote_copy(
-                src_ref=group_of(arrived), dst_ref=group_of(arrived),
+                src_ref=group_of(arrived, part), dst_ref=group_of(arrived, part),
                 send_sem=send_sems.at[idx], recv_sem=recv_sems.at[idx],
                 device_id=device(r, source), device_id_type=MESH_ID,
             )
@@ -283,15 +289,16 @@
             for incoming in r["last"].values():
                 incoming.wait_recv()
 
+    height = piece_ref.shape[0]
     stage([
-        ring("y", lambda k: out_ref.at[zi, k, :, cols[0]], piece_ref.at[:, cols[0]]),
-        ring("z", lambda k: out_ref.at[k, yi, :, cols[1]], piece_ref.at[:, cols[1]]),
+        ring("y", lambda k, p: out_ref.at[zi, k, p, cols[0]], lambda p: piece_ref.at[p, cols[0]], height),
+        ring("z", lambda k, p: out_ref.at[k, yi, p, cols[1]], lambda p: piece_ref.at[p, cols[1]], height),
     ])
     own.wait()
     stage([
-        ring("z", lambda k: out_ref.at[k, :, :, cols[0]], out_ref.at[zi, :, :, cols[0]]),
-        ring("y", lambda k: out_ref.at[:, k, :, cols[1]], out_ref.at[:, yi, :, cols[1]]),
-        ring("t", lambda k: rows_out.at[k], rows_ref),
+        ring("z", lambda k, p: out_ref.at[k, :, p, cols[0]], lambda p: out_ref.at[zi, :, p, cols[0]], height),
+        ring("y", lambda k, p: out_ref.at[:, k, p, cols[1]], lambda p: out_ref.at[:, yi, p, cols[1]], height),
+        ring("t", lambda k, p: rows_out.at[k, p, :], lambda p: rows_ref.at[p, :], rows_ref.shape[0]),
     ])
     own_rows.wait()
     for send in sends:
@@ -301,7 +308,7 @@
 def gather_blocks(piece, rows):
     ny, nz, nt = lax.axis_size("cy"), lax.axis_size("cz"), lax.axis_size("tp")
     height, width = piece.shape
-    count = sum(sum(2 if both else 1 for _, both in ring_steps(n)) for n in (ny, nz, nz, ny, nt))
+    count = sum(2 * len(ring_steps(n)) for n in (ny, nz, nz, ny, nt))
     out, rows_out = pl.pallas_call(
         functools.partial(gather_kernel, ny, nz, nt),
         out_shape=(

time: 208 us -> 200 us (0.962)
  Pallas kernels: 169 us -> 161 us
    pallas_call x1, Pallas kernels: 97.6 us -> 86.2 us  [gather_blocks(): pl.pallas_call(functools.partial(gather_kernel, ny, nz, nt), out_shape=(j...]
    pallas_call x1, Pallas kernels: 30.8 us -> 34.2 us  [carried_in(): pl.pallas_call(functools.partial(scan_kernel, ny, nz, zshifts), out_shape...]
where the time goes in v15:
time: 200 us; the launch traced here: 199 us
  Pallas kernels  161 us (80%)
  matrix products  20.2 us (10%)
  other arithmetic  8.99 us (4%)
  local copies, waits for them, and re-layouts  6.05 us (3%)
  between operations  2.09 us (1%)
    pallas_call x1, Pallas kernels, gather_blocks(): pl.pallas_call(functools.partial(gather_kernel, ny, nz, nt), out_shape=(j...  86.2 us
    pallas_call x1, Pallas kernels, scatter_rows(): pl.pallas_call(functools.partial(scatter_kernel, nt), out_shape=jax.Shape...  40.9 us
    pallas_call x1, Pallas kernels, carried_in(): pl.pallas_call(functools.partial(scan_kernel, ny, nz, zshifts), out_shape...  34.2 us
    dot_general x1, matrix products, local(): jnp.dot(every_row_list, parameter_collection, preferred_element_type=jnp....  12.1 us

profile of v15, /device:TPU:224, one launch (start us, length us, event | category | flops | bytes accessed | tf_op | source)
XLA Modules:
  0.0 198.6 jit_solution(3235911322531026083)
XLA Ops:
  0.0 0.0 copy-start
  0.0 0.0 copy-start.1
  0.0 0.8 multiply_reduce_fusion.1
  0.8 1.0 reduce-window.16
  1.7 0.1 slice.38
  1.8 0.1 slice_reduce_fusion.1
  2.6 0.7 negate_reduce_fusion
  3.3 0.3 reduce-window.24
  3.6 0.1 slice.40
  3.7 0.1 slice_reduce_fusion
  3.8 0.1 select_multiply_fusion
  3.9 1.0 copy.13
  4.9 1.7 pad_maximum_fusion.piece_ref
  6.7 0.0 copy-done
  6.7 0.3 fusion.6
  6.9 0.0 copy-done.1
  6.9 1.1 fusion.8.rows_ref
  8.1 86.2 %shard_map.91 = (bf16[8,4,128,1536]{3,2,1,0:T(8,128)(2,1)}, bf16[8,96,4096]{2,1,0:T(8,128)(2,1)}) custom-call(bf16[128,1536]{1,0:T(8,128)(2,1)} %pad_maximum_fusion.piece_ref, bf16[96,4096]{1,0:T(8,128)(2,1)} %fusion.8.rows_ref), custom_call_target="tpu_custom_call" | custom-call | tf_op jit(solution)/shard_map/pallas_call | solution.py:312
  94.3 12.1 %fusion.3 = bf16[768,1024]{1,0:T(8,128)(2,1)} fusion(bf16[768,4096]{1,0:T(8,128)(2,1)} %bitcast.36, bf16[4096,1536]{1,0:T(8,128)(2,1)} %bitcast.32), kind=kOutput, calls=%fused_computation.8 | convolution fusion | flops 6443237376 | bytes 16252928 | tf_op jit(solution)/shard_map/dot_general | solution.py:463
  106.3 2.8 %fusion.10 = f32[768,512]{1,0:T(8,128)S(1)} fusion(f32[768]{0:T(1024)S(1)} %multiply_reduce_fusion.1, f32[768]{0:T(1024)S(1)} %get-tuple-element.11, s32[768]{0:T(1024)S(1)} %get-tuple-element.10, bf16[768,1024]{1,0:T(8,128)(2,1)} %fusion.3), kind=kOutput, calls=%fused_computation.16 | convolution fusion | flops 911867904 | bytes 3166208 | tf_op jit(solution)/shard_map/dot_general | solution.py:420
  109.1 0.6 slice.44
  109.7 0.6 slice.43
  110.4 1.3 exponential_select_fusion
  111.7 2.6 %fusion.20.state_ref = f32[256,512]{1,0:T(8,128)} fusion(bf16[768,1024]{1,0:T(8,128)(2,1)} %fusion.3, f32[768]{0:T(1024)S(1)} %exponential_select_fusion), kind=kOutput, calls=%fused_computation.27 | convolution fusion | flops 201916416 | bytes 1707008 | tf_op jit(solution)/shard_map/dot_general | solution.py:425
  115.6 0.6 broadcast_in_dim.5.decay_ref
  116.2 34.2 %shard_map.92 = f32[256,512]{1,0:T(8,128)} custom-call(f32[256,512]{1,0:T(8,128)} %fusion.20.state_ref, f32[16,512]{1,0:T(8,128)} %broadcast_in_dim.5.decay_ref), custom_call_target="tpu_custom_call" | custom-call | tf_op jit(solution)/shard_map/pallas_call | solution.py:182
  150.4 2.7 %fusion.38 = (f32[768]{0:T(1024)S(1)}, f32[768,512]{1,0:T(8,128)S(1)}) fusion(f32[768,512]{1,0:T(8,128)S(1)} %fusion.10, f32[256,512]{1,0:T(8,128)} %shard_map.92, f32[768]{0:T(1024)S(1)} %get-tuple-element.9, bf16[768,1024]{1,0:T(8,128)(2,1)} %fusion.3), kind=kOutput, calls=%fused_computation.58 | convolution fusion | flops 1209138432 | bytes 4069376 | tf_op jit(solution)/shard_map/dot_general | solution.py:435
  153.1 0.0 copy-start.2
  153.1 0.3 multiply_reduce_fusion
  153.5 0.3 copy-done.2
  153.8 0.3 multiply_convert_fusion.1.heads_ref
  154.1 2.5 %slice.50.weight_ref = bf16[4096,512]{1,0:T(8,128)(2,1)S(1)} slice(bf16[4096,1536]{1,0:T(8,128)(2,1)} %bitcast.33), slice={[0:4096], [1024:1536]} | slice | bytes 8388608 | tf_op jit(solution)/shard_map/slice | solution.py:462
  156.6 40.9 %shard_map.93 = bf16[96,4096]{1,0:T(8,128)(2,1)S(1)} custom-call(bf16[768,512]{1,0:T(8,128)(2,1)S(1)} %multiply_convert_fusion.1.heads_ref, bf16[4096,512]{1,0:T(8,128)(2,1)S(1)} %slice.50.weight_ref), custom_call_target="tpu_custom_call" | custom-call | tf_op jit(solution)/shard_map/pallas_call | solution.py:383
  197.5 1.1 fusion.9
  (6 shorter events, 0.1 us)
Async XLA Ops:
  0.0 6.7 %copy-start = (bf16[96,4096]{1,0:T(8,128)(2,1)S(1)}, bf16[96,4096]{1,0:T(8,128)(2,1)}, u32[]{:S(2)}) copy-start(bf16[96,4096]{1,0:T(8,128)(2,1)} %param.9) | copy-start | bytes 2359300
  0.0 6.9 %copy-start.1 = (f32[4096]{0:T(1024)S(1)}, f32[4096]{0:T(1024)}, u32[]{:S(2)}) copy-start(f32[4096]{0:T(1024)} %param.10) | copy-start | bytes 49156
  153.1 0.7 copy-start.2

commit v16 on v15

--- a/solution.py
+++ b/solution.py
@@ -290,16 +290,33 @@
                 incoming.wait_recv()
 
     height = piece_ref.shape[0]
-    stage([
-        ring("y", lambda k, p: out_ref.at[zi, k, p, cols[0]], lambda p: piece_ref.at[p, cols[0]], height),
-        ring("z", lambda k, p: out_ref.at[k, yi, p, cols[1]], lambda p: piece_ref.at[p, cols[1]], height),
-    ])
+    a1 = ring("y", lambda k, p: out_ref.at[zi, k, p, cols[0]], lambda p: piece_ref.at[p, cols[0]], height)
+    b1 = ring("z", lambda k, p: out_ref.at[k, yi, p, cols[1]], lambda p: piece_ref.at[p, cols[1]], height)
+    a2 = ring("z", lambda k, p: out_ref.at[k, :, p, cols[0]], lambda p: out_ref.at[zi, :, p, cols[0]], height)
+    b2 = ring("y", lambda k, p: out_ref.at[:, k, p, cols[1]], lambda p: out_ref.at[:, yi, p, cols[1]], height)
+    rt = ring("t", lambda k, p: rows_out.at[k, p, :], lambda p: rows_ref.at[p, :], rows_ref.shape[0])
+
+    def finish(r):
+        for incoming in r["last"].values():
+            incoming.wait_recv()
+        r["last"] = {}
+
+    for t in range(1, len(a1["steps"]) + 1):
+        step(a1, t)
+        step(b1, t)
+    finish(a1)
     own.wait()
-    stage([
-        ring("z", lambda k, p: out_ref.at[k, :, p, cols[0]], lambda p: out_ref.at[zi, :, p, cols[0]], height),
-        ring("y", lambda k, p: out_ref.at[:, k, p, cols[1]], lambda p: out_ref.at[:, yi, p, cols[1]], height),
-        ring("t", lambda k, p: rows_out.at[k, p, :], lambda p: rows_ref.at[p, :], rows_ref.shape[0]),
-    ])
+    step(a2, 1)
+    for t in range(len(a1["steps"]) + 1, len(b1["steps"]) + 1):
+        step(b1, t)
+    finish(b1)
+    later = max(len(a2["steps"]), len(b2["steps"]) + 1, len(rt["steps"]) + 1)
+    for t in range(1, later + 1):
+        step(b2, t)
+        step(rt, t)
+        step(a2, t + 1)
+    for r in (a2, b2, rt):
+        finish(r)
     own_rows.wait()
     for send in sends:
         send.wait_send()

time: 200 us -> 215 us (1.075)
  Pallas kernels: 161 us -> 176 us
    pallas_call x1, Pallas kernels: 86.2 us -> 102 us  [gather_blocks(): pl.pallas_call(functools.partial(gather_kernel, ny, nz, nt), out_shape=(j...]
where the time goes in v16:
time: 215 us; the launch traced here: 213 us
  Pallas kernels  176 us (82%)
  matrix products  20.2 us (9%)
  other arithmetic  8.99 us (4%)
  local copies, waits for them, and re-layouts  6.05 us (3%)
    pallas_call x1, Pallas kernels, gather_blocks(): pl.pallas_call(functools.partial(gather_kernel, ny, nz, nt), out_shape=(j...  102 us
    pallas_call x1, Pallas kernels, scatter_rows(): pl.pallas_call(functools.partial(scatter_kernel, nt), out_shape=jax.Shape...  40.9 us
    pallas_call x1, Pallas kernels, carried_in(): pl.pallas_call(functools.partial(scan_kernel, ny, nz, zshifts), out_shape...  33.5 us
    dot_general x1, matrix products, local(): jnp.dot(every_row_list, parameter_collection, preferred_element_type=jnp....  12.1 us

profile of v16, /device:TPU:224, one launch (start us, length us, event | category | flops | bytes accessed | tf_op | source)
XLA Modules:
  0.0 213.4 jit_solution(9544443777149600375)
XLA Ops:
  0.0 0.0 copy-start
  0.0 0.0 copy-start.1
  0.0 0.8 multiply_reduce_fusion.1
  0.8 1.0 reduce-window.16
  1.7 0.1 slice.38
  1.8 0.1 slice_reduce_fusion.1
  2.6 0.7 negate_reduce_fusion
  3.3 0.3 reduce-window.24
  3.6 0.1 slice.40
  3.7 0.1 slice_reduce_fusion
  3.8 0.1 select_multiply_fusion
  3.9 1.0 copy.13
  4.9 1.7 pad_maximum_fusion.piece_ref
  6.7 0.0 copy-done
  6.7 0.3 fusion.6
  6.9 0.0 copy-done.1
  6.9 1.1 fusion.8.rows_ref
  8.1 101.7 %shard_map.91 = (bf16[8,4,128,1536]{3,2,1,0:T(8,128)(2,1)}, bf16[8,96,4096]{2,1,0:T(8,128)(2,1)}) custom-call(bf16[128,1536]{1,0:T(8,128)(2,1)} %pad_maximum_fusion.piece_ref, bf16[96,4096]{1,0:T(8,128)(2,1)} %fusion.8.rows_ref), custom_call_target="tpu_custom_call" | custom-call | tf_op jit(solution)/shard_map/pallas_call | solution.py:329
  109.8 12.1 %fusion.3 = bf16[768,1024]{1,0:T(8,128)(2,1)} fusion(bf16[768,4096]{1,0:T(8,128)(2,1)} %bitcast.36, bf16[4096,1536]{1,0:T(8,128)(2,1)} %bitcast.32), kind=kOutput, calls=%fused_computation.8 | convolution fusion | flops 6443237376 | bytes 16252928 | tf_op jit(solution)/shard_map/dot_general | solution.py:480
  121.9 2.8 %fusion.10 = f32[768,512]{1,0:T(8,128)S(1)} fusion(f32[768]{0:T(1024)S(1)} %multiply_reduce_fusion.1, f32[768]{0:T(1024)S(1)} %get-tuple-element.11, s32[768]{0:T(1024)S(1)} %get-tuple-element.10, bf16[768,1024]{1,0:T(8,128)(2,1)} %fusion.3), kind=kOutput, calls=%fused_computation.16 | convolution fusion | flops 911867904 | bytes 3166208 | tf_op jit(solution)/shard_map/dot_general | solution.py:437
  124.6 0.6 slice.44
  125.2 0.6 slice.43
  125.9 1.3 exponential_select_fusion
  127.2 2.6 %fusion.20.state_ref = f32[256,512]{1,0:T(8,128)} fusion(bf16[768,1024]{1,0:T(8,128)(2,1)} %fusion.3, f32[768]{0:T(1024)S(1)} %exponential_select_fusion), kind=kOutput, calls=%fused_computation.27 | convolution fusion | flops 201916416 | bytes 1707008 | tf_op jit(solution)/shard_map/dot_general | solution.py:442
  131.1 0.6 broadcast_in_dim.5.decay_ref
  131.7 33.5 %shard_map.92 = f32[256,512]{1,0:T(8,128)} custom-call(f32[256,512]{1,0:T(8,128)} %fusion.20.state_ref, f32[16,512]{1,0:T(8,128)} %broadcast_in_dim.5.decay_ref), custom_call_target="tpu_custom_call" | custom-call | tf_op jit(solution)/shard_map/pallas_call | solution.py:182
  165.3 2.7 %fusion.38 = (f32[768]{0:T(1024)S(1)}, f32[768,512]{1,0:T(8,128)S(1)}) fusion(f32[768,512]{1,0:T(8,128)S(1)} %fusion.10, f32[256,512]{1,0:T(8,128)} %shard_map.92, f32[768]{0:T(1024)S(1)} %get-tuple-element.9, bf16[768,1024]{1,0:T(8,128)(2,1)} %fusion.3), kind=kOutput, calls=%fused_computation.58 | convolution fusion | flops 1209138432 | bytes 4069376 | tf_op jit(solution)/shard_map/dot_general | solution.py:452
  168.0 0.0 copy-start.2
  168.0 0.3 multiply_reduce_fusion
  168.4 0.3 copy-done.2
  168.7 0.3 multiply_convert_fusion.1.heads_ref
  169.0 2.5 %slice.50.weight_ref = bf16[4096,512]{1,0:T(8,128)(2,1)S(1)} slice(bf16[4096,1536]{1,0:T(8,128)(2,1)} %bitcast.33), slice={[0:4096], [1024:1536]} | slice | bytes 8388608 | tf_op jit(solution)/shard_map/slice | solution.py:479
  171.4 40.9 %shard_map.93 = bf16[96,4096]{1,0:T(8,128)(2,1)S(1)} custom-call(bf16[768,512]{1,0:T(8,128)(2,1)S(1)} %multiply_convert_fusion.1.heads_ref, bf16[4096,512]{1,0:T(8,128)(2,1)S(1)} %slice.50.weight_ref), custom_call_target="tpu_custom_call" | custom-call | tf_op jit(solution)/shard_map/pallas_call | solution.py:400
  212.3 1.1 fusion.9
  (6 shorter events, 0.1 us)
Async XLA Ops:
  0.0 6.7 %copy-start = (bf16[96,4096]{1,0:T(8,128)(2,1)S(1)}, bf16[96,4096]{1,0:T(8,128)(2,1)}, u32[]{:S(2)}) copy-start(bf16[96,4096]{1,0:T(8,128)(2,1)} %param.9) | copy-start | bytes 2359300
  0.0 6.9 %copy-start.1 = (f32[4096]{0:T(1024)S(1)}, f32[4096]{0:T(1024)}, u32[]{:S(2)}) copy-start(f32[4096]{0:T(1024)} %param.10) | copy-start | bytes 49156
  168.0 0.7 copy-start.2

commit v17 on v15

--- a/solution.py
+++ b/solution.py
@@ -296,9 +296,9 @@
     ])
     own.wait()
     stage([
+        ring("t", lambda k, p: rows_out.at[k, p, :], lambda p: rows_ref.at[p, :], rows_ref.shape[0]),
         ring("z", lambda k, p: out_ref.at[k, :, p, cols[0]], lambda p: out_ref.at[zi, :, p, cols[0]], height),
         ring("y", lambda k, p: out_ref.at[:, k, p, cols[1]], lambda p: out_ref.at[:, yi, p, cols[1]], height),
-        ring("t", lambda k, p: rows_out.at[k, p, :], lambda p: rows_ref.at[p, :], rows_ref.shape[0]),
     ])
     own_rows.wait()
     for send in sends:

time: 200 us -> 196 us (0.980)
  Pallas kernels: 161 us -> 158 us
    pallas_call x1, Pallas kernels: 34.2 us -> 30.2 us  [carried_in(): pl.pallas_call(functools.partial(scan_kernel, ny, nz, zshifts), out_shape...]
where the time goes in v17:
time: 196 us; the launch traced here: 195 us
  Pallas kernels  158 us (81%)
  matrix products  20.2 us (10%)
  other arithmetic  8.99 us (5%)
  local copies, waits for them, and re-layouts  6.05 us (3%)
  between operations  2.09 us (1%)
    pallas_call x1, Pallas kernels, gather_blocks(): pl.pallas_call(functools.partial(gather_kernel, ny, nz, nt), out_shape=(j...  86.3 us
    pallas_call x1, Pallas kernels, scatter_rows(): pl.pallas_call(functools.partial(scatter_kernel, nt), out_shape=jax.Shape...  41.2 us
    pallas_call x1, Pallas kernels, carried_in(): pl.pallas_call(functools.partial(scan_kernel, ny, nz, zshifts), out_shape...  30.2 us
    dot_general x1, matrix products, local(): jnp.dot(every_row_list, parameter_collection, preferred_element_type=jnp....  12.1 us

profile of v17, /device:TPU:224, one launch (start us, length us, event | category | flops | bytes accessed | tf_op | source)
XLA Modules:
  0.0 195.0 jit_solution(10644617738530373152)
XLA Ops:
  0.0 0.0 copy-start
  0.0 0.0 copy-start.1
  0.0 0.8 multiply_reduce_fusion.1
  0.8 1.0 reduce-window.16
  1.7 0.1 slice.38
  1.8 0.1 slice_reduce_fusion.1
  2.6 0.7 negate_reduce_fusion
  3.3 0.3 reduce-window.24
  3.6 0.1 slice.40
  3.7 0.1 slice_reduce_fusion
  3.8 0.1 select_multiply_fusion
  3.9 1.0 copy.13
  4.9 1.7 pad_maximum_fusion.piece_ref
  6.7 0.0 copy-done
  6.7 0.3 fusion.6
  6.9 0.0 copy-done.1
  6.9 1.1 fusion.8.rows_ref
  8.1 86.3 %shard_map.91 = (bf16[8,4,128,1536]{3,2,1,0:T(8,128)(2,1)}, bf16[8,96,4096]{2,1,0:T(8,128)(2,1)}) custom-call(bf16[128,1536]{1,0:T(8,128)(2,1)} %pad_maximum_fusion.piece_ref, bf16[96,4096]{1,0:T(8,128)(2,1)} %fusion.8.rows_ref), custom_call_target="tpu_custom_call" | custom-call | tf_op jit(solution)/shard_map/pallas_call | solution.py:312
  94.4 12.1 %fusion.3 = bf16[768,1024]{1,0:T(8,128)(2,1)} fusion(bf16[768,4096]{1,0:T(8,128)(2,1)} %bitcast.36, bf16[4096,1536]{1,0:T(8,128)(2,1)} %bitcast.32), kind=kOutput, calls=%fused_computation.8 | convolution fusion | flops 6443237376 | bytes 16252928 | tf_op jit(solution)/shard_map/dot_general | solution.py:463
  106.4 2.7 %fusion.10 = f32[768,512]{1,0:T(8,128)S(1)} fusion(f32[768]{0:T(1024)S(1)} %multiply_reduce_fusion.1, f32[768]{0:T(1024)S(1)} %get-tuple-element.11, s32[768]{0:T(1024)S(1)} %get-tuple-element.10, bf16[768,1024]{1,0:T(8,128)(2,1)} %fusion.3), kind=kOutput, calls=%fused_computation.16 | convolution fusion | flops 911867904 | bytes 3166208 | tf_op jit(solution)/shard_map/dot_general | solution.py:420
  109.2 0.6 slice.44
  109.8 0.6 slice.43
  110.4 1.3 exponential_select_fusion
  111.7 2.6 %fusion.20.state_ref = f32[256,512]{1,0:T(8,128)} fusion(bf16[768,1024]{1,0:T(8,128)(2,1)} %fusion.3, f32[768]{0:T(1024)S(1)} %exponential_select_fusion), kind=kOutput, calls=%fused_computation.27 | convolution fusion | flops 201916416 | bytes 1707008 | tf_op jit(solution)/shard_map/dot_general | solution.py:425
  115.7 0.6 broadcast_in_dim.5.decay_ref
  116.3 30.2 %shard_map.92 = f32[256,512]{1,0:T(8,128)} custom-call(f32[256,512]{1,0:T(8,128)} %fusion.20.state_ref, f32[16,512]{1,0:T(8,128)} %broadcast_in_dim.5.decay_ref), custom_call_target="tpu_custom_call" | custom-call | tf_op jit(solution)/shard_map/pallas_call | solution.py:182
  146.5 2.7 %fusion.38 = (f32[768]{0:T(1024)S(1)}, f32[768,512]{1,0:T(8,128)S(1)}) fusion(f32[768,512]{1,0:T(8,128)S(1)} %fusion.10, f32[256,512]{1,0:T(8,128)} %shard_map.92, f32[768]{0:T(1024)S(1)} %get-tuple-element.9, bf16[768,1024]{1,0:T(8,128)(2,1)} %fusion.3), kind=kOutput, calls=%fused_computation.58 | convolution fusion | flops 1209138432 | bytes 4069376 | tf_op jit(solution)/shard_map/dot_general | solution.py:435
  149.2 0.0 copy-start.2
  149.3 0.3 multiply_reduce_fusion
  149.6 0.3 copy-done.2
  149.9 0.3 multiply_convert_fusion.1.heads_ref
  150.2 2.5 %slice.50.weight_ref = bf16[4096,512]{1,0:T(8,128)(2,1)S(1)} slice(bf16[4096,1536]{1,0:T(8,128)(2,1)} %bitcast.33), slice={[0:4096], [1024:1536]} | slice | bytes 8388608 | tf_op jit(solution)/shard_map/slice | solution.py:462
  152.7 41.2 %shard_map.93 = bf16[96,4096]{1,0:T(8,128)(2,1)S(1)} custom-call(bf16[768,512]{1,0:T(8,128)(2,1)S(1)} %multiply_convert_fusion.1.heads_ref, bf16[4096,512]{1,0:T(8,128)(2,1)S(1)} %slice.50.weight_ref), custom_call_target="tpu_custom_call" | custom-call | tf_op jit(solution)/shard_map/pallas_call | solution.py:383
  193.9 1.1 fusion.9
  (6 shorter events, 0.1 us)
Async XLA Ops:
  0.0 6.7 %copy-start = (bf16[96,4096]{1,0:T(8,128)(2,1)S(1)}, bf16[96,4096]{1,0:T(8,128)(2,1)}, u32[]{:S(2)}) copy-start(bf16[96,4096]{1,0:T(8,128)(2,1)} %param.9) | copy-start | bytes 2359300
  0.0 6.9 %copy-start.1 = (f32[4096]{0:T(1024)S(1)}, f32[4096]{0:T(1024)}, u32[]{:S(2)}) copy-start(f32[4096]{0:T(1024)} %param.10) | copy-start | bytes 49156
  149.2 0.7 copy-start.2

commit v18 on v17

--- a/solution.py
+++ b/solution.py
@@ -358,9 +358,11 @@
     first = [own(lax.rem(tp + nt * nt - sign, nt), side) for side, sign in sides]
     pl.semaphore_wait(barrier, 2)
     for step in range(1, nt):
+        mine = first if step == 1 else [
+            own(lax.rem(tp + nt * nt - sign * step, nt), side) for side, sign in sides
+        ]
         for side, sign in sides:
-            chunk = lax.rem(tp + nt * nt - sign * step, nt)
-            total = first[side] if step == 1 else own(chunk, side)
+            total = mine[side]
             if step > 1:
                 copy(side, step - 1, lax.rem(tp + nt - sign, nt)).wait_recv()
                 total = total + recv_buf[side * nt + step - 1].astype(jnp.float32)

time: 196 us -> 195 us (level)
  no operation moved by 1% of the time
where the time goes in v18:
time: 195 us
  Pallas kernels  157 us (81%)
  matrix products  20.2 us (10%)
  other arithmetic  8.99 us (5%)
  local copies, waits for them, and re-layouts  6.05 us (3%)
  between operations  2.09 us (1%)
    pallas_call x1, Pallas kernels, gather_blocks(): pl.pallas_call(functools.partial(gather_kernel, ny, nz, nt), out_shape=(j...  86.3 us
    pallas_call x1, Pallas kernels, scatter_rows(): pl.pallas_call(functools.partial(scatter_kernel, nt), out_shape=jax.Shape...  40.7 us
    pallas_call x1, Pallas kernels, carried_in(): pl.pallas_call(functools.partial(scan_kernel, ny, nz, zshifts), out_shape...  30.2 us
    dot_general x1, matrix products, local(): jnp.dot(every_row_list, parameter_collection, preferred_element_type=jnp....  12.1 us

profile of v18, /device:TPU:224, one launch (start us, length us, event | category | flops | bytes accessed | tf_op | source)
XLA Modules:
  0.0 194.5 jit_solution(2668339937152635061)
XLA Ops:
  0.0 0.0 copy-start
  0.0 0.0 copy-start.1
  0.0 0.8 multiply_reduce_fusion.1
  0.8 1.0 reduce-window.16
  1.7 0.1 slice.38
  1.8 0.1 slice_reduce_fusion.1
  2.6 0.7 negate_reduce_fusion
  3.3 0.3 reduce-window.24
  3.6 0.1 slice.40
  3.7 0.1 slice_reduce_fusion
  3.8 0.1 select_multiply_fusion
  3.9 1.0 copy.13
  4.9 1.7 pad_maximum_fusion.piece_ref
  6.7 0.0 copy-done
  6.7 0.3 fusion.6
  6.9 0.0 copy-done.1
  6.9 1.1 fusion.8.rows_ref
  8.1 86.3 %shard_map.91 = (bf16[8,4,128,1536]{3,2,1,0:T(8,128)(2,1)}, bf16[8,96,4096]{2,1,0:T(8,128)(2,1)}) custom-call(bf16[128,1536]{1,0:T(8,128)(2,1)} %pad_maximum_fusion.piece_ref, bf16[96,4096]{1,0:T(8,128)(2,1)} %fusion.8.rows_ref), custom_call_target="tpu_custom_call" | custom-call | tf_op jit(solution)/shard_map/pallas_call | solution.py:312
  94.4 12.1 %fusion.3 = bf16[768,1024]{1,0:T(8,128)(2,1)} fusion(bf16[768,4096]{1,0:T(8,128)(2,1)} %bitcast.36, bf16[4096,1536]{1,0:T(8,128)(2,1)} %bitcast.32), kind=kOutput, calls=%fused_computation.8 | convolution fusion | flops 6443237376 | bytes 16252928 | tf_op jit(solution)/shard_map/dot_general | solution.py:465
  106.4 2.7 %fusion.10 = f32[768,512]{1,0:T(8,128)S(1)} fusion(f32[768]{0:T(1024)S(1)} %multiply_reduce_fusion.1, f32[768]{0:T(1024)S(1)} %get-tuple-element.11, s32[768]{0:T(1024)S(1)} %get-tuple-element.10, bf16[768,1024]{1,0:T(8,128)(2,1)} %fusion.3), kind=kOutput, calls=%fused_computation.16 | convolution fusion | flops 911867904 | bytes 3166208 | tf_op jit(solution)/shard_map/dot_general | solution.py:422
  109.2 0.6 slice.44
  109.8 0.6 slice.43
  110.4 1.3 exponential_select_fusion
  111.7 2.6 %fusion.20.state_ref = f32[256,512]{1,0:T(8,128)} fusion(bf16[768,1024]{1,0:T(8,128)(2,1)} %fusion.3, f32[768]{0:T(1024)S(1)} %exponential_select_fusion), kind=kOutput, calls=%fused_computation.27 | convolution fusion | flops 201916416 | bytes 1707008 | tf_op jit(solution)/shard_map/dot_general | solution.py:427
  115.7 0.6 broadcast_in_dim.5.decay_ref
  116.3 30.2 %shard_map.92 = f32[256,512]{1,0:T(8,128)} custom-call(f32[256,512]{1,0:T(8,128)} %fusion.20.state_ref, f32[16,512]{1,0:T(8,128)} %broadcast_in_dim.5.decay_ref), custom_call_target="tpu_custom_call" | custom-call | tf_op jit(solution)/shard_map/pallas_call | solution.py:182
  146.5 2.7 %fusion.38 = (f32[768]{0:T(1024)S(1)}, f32[768,512]{1,0:T(8,128)S(1)}) fusion(f32[768,512]{1,0:T(8,128)S(1)} %fusion.10, f32[256,512]{1,0:T(8,128)} %shard_map.92, f32[768]{0:T(1024)S(1)} %get-tuple-element.9, bf16[768,1024]{1,0:T(8,128)(2,1)} %fusion.3), kind=kOutput, calls=%fused_computation.58 | convolution fusion | flops 1209138432 | bytes 4069376 | tf_op jit(solution)/shard_map/dot_general | solution.py:437
  149.2 0.0 copy-start.2
  149.3 0.3 multiply_reduce_fusion
  149.6 0.3 copy-done.2
  149.9 0.3 multiply_convert_fusion.1.heads_ref
  150.2 2.5 %slice.50.weight_ref = bf16[4096,512]{1,0:T(8,128)(2,1)S(1)} slice(bf16[4096,1536]{1,0:T(8,128)(2,1)} %bitcast.33), slice={[0:4096], [1024:1536]} | slice | bytes 8388608 | tf_op jit(solution)/shard_map/slice | solution.py:464
  152.7 40.7 %shard_map.93 = bf16[96,4096]{1,0:T(8,128)(2,1)S(1)} custom-call(bf16[768,512]{1,0:T(8,128)(2,1)S(1)} %multiply_convert_fusion.1.heads_ref, bf16[4096,512]{1,0:T(8,128)(2,1)S(1)} %slice.50.weight_ref), custom_call_target="tpu_custom_call" | custom-call | tf_op jit(solution)/shard_map/pallas_call | solution.py:385
  193.4 1.1 fusion.9
  (6 shorter events, 0.1 us)
Async XLA Ops:
  0.0 6.7 %copy-start = (bf16[96,4096]{1,0:T(8,128)(2,1)S(1)}, bf16[96,4096]{1,0:T(8,128)(2,1)}, u32[]{:S(2)}) copy-start(bf16[96,4096]{1,0:T(8,128)(2,1)} %param.9) | copy-start | bytes 2359300
  0.0 6.9 %copy-start.1 = (f32[4096]{0:T(1024)S(1)}, f32[4096]{0:T(1024)}, u32[]{:S(2)}) copy-start(f32[4096]{0:T(1024)} %param.10) | copy-start | bytes 49156
  149.2 0.7 copy-start.2

commit v19 on v18

--- a/solution.py
+++ b/solution.py
@@ -327,7 +327,7 @@
     return out.reshape(nz * ny * height, width), rows_out.reshape(nt * rows.shape[0], rows.shape[1])
 
 
-def scatter_kernel(nt, heads_ref, weight_ref, out_ref, send_buf, recv_buf, send_sems, recv_sems):
+def scatter_kernel(nt, heads_ref, weight_ref, tokens_ref, out_ref, send_buf, recv_buf, send_sems, recv_sems):
     tp = lax.axis_index("tp")
     rows = out_ref.shape[0]
     half = out_ref.shape[1] // 2
@@ -372,20 +372,22 @@
     for side, sign in sides:
         copy(side, nt - 1, lax.rem(tp + nt - sign, nt)).wait_recv()
         total = last[side] + recv_buf[side * nt + nt - 1].astype(jnp.float32)
-        out_ref[:, side * half : (side + 1) * half] = total.astype(out_ref.dtype)
+        summed = total.astype(jnp.bfloat16).astype(jnp.float32)
+        residual = tokens_ref[:, side * half : (side + 1) * half].astype(jnp.float32)
+        out_ref[:, side * half : (side + 1) * half] = (residual + summed).astype(out_ref.dtype)
     for step in range(1, nt):
         for side, sign in sides:
             copy(side, step, lax.rem(tp + nt + sign, nt)).wait_send()
 
 
-def scatter_rows(heads, weight):
+def scatter_rows(heads, weight, tokens):
     nt = lax.axis_size("tp")
     rows = heads.shape[0] // nt
     width = weight.shape[0]
     return pl.pallas_call(
         functools.partial(scatter_kernel, nt),
         out_shape=jax.ShapeDtypeStruct((rows, width), jnp.bfloat16),
-        in_specs=[pl.BlockSpec(memory_space=pltpu.VMEM)] * 2,
+        in_specs=[pl.BlockSpec(memory_space=pltpu.VMEM)] * 3,
         out_specs=pl.BlockSpec(memory_space=pltpu.VMEM),
         scratch_shapes=[
             pltpu.VMEM((2 * nt, rows, width // 2), jnp.bfloat16),
@@ -396,7 +398,7 @@
         compiler_params=pltpu.CompilerParams(
             collective_id=2, has_side_effects=True, vmem_limit_bytes=48 * 1024 * 1024
         ),
-    )(heads, weight)
+    )(heads, weight, tokens)
 
 
 def rms_rows(embedded_entries, norm_gain):
@@ -495,8 +497,7 @@
         incoming[attention_slot_number],
     )
     normed_heads = head_norm(head_out, head_gain)
-    summed = scatter_rows(normed_heads, out_rows).astype(jnp.float32)
-    return (tokens.astype(jnp.float32) + summed).astype(jnp.bfloat16)
+    return scatter_rows(normed_heads, out_rows, tokens)
 
 
 def solution(mesh):

time: 195 us -> 199 us (1.021)
  Pallas kernels: 157 us -> 160 us
  local copies, waits for them, and re-layouts: 6.05 us -> 8.89 us
    pallas_call x1, Pallas kernels: 40.7 us -> 43.1 us  [scatter_rows(): pl.pallas_call(functools.partial(scatter_kernel, nt), out_shape=jax.Shape...]
where the time goes in v19:
time: 199 us
  Pallas kernels  160 us (80%)
  matrix products  20.2 us (10%)
  local copies, waits for them, and re-layouts  8.89 us (4%)
  other arithmetic  7.9 us (4%)
  between operations  2.09 us (1%)
    pallas_call x1, Pallas kernels, gather_blocks(): pl.pallas_call(functools.partial(gather_kernel, ny, nz, nt), out_shape=(j...  86.3 us
    pallas_call x1, Pallas kernels, scatter_rows(): pl.pallas_call(functools.partial(scatter_kernel, nt), out_shape=jax.Shape...  43.1 us
    pallas_call x1, Pallas kernels, carried_in(): pl.pallas_call(functools.partial(scan_kernel, ny, nz, zshifts), out_shape...  30.2 us
    dot_general x1, matrix products, local(): jnp.dot(every_row_list, parameter_collection, preferred_element_type=jnp....  12.1 us
    slice x1, local copies, waits for them, and re-layouts, local(): out_rows = both[:, width:]  4.42 us

profile of v19, /device:TPU:224, one launch (start us, length us, event | category | flops | bytes accessed | tf_op | source)
XLA Modules:
  0.0 198.6 jit_solution(5083233386298173623)
XLA Ops:
  0.0 0.0 copy-start
  0.0 0.0 copy-start.1
  0.0 0.8 multiply_reduce_fusion.1
  0.8 1.0 reduce-window.16
  1.7 0.1 slice.38
  1.8 0.1 slice_reduce_fusion.1
  2.6 0.7 negate_reduce_fusion
  3.3 0.3 reduce-window.24
  3.6 0.1 slice.40
  3.7 0.1 slice_reduce_fusion
  3.8 0.1 select_multiply_fusion
  3.9 1.0 copy.13
  4.9 1.7 pad_maximum_fusion.piece_ref
  6.7 0.0 copy-done
  6.7 0.3 fusion.6
  6.9 0.0 copy-done.1
  6.9 1.1 fusion.8.rows_ref
  8.1 86.3 %shard_map.91 = (bf16[8,4,128,1536]{3,2,1,0:T(8,128)(2,1)}, bf16[8,96,4096]{2,1,0:T(8,128)(2,1)}) custom-call(bf16[128,1536]{1,0:T(8,128)(2,1)} %pad_maximum_fusion.piece_ref, bf16[96,4096]{1,0:T(8,128)(2,1)} %fusion.8.rows_ref), custom_call_target="tpu_custom_call" | custom-call | tf_op jit(solution)/shard_map/pallas_call | solution.py:312
  94.4 12.1 %fusion.3 = bf16[768,1024]{1,0:T(8,128)(2,1)} fusion(bf16[768,4096]{1,0:T(8,128)(2,1)} %bitcast.36, bf16[4096,1536]{1,0:T(8,128)(2,1)} %bitcast.32), kind=kOutput, calls=%fused_computation.7 | convolution fusion | flops 6443237376 | bytes 16252928 | tf_op jit(solution)/shard_map/dot_general | solution.py:467
  106.4 2.7 %fusion.9 = f32[768,512]{1,0:T(8,128)S(1)} fusion(f32[768]{0:T(1024)S(1)} %multiply_reduce_fusion.1, f32[768]{0:T(1024)S(1)} %get-tuple-element.11, s32[768]{0:T(1024)S(1)} %get-tuple-element.10, bf16[768,1024]{1,0:T(8,128)(2,1)} %fusion.3), kind=kOutput, calls=%fused_computation.14 | convolution fusion | flops 911867904 | bytes 3166208 | tf_op jit(solution)/shard_map/dot_general | solution.py:424
  109.2 0.6 slice.44
  109.8 0.6 slice.43
  110.4 1.3 exponential_select_fusion
  111.7 2.6 %fusion.19.state_ref = f32[256,512]{1,0:T(8,128)} fusion(bf16[768,1024]{1,0:T(8,128)(2,1)} %fusion.3, f32[768]{0:T(1024)S(1)} %exponential_select_fusion), kind=kOutput, calls=%fused_computation.25 | convolution fusion | flops 201916416 | bytes 1707008 | tf_op jit(solution)/shard_map/dot_general | solution.py:429
  115.7 0.6 broadcast_in_dim.5.decay_ref
  116.3 30.2 %shard_map.92 = f32[256,512]{1,0:T(8,128)} custom-call(f32[256,512]{1,0:T(8,128)} %fusion.19.state_ref, f32[16,512]{1,0:T(8,128)} %broadcast_in_dim.5.decay_ref), custom_call_target="tpu_custom_call" | custom-call | tf_op jit(solution)/shard_map/pallas_call | solution.py:182
  146.5 2.7 %fusion.37 = (f32[768]{0:T(1024)S(1)}, f32[768,512]{1,0:T(8,128)S(1)}) fusion(f32[768,512]{1,0:T(8,128)S(1)} %fusion.9, f32[256,512]{1,0:T(8,128)} %shard_map.92, f32[768]{0:T(1024)S(1)} %get-tuple-element.9, bf16[768,1024]{1,0:T(8,128)(2,1)} %fusion.3), kind=kOutput, calls=%fused_computation.56 | convolution fusion | flops 1209138432 | bytes 4069376 | tf_op jit(solution)/shard_map/dot_general | solution.py:439
  149.2 0.0 copy-start.2
  149.3 0.3 multiply_reduce_fusion
  149.6 0.3 copy-done.2
  149.9 0.3 multiply_convert_fusion.1.heads_ref
  150.2 4.4 %slice.50.weight_ref = bf16[4096,512]{1,0:T(8,128)(2,1)} slice(bf16[4096,1536]{1,0:T(8,128)(2,1)} %bitcast.33), slice={[0:4096], [1024:1536]} | slice | bytes 8388608 | tf_op jit(solution)/shard_map/slice | solution.py:466
  154.6 43.1 %shard_map.93 = bf16[96,4096]{1,0:T(8,128)(2,1)S(1)} custom-call(bf16[768,512]{1,0:T(8,128)(2,1)S(1)} %multiply_convert_fusion.1.heads_ref, bf16[4096,512]{1,0:T(8,128)(2,1)} %slice.50.weight_ref, bf16[96,4096]{1,0:T(8,128)(2,1)S(1)} %copy-done), custom_call_target="tpu_custom_call" | custom-call | tf_op jit(solution)/shard_map/pallas_call | solution.py:387
  197.7 0.9 copy.20
  (6 shorter events, 0.1 us)
Async XLA Ops:
  0.0 6.7 %copy-start = (bf16[96,4096]{1,0:T(8,128)(2,1)S(1)}, bf16[96,4096]{1,0:T(8,128)(2,1)}, u32[]{:S(2)}) copy-start(bf16[96,4096]{1,0:T(8,128)(2,1)} %tokens_ref.1) | copy-start | bytes 2359300
  0.0 6.9 %copy-start.1 = (f32[4096]{0:T(1024)S(1)}, f32[4096]{0:T(1024)}, u32[]{:S(2)}) copy-start(f32[4096]{0:T(1024)} %param.10) | copy-start | bytes 49156
  149.2 0.7 copy-start.2

commit v20 on v18

--- a/solution.py
+++ b/solution.py
@@ -139,16 +139,16 @@
         )
 
     for y in range(ny):
-        done = prefix_decay[y][0:1, :] * z_total[...] + prefix_total[y]
-
-        @pl.when(yi == y)
-        def _():
-            out_ref[:, y * quarter : (y + 1) * quarter] = done
-
         @pl.when(yi != y)
         def _():
+            done = prefix_decay[y][0:1, :] * z_total[...] + prefix_total[y]
             c_send[y] = done.astype(jnp.bfloat16)
             c_copy(y, y, yi).start()
+
+    for y in range(ny):
+        @pl.when(yi == y)
+        def _():
+            out_ref[:, y * quarter : (y + 1) * quarter] = prefix_decay[y][0:1, :] * z_total[...] + prefix_total[y]
 
     for y in range(ny):
         @pl.when(yi != y)

time: 195 us -> 195 us (level)
  no operation moved by 1% of the time
where the time goes in v20:
time: 195 us
  Pallas kernels  157 us (81%)
  matrix products  20.2 us (10%)
  other arithmetic  8.99 us (5%)
  local copies, waits for them, and re-layouts  6.05 us (3%)
  between operations  2.09 us (1%)
    pallas_call x1, Pallas kernels, gather_blocks(): pl.pallas_call(functools.partial(gather_kernel, ny, nz, nt), out_shape=(j...  86.3 us
    pallas_call x1, Pallas kernels, scatter_rows(): pl.pallas_call(functools.partial(scatter_kernel, nt), out_shape=jax.Shape...  40.7 us
    pallas_call x1, Pallas kernels, carried_in(): pl.pallas_call(functools.partial(scan_kernel, ny, nz, zshifts), out_shape...  30.3 us
    dot_general x1, matrix products, local(): jnp.dot(every_row_list, parameter_collection, preferred_element_type=jnp....  12.1 us

profile of v20, /device:TPU:224, one launch (start us, length us, event | category | flops | bytes accessed | tf_op | source)
XLA Modules:
  0.0 194.5 jit_solution(11929186711769205313)
XLA Ops:
  0.0 0.0 copy-start
  0.0 0.0 copy-start.1
  0.0 0.8 multiply_reduce_fusion.1
  0.8 1.0 reduce-window.16
  1.7 0.1 slice.38
  1.8 0.1 slice_reduce_fusion.1
  2.6 0.7 negate_reduce_fusion
  3.3 0.3 reduce-window.24
  3.6 0.1 slice.40
  3.7 0.1 slice_reduce_fusion
  3.8 0.1 select_multiply_fusion
  3.9 1.0 copy.13
  4.9 1.7 pad_maximum_fusion.piece_ref
  6.7 0.0 copy-done
  6.7 0.3 fusion.6
  6.9 0.0 copy-done.1
  6.9 1.1 fusion.8.rows_ref
  8.1 86.3 %shard_map.91 = (bf16[8,4,128,1536]{3,2,1,0:T(8,128)(2,1)}, bf16[8,96,4096]{2,1,0:T(8,128)(2,1)}) custom-call(bf16[128,1536]{1,0:T(8,128)(2,1)} %pad_maximum_fusion.piece_ref, bf16[96,4096]{1,0:T(8,128)(2,1)} %fusion.8.rows_ref), custom_call_target="tpu_custom_call" | custom-call | tf_op jit(solution)/shard_map/pallas_call | solution.py:312
  94.4 12.1 %fusion.3 = bf16[768,1024]{1,0:T(8,128)(2,1)} fusion(bf16[768,4096]{1,0:T(8,128)(2,1)} %bitcast.36, bf16[4096,1536]{1,0:T(8,128)(2,1)} %bitcast.32), kind=kOutput, calls=%fused_computation.8 | convolution fusion | flops 6443237376 | bytes 16252928 | tf_op jit(solution)/shard_map/dot_general | solution.py:465
  106.4 2.7 %fusion.10 = f32[768,512]{1,0:T(8,128)S(1)} fusion(f32[768]{0:T(1024)S(1)} %multiply_reduce_fusion.1, f32[768]{0:T(1024)S(1)} %get-tuple-element.11, s32[768]{0:T(1024)S(1)} %get-tuple-element.10, bf16[768,1024]{1,0:T(8,128)(2,1)} %fusion.3), kind=kOutput, calls=%fused_computation.16 | convolution fusion | flops 911867904 | bytes 3166208 | tf_op jit(solution)/shard_map/dot_general | solution.py:422
  109.2 0.6 slice.44
  109.8 0.6 slice.43
  110.4 1.3 exponential_select_fusion
  111.7 2.6 %fusion.20.state_ref = f32[256,512]{1,0:T(8,128)} fusion(bf16[768,1024]{1,0:T(8,128)(2,1)} %fusion.3, f32[768]{0:T(1024)S(1)} %exponential_select_fusion), kind=kOutput, calls=%fused_computation.27 | convolution fusion | flops 201916416 | bytes 1707008 | tf_op jit(solution)/shard_map/dot_general | solution.py:427
  115.7 0.6 broadcast_in_dim.5.decay_ref
  116.3 30.3 %shard_map.92 = f32[256,512]{1,0:T(8,128)} custom-call(f32[256,512]{1,0:T(8,128)} %fusion.20.state_ref, f32[16,512]{1,0:T(8,128)} %broadcast_in_dim.5.decay_ref), custom_call_target="tpu_custom_call" | custom-call | tf_op jit(solution)/shard_map/pallas_call | solution.py:182
  146.5 2.7 %fusion.38 = (f32[768]{0:T(1024)S(1)}, f32[768,512]{1,0:T(8,128)S(1)}) fusion(f32[768,512]{1,0:T(8,128)S(1)} %fusion.10, f32[256,512]{1,0:T(8,128)} %shard_map.92, f32[768]{0:T(1024)S(1)} %get-tuple-element.9, bf16[768,1024]{1,0:T(8,128)(2,1)} %fusion.3), kind=kOutput, calls=%fused_computation.58 | convolution fusion | flops 1209138432 | bytes 4069376 | tf_op jit(solution)/shard_map/dot_general | solution.py:437
  149.3 0.0 copy-start.2
  149.3 0.3 multiply_reduce_fusion
  149.6 0.3 copy-done.2
  150.0 0.3 multiply_convert_fusion.1.heads_ref
  150.2 2.5 %slice.50.weight_ref = bf16[4096,512]{1,0:T(8,128)(2,1)S(1)} slice(bf16[4096,1536]{1,0:T(8,128)(2,1)} %bitcast.33), slice={[0:4096], [1024:1536]} | slice | bytes 8388608 | tf_op jit(solution)/shard_map/slice | solution.py:464
  152.7 40.7 %shard_map.93 = bf16[96,4096]{1,0:T(8,128)(2,1)S(1)} custom-call(bf16[768,512]{1,0:T(8,128)(2,1)S(1)} %multiply_convert_fusion.1.heads_ref, bf16[4096,512]{1,0:T(8,128)(2,1)S(1)} %slice.50.weight_ref), custom_call_target="tpu_custom_call" | custom-call | tf_op jit(solution)/shard_map/pallas_call | solution.py:385
  193.4 1.1 fusion.9
  (6 shorter events, 0.1 us)
Async XLA Ops:
  0.0 6.7 %copy-start = (bf16[96,4096]{1,0:T(8,128)(2,1)S(1)}, bf16[96,4096]{1,0:T(8,128)(2,1)}, u32[]{:S(2)}) copy-start(bf16[96,4096]{1,0:T(8,128)(2,1)} %param.9) | copy-start | bytes 2359300
  0.0 6.9 %copy-start.1 = (f32[4096]{0:T(1024)S(1)}, f32[4096]{0:T(1024)}, u32[]{:S(2)}) copy-start(f32[4096]{0:T(1024)} %param.10) | copy-start | bytes 49156
  149.3 0.7 copy-start.2
